TPU v7x, 128 devices: a whole 4x4x4 slice. The times are simulated.
128 devices in a mesh: kz: 16 (over y_hi, x, core), pw: 8 (over z, y_lo).
Axes of the slice: x: 4, y: 4 (y_hi: 2, y_lo: 2; y = y_hi * 2 + y_lo), z: 4, core: 2. Of those that a mesh axis runs over, the one named last changes fastest.
Arguments:
- states: bfloat16 [16, 2, 384, 1024, 128], P('kz', None, None, 'pw'), may hold values from -1 to 1
- stick_perm: int32 [1024], P('pw'), may hold values from 0 to 1023, as said below
Outputs:
- margin: float32 [384, 16, 2, 384], P('pw', 'kz')
Inputs may be any that keep to these rules, and one draw needn't show every extreme that they name: `stick_perm`: each aligned run of 128 entries, starting at a multiple of 128, is a permutation of the stick numbers of that run.
All inputs are finite; a program needn't handle non-finite values.
Results may differ from a plain program's by a relative error of at most 0.0003.
Values may be sent and summed in bfloat16 or wider, within the bound.
No kernel may reach another device: no remote copies, remote signals or barrier semaphores. Data moves between devices by JAX's collectives and lax.ppermute only.
A program may use at most 192 MiB of HBM per device.

v0:
```python
import jax
import jax.numpy as jnp
from jax import lax
from jax.sharding import PartitionSpec as P


def from_behind(value, axis, steps):
    count = lax.axis_size(axis)
    pairs = [(source, (source + steps) % count) for source in range(count)]
    return lax.ppermute(value, axis, pairs)


def wrap_shift(state, local_perm):
    moved = jnp.take(state, local_perm, axis=2)
    return jnp.concatenate([moved[..., 1:], jnp.zeros_like(moved[..., :1])], axis=-1)


def pair_block(left_rows, right_full):
    products = jnp.einsum(
        "kamp,kbnp->mkabn", left_rows, right_full, preferred_element_type=jnp.float32
    )
    real_part = products[:, :, 0, 0] + products[:, :, 1, 1]
    imag_part = products[:, :, 0, 1] - products[:, :, 1, 0]
    return jnp.stack([real_part, imag_part], axis=2)


def shards(states, stick_perm):
    kpoints = states.shape[0]
    bands = states.shape[2]
    sticks = states.shape[3]
    flat_states = states.reshape(kpoints, 2, bands, -1)
    kz_index = lax.axis_index("kz")
    local_perm = stick_perm - lax.axis_index("pw") * sticks
    wrapped = wrap_shift(states[0], local_perm)
    sent = jnp.where(kz_index == 0, wrapped, states[0])
    arrived = from_behind(sent, "kz", -1)
    arrived_flat = arrived.reshape(1, 2, bands, -1)
    inner = pair_block(flat_states[:-1], flat_states[1:])
    edge = pair_block(flat_states, arrived_flat)
    return lax.psum_scatter(
        jnp.concatenate([inner, edge], axis=1), "pw", scatter_dimension=0, tiled=True
    )


def solution(mesh):
    in_specs = (P("kz", None, None, "pw", None), P("pw"))
    out_specs = P("pw", "kz", None, None)
    return jax.shard_map(shards, mesh=mesh, in_specs=in_specs, out_specs=out_specs, check_vma=False)
```

profile of v0, /device:TPU:7, one launch (start us, length us, event | category | flops | bytes accessed | tf_op | source)
XLA Modules:
  0.0 565.0 jit_solution(10752777381869396505)
XLA Ops:
  6.5 0.0 all-reduce.4.cloned.1.call-start
  6.5 0.7 compare_and_fusion
  7.2 26.9 %copy.13 = bf16[2,384,128,128]{3,1,2,0:T(8,128)(2,1)} copy(bf16[2,384,128,128]{3,2,1,0:T(8,128)(2,1)} %bitcast.34) | data formatting | bytes 50331648 | tf_op jit(solution)/shard_map/squeeze | solution.py:34
  34.1 19.2 %gather_fusion = bf16[128,2,384,128]{3,2,1,0:T(8,128)(2,1)} fusion(bf16[2,384,128,128]{3,1,2,0:T(8,128)(2,1)} %copy.13, s32[1024]{0:T(1024)S(1)} %pad_clamp_fusion), kind=kCustom, calls=%fused_computation | custom fusion | bytes 50332160 | tf_op jit(solution)/shard_map/jit(_take)/gather | solution.py:14
  53.3 12.7 %select_bitcast_fusion = bf16[2,384,128,128]{3,1,0,2:T(8,128)(2,1)S(1)} fusion(bf16[128,2,384,128]{3,2,1,0:T(8,128)(2,1)} %gather_fusion, pred[128]{0:T(512)(128)(4,1)S(1)} %get-tuple-element.5), kind=kLoop, calls=%fused_computation.4 | loop fusion | flops 12582912 | bytes 50331776 | tf_op jit(solution)/shard_map/jit(_take)/select_n | solution.py:14
  66.0 12.7 %slice.22 = bf16[2,384,128,127]{3,1,0,2:T(8,128)(2,1)} slice(bf16[2,384,128,128]{3,1,0,2:T(8,128)(2,1)S(1)} %select_bitcast_fusion), slice={[0:2], [0:384], [0:128], [1:128]} | slice | bytes 49938432 | tf_op jit(solution)/shard_map/slice | solution.py:15
  78.7 30.8 %bitcast_select_fusion = bf16[2,384,128,128]{3,1,0,2:T(8,128)(2,1)} fusion(bf16[1,2,384,128,128]{4,3,2,1,0:T(8,128)(2,1)} %param.2, bf16[2,384,128,127]{3,1,0,2:T(8,128)(2,1)} %slice.22, pred[]{:T(512)S(6)} %eq.3), kind=kLoop, calls=%fused_computation.3 | loop fusion | flops 12582912 | bytes 75300864 | tf_op jit(solution)/shard_map/jit(_where)/select_n | solution.py:35
  109.6 0.7 collective-permute-start
  110.2 37.3 %reshape.74 = bf16[2,384,16384,1]{2,1,0,3:T(8,128)(2,1)} reshape(bf16[1,2,384,128,128]{4,3,2,1,0:T(8,128)(2,1)} %param.2) | data formatting | bytes 50331648 | tf_op jit(solution)/shard_map/reshape.4
  147.6 238.5 %collective-permute-done = bf16[2,384,128,128]{3,1,0,2:T(8,128)(2,1)} collective-permute-done((bf16[2,384,128,128]{3,1,0,2:T(8,128)(2,1)}, bf16[2,384,128,128]{3,1,0,2:T(8,128)(2,1)}, u32[]{:S(2)}, u32[]{:S(2)}) %collective-permute-start) | collective-permute-done | bytes 25165856 | tf_op jit(solution)/shard_map/ppermute | solution.py:10
  386.1 26.9 %copy.14 = bf16[2,384,128,128]{3,2,1,0:T(8,128)(2,1)} copy(bf16[2,384,128,128]{3,1,0,2:T(8,128)(2,1)} %collective-permute-done) | data formatting | bytes 50331648 | tf_op jit(solution)/shard_map/ppermute | solution.py:10
  413.0 37.4 %reshape.73 = bf16[2,384,16384,1]{2,1,0,3:T(8,128)(2,1)} reshape(bf16[2,384,128,128]{3,2,1,0:T(8,128)(2,1)} %copy.14) | data formatting | bytes 50331648 | tf_op jit(solution)/shard_map/reshape.1
  450.4 0.0 copy-start
  450.4 24.9 %fusion.2 = f32[384,1,2,2,384]{0,4,2,3,1:T(8,128)S(1)} fusion(bf16[2,384,16384,1]{2,1,0,3:T(8,128)(2,1)} %reshape.74, bf16[2,384,16384,1]{2,1,0,3:T(8,128)(2,1)} %reshape.73), kind=kOutput, calls=%fused_computation.5 | convolution fusion | flops 19327352832 | bytes 52690944 | tf_op jit(solution)/shard_map/kamp,kbnp->mkabn/dot_general | solution.py:19
  475.3 0.1 fusion.5
  475.4 0.1 fusion.7
  475.4 0.1 pad_maximum_fusion
  475.5 2.0 copy.17
  477.5 0.0 all-reduce.4.cloned.1.call-update
  477.5 0.0 copy-done
  477.5 0.6 dynamic-slice
  478.8 77.8 %all-reduce.4.cloned.1.call-done = f32[384,1,2,384]{3,2,1,0:T(2,128)} async-done(((f32[384,1,2,384]{3,2,1,0:T(2,128)}), f32[384,1,2,384]{3,2,1,0:T(2,128)}) %all-reduce.4.cloned.1.call-update) | async-done | bytes 1179664
  556.6 1.6 constant_dynamic-slice_fusion
  (1 shorter events, 0.0 us)
Async XLA Ops:
  6.5 550.0 %all-reduce.4.cloned.1.call-start = ((), (), s32[]{:S(2)}) async-start(), calls=%async_computation | async-start | bytes 2359296
  109.6 276.6 %collective-permute-start = (bf16[2,384,128,128]{3,1,0,2:T(8,128)(2,1)}, bf16[2,384,128,128]{3,1,0,2:T(8,128)(2,1)}, u32[]{:S(2)}, u32[]{:S(2)}) collective-permute-start(bf16[2,384,128,128]{3,1,0,2:T(8,128)(2,1)} %bitcast_select_fusion), channel_id=1, source_target_pairs={{0,120},{8,0},{16,8},{24,16},{32,24},{40,32},{48,40},{56,48},{64,5... | collective-permute-start | bytes 75497480 | tf_op jit(solution)/shard_map/ppermute | solution.py:10
  450.4 27.2 %copy-start = (u32[128]{0:T(128)S(1)}, u32[128]{0:T(128)}, u32[]{:S(2)}) copy-start(u32[128]{0:T(128)} %constant.34) | copy-start | bytes 1540
Sparse Core Ops, SparseCore 0:
  477.6 78.8 all-reduce.3
where the time goes:
time: 573 us; the launch traced here: 565 us
  waiting for transfers between devices  316 us (55%)
  local copies, waits for them, and re-layouts  165 us (29%)
  other arithmetic  44.4 us (8%)
  matrix products  24.9 us (4%)
  between operations  14.1 us (2%)
    ppermute x1, waiting for transfers between devices, from_behind(): return lax.ppermute(value, axis, pairs)  239 us
    unnamed x2, waiting for transfers between devices  77.8 us
    another operation x2, local copies, waits for them, and re-layouts  74.7 us
    select_n x1, other arithmetic, shards(): sent = jnp.where(kz_index == 0, wrapped, states[0])  30.8 us
    squeeze x1, local copies, waits for them, and re-layouts, shards(): wrapped = wrap_shift(states[0], local_perm)  26.9 us
    ppermute x1, local copies, waits for them, and re-layouts, from_behind(): return lax.ppermute(value, axis, pairs)  26.9 us
    dot_general x1, matrix products, pair_block(): jnp.einsum('kamp,kbnp->mkabn', left_rows, right_full, preferred_element_t...  24.9 us
    gather x1, local copies, waits for them, and re-layouts, wrap_shift(): moved = jnp.take(state, local_perm, axis=2)  19.2 us
  transfers between devices with their start and end apart: 2, of which 2 were waited for; matrix products, arithmetic and copies ran while one was open for 7% of the time, Pallas kernels for 0%

commit v1 on v0

v1 whole, which is shorter than its diff:
```python
import jax
import jax.numpy as jnp
from jax import lax
from jax.experimental import pallas as pl
from jax.experimental.pallas import tpu as pltpu
from jax.sharding import PartitionSpec as P

SUB = 64
LANES = 128
PITCH = SUB + 1
CHUNKS = ((0, 1, (64,)), (1, 1, (64,)), (2, 2, (64,)), (4, 2, (48, 16)))
GROUPS = ((0, 1), (2,), (3,))
STEP = 16
PARAMS = pltpu.CompilerParams(vmem_limit_bytes=56 << 20)


def shifted(value, axis, steps):
    count = lax.axis_size(axis)
    return lax.ppermute(value, axis, [(s, (s + steps) % count) for s in range(count)])


def relayout(states, perm, wraps, chunk, left):
    first, units, pieces = chunk
    sticks = states.shape[2]
    half = sticks // 2
    bands = units * SUB

    def body(perm_ref, wraps_ref, x_ref, *refs):
        outs, scratch = refs[:-1], refs[-1]
        x = x_ref.at[0]
        for m in range(SUB):
            row = x[m] if left else x[m // 8, m % 8]
            scratch[pl.ds(m, sticks, stride=PITCH), :] = row.astype(jnp.float32)

        def put(s, value):
            value = value.astype(jnp.bfloat16)
            sent = s < half if left else s >= half
            if not sent:
                outs[-1][0, s % half] = value
                return
            at = s % half
            for piece, size in enumerate(pieces):
                if at < size:
                    outs[piece][0, at] = value
                    return
                at -= size

        def plain():
            for s in range(sticks):
                put(s, scratch[pl.ds(s * PITCH, SUB), :])

        def wrapped():
            keep = lax.broadcasted_iota(jnp.int32, (SUB, LANES), 1) < LANES - 1
            for s in range(sticks):
                value = scratch[pl.ds(perm_ref[s] * PITCH, SUB), :]
                put(s, jnp.where(keep, pltpu.roll(value, LANES - 1, 1), 0.0))

        if left:
            pl.when(wraps_ref[0] == 0)(plain)
            pl.when(wraps_ref[0] != 0)(wrapped)
        else:
            plain()

    if left:
        view = states
        in_spec = pl.BlockSpec((1, SUB, sticks, LANES), lambda c, g, *_: (c, first + g, 0, 0))
    else:
        view = states.reshape(2, 8, states.shape[1] // 8, sticks, LANES)
        in_spec = pl.BlockSpec((1, 8, 8, sticks, LANES), lambda c, g, *_: (c, 0, first + g, 0, 0))
    sizes = (*pieces, half)
    return pl.pallas_call(
        body,
        grid_spec=pltpu.PrefetchScalarGridSpec(
            num_scalar_prefetch=2,
            grid=(2, units),
            in_specs=[in_spec],
            out_specs=[pl.BlockSpec((1, n, SUB, LANES), lambda c, g, *_: (c, 0, g, 0)) for n in sizes],
            scratch_shapes=[pltpu.VMEM((sticks * PITCH, LANES), jnp.float32)],
        ),
        out_shape=[jax.ShapeDtypeStruct((2, n, bands, LANES), jnp.bfloat16) for n in sizes],
        compiler_params=PARAMS,
        name="relayout_left" if left else "relayout_right",
    )(perm, wraps, view)


def products(rows, columns, offset_rows, offset_columns, sticks, start, finish):
    n_rows = sum(r.shape[2] for r in rows)
    n_columns = sum(c.shape[2] for c in columns)
    shape = (2 * n_rows, 2 * n_columns)
    steps = sticks // STEP

    def side(refs):
        return jnp.concatenate(
            [jnp.concatenate([r[c, j] for j in range(STEP)], -1) for c in range(2) for r in refs], 0
        )

    def body(*refs):
        row_refs, refs = refs[: len(rows)], refs[len(rows) :]
        column_refs, refs = refs[: len(columns)], refs[len(columns) :]
        start_ref = None
        if start is not None:
            start_ref, refs = refs[0], refs[1:]
        out, total = refs
        step = pl.program_id(0)
        new = lax.dot_general(
            side(row_refs), side(column_refs), (((1,), (1,)), ((), ())), preferred_element_type=jnp.float32
        )

        @pl.when(step == 0)
        def _():
            total[...] = new if start_ref is None else start_ref[...] + new

        @pl.when(step > 0)
        def _():
            total[...] += new

        @pl.when(step == steps - 1)
        def _():
            if not finish:
                out[...] = total[...]
                return
            real = total[:n_rows, :n_columns] + total[n_rows:, n_columns:]
            imag = total[:n_rows, n_columns:] - total[n_rows:, :n_columns]
            for u in range(n_rows // SUB):
                for q in range(8):
                    at = u * SUB + q * 8
                    out[q, 0, 8 * u : 8 * u + 8] = real[at : at + 8]
                    out[q, 1, 8 * u : 8 * u + 8] = imag[at : at + 8]

    def spec(array, offset):
        return pl.BlockSpec((2, STEP, array.shape[2], LANES), lambda s: (0, offset + s, 0, 0))

    in_specs = [spec(r, offset_rows // STEP) for r in rows] + [spec(c, offset_columns // STEP) for c in columns]
    operands = [*rows, *columns]
    if start is not None:
        in_specs.append(pl.BlockSpec(shape, lambda s: (0, 0)))
        operands.append(start)
    out_shape = (8, 2, n_rows // 8, n_columns) if finish else shape
    return pl.pallas_call(
        body,
        grid=(steps,),
        in_specs=in_specs,
        out_specs=pl.BlockSpec(out_shape, lambda s: (0,) * len(out_shape)),
        out_shape=jax.ShapeDtypeStruct(out_shape, jnp.float32),
        scratch_shapes=[pltpu.VMEM(shape, jnp.float32)],
        compiler_params=PARAMS,
        name="products",
    )(*operands)


def shards(states, stick_perm):
    states = states[0]
    sticks = states.shape[2]
    perm = stick_perm - lax.axis_index("pw") * sticks
    wraps = (lax.axis_index("kz") == 0).astype(jnp.int32).reshape(1)
    from_right, from_left, own_rows, own_columns = [], [], [], []
    for chunk in CHUNKS:
        *sent, kept = relayout(states, perm, wraps, chunk, True)
        wraps, kept = lax.optimization_barrier((wraps, kept))
        own_columns.append(kept)
        from_right.append([shifted(piece, "kz", -1) for piece in sent])
        *sent, kept = relayout(states, perm, wraps, chunk, False)
        wraps, kept = lax.optimization_barrier((wraps, kept))
        own_rows.append(kept)
        from_left.append([shifted(piece, "kz", 1) for piece in sent])

    left_parts, right_parts = [], []
    for group in GROUPS:
        pieces = CHUNKS[group[0]][2]
        right_total = left_total = None
        offset = 0
        for index, size in enumerate(pieces):
            last = index == len(pieces) - 1
            right_total = products(
                [from_left[c][index] for c in group], own_columns, 0, offset, size, right_total, last
            )
            left_total = products(
                own_rows, [from_right[c][index] for c in group], offset, 0, size, left_total, last
            )
            offset += size
        own_rows, own_columns, right_total, left_total = lax.optimization_barrier(
            (own_rows, own_columns, right_total, left_total)
        )
        mine = lax.all_to_all(right_total, "pw", 0, 0, tiled=True).sum(0)
        right_parts.append(shifted(mine, "kz", -1))
        left_parts.append(lax.all_to_all(left_total, "pw", 0, 0, tiled=True).sum(0))
    margin = jnp.concatenate(left_parts, 2) + jnp.concatenate(right_parts, 1)
    return jnp.transpose(margin, (1, 0, 2))[:, None]


def solution(mesh):
    in_specs = (P("kz", None, None, "pw", None), P("pw"))
    out_specs = P("pw", "kz", None, None)
    return jax.shard_map(shards, mesh=mesh, in_specs=in_specs, out_specs=out_specs, check_vma=False)
```

time: 573 us -> 266 us (0.46); the launches traced: 565 us -> 265 us
  waiting for transfers between devices: 316 us -> 81 us
  local copies, waits for them, and re-layouts: 165 us -> 3.82 us
  Pallas kernels: 0 us -> 111 us
  other arithmetic: 44.4 us -> 3.33 us
  starting transfers between devices: 0.68 us -> 40.7 us
  blocking collectives: 0 us -> 25 us
  matrix products: 24.9 us -> 0 us
  between operations: 14.1 us -> 0.13 us
    ppermute x1 -> x13, waiting for transfers between devices: 239 us -> 45.6 us  [shifted(): lax.ppermute(value, axis, [(s, (s + steps) % count) for s in range(count)])]
    pallas_call x0 -> x16, Pallas kernels: none -> 111 us  [the longest x8 58.4 us: products(): pl.pallas_call(body, grid=(steps,), in_specs=in_specs, out_specs=pl.Block...]
    unnamed x2 -> x0, waiting for transfers between devices: 77.8 us -> none
    another operation x3 -> x0, local copies, waits for them, and re-layouts: 76.7 us -> none
    select_n x2 -> x0, other arithmetic: 43.5 us -> none  [the longest x1 30.8 us: shards(): sent = jnp.where(kz_index == 0, wrapped, states[0])]
    all_to_all x0 -> x4, waiting for transfers between devices: none -> 35.4 us  [the longest x2 35.4 us: shards(): left_parts.append(lax.all_to_all(left_total, 'pw', 0, 0, tiled=True).sum(0))]
    squeeze x1 -> x0, local copies, waits for them, and re-layouts: 26.9 us -> none  [shards(): wrapped = wrap_shift(states[0], local_perm)]
    ppermute x1 -> x0, local copies, waits for them, and re-layouts: 26.9 us -> none  [from_behind(): return lax.ppermute(value, axis, pairs)]
  transfers between devices with their start and end apart: 2 -> 17, of which waited for: 2 -> 7; matrix products, arithmetic and copies ran while one was open for 7% -> 1% of each run, Pallas kernels for 0% -> 40%
where the time goes in v1:
time: 266 us; the launch traced here: 265 us
  Pallas kernels  111 us (42%)
  waiting for transfers between devices  81 us (30%)
  starting transfers between devices  40.7 us (15%)
  blocking collectives  25 us (9%)
  local copies, waits for them, and re-layouts  3.82 us (1%)
  other arithmetic  3.33 us (1%)
    pallas_call x8, Pallas kernels, products(): pl.pallas_call(body, grid=(steps,), in_specs=in_specs, out_specs=pl.Block...  58.4 us
    pallas_call x8, Pallas kernels, relayout(): pl.pallas_call(body, grid_spec=pltpu.PrefetchScalarGridSpec(num_scalar_pr...  52.5 us
    ppermute x13, waiting for transfers between devices, shifted(): lax.ppermute(value, axis, [(s, (s + steps) % count) for s in range(count)])  45.6 us
    all_to_all x2, waiting for transfers between devices, shards(): left_parts.append(lax.all_to_all(left_total, 'pw', 0, 0, tiled=True).sum(0))  35.4 us
    ppermute x13, starting transfers between devices, shifted(): lax.ppermute(value, axis, [(s, (s + steps) % count) for s in range(count)])  23 us
    all_to_all x1, blocking collectives, shards(): left_parts.append(lax.all_to_all(left_total, 'pw', 0, 0, tiled=True).sum(0))  12.9 us
    all_to_all x1, blocking collectives, shards(): mine = lax.all_to_all(right_total, 'pw', 0, 0, tiled=True).sum(0)  12.1 us
    all_to_all x2, starting transfers between devices, shards(): left_parts.append(lax.all_to_all(left_total, 'pw', 0, 0, tiled=True).sum(0))  9.5 us
  transfers between devices with their start and end apart: 17, of which 7 were waited for; matrix products, arithmetic and copies ran while one was open for 1% of the time, Pallas kernels for 40%

profile of v1, /device:TPU:7, one launch (start us, length us, event | category | flops | bytes accessed | tf_op | source)
XLA Modules:
  0.0 265.0 jit_solution(8750734554671455923)
XLA Ops:
  1.2 4.7 %relayout_left.4 = (bf16[2,64,64,128]{3,2,1,0:T(8,128)(2,1)}, bf16[2,64,64,128]{3,2,1,0:T(8,128)(2,1)}) custom-call(s32[128]{0:T(128)} %broadcast_subtract_fusion.perm_ref, s32[1]{0:T(128)} %bitcast.wraps_ref, bf16[2,384,128,128]{3,2,1,0:T(8,128)(2,1)} %bitcast.7), custom_call_target="tpu_custom_call" | custom-call | tf_op jit(solution)/shard_map/relayout_left/pallas_call | solution.py:71
  6.6 4.6 %relayout_right.4 = (bf16[2,64,64,128]{3,2,1,0:T(8,128)(2,1)}, bf16[2,64,64,128]{3,2,1,0:T(8,128)(2,1)}) custom-call(s32[128]{0:T(128)} %broadcast_subtract_fusion.perm_ref, s32[1]{0:T(128)} %bitcast.wraps_ref, bf16[2,8,48,128,128]{4,3,2,1,0:T(8,128)(2,1)} %bitcast.8), custom_call_target="tpu_custom_call" | custom-call | tf_op jit(solution)/shard_map/relayout_right/pallas_call | solution.py:71
  11.2 4.7 %collective-permute-start = (bf16[2,64,64,128]{3,2,1,0:T(8,128)(2,1)}, bf16[2,64,64,128]{3,2,1,0:T(8,128)(2,1)S(1)}, u32[]{:S(2)}, u32[]{:S(2)}) collective-permute-start(bf16[2,64,64,128]{3,2,1,0:T(8,128)(2,1)} %get-tuple-element.83), channel_id=1, source_target_pairs={{0,8},{8,16},{16,24},{24,32},{32,40},{40,48},{48,56},{56,64},{64,7... | collective-permute-start | bytes 6291464 | tf_op jit(solution)/shard_map/ppermute | solution.py:19
  15.9 4.8 %relayout_left.5 = (bf16[2,64,64,128]{3,2,1,0:T(8,128)(2,1)}, bf16[2,64,64,128]{3,2,1,0:T(8,128)(2,1)}) custom-call(s32[128]{0:T(128)} %broadcast_subtract_fusion.perm_ref, s32[1]{0:T(128)} %bitcast.wraps_ref, bf16[2,384,128,128]{3,2,1,0:T(8,128)(2,1)} %bitcast.9), custom_call_target="tpu_custom_call" | custom-call | tf_op jit(solution)/shard_map/relayout_left/pallas_call | solution.py:71
  20.7 4.6 %relayout_right.5 = (bf16[2,64,64,128]{3,2,1,0:T(8,128)(2,1)}, bf16[2,64,64,128]{3,2,1,0:T(8,128)(2,1)}) custom-call(s32[128]{0:T(128)} %broadcast_subtract_fusion.perm_ref, s32[1]{0:T(128)} %bitcast.wraps_ref, bf16[2,8,48,128,128]{4,3,2,1,0:T(8,128)(2,1)} %bitcast.10), custom_call_target="tpu_custom_call" | custom-call | tf_op jit(solution)/shard_map/relayout_right/pallas_call | solution.py:71
  25.3 8.5 %relayout_left.6 = (bf16[2,64,128,128]{3,2,1,0:T(8,128)(2,1)}, bf16[2,64,128,128]{3,2,1,0:T(8,128)(2,1)}) custom-call(s32[128]{0:T(128)} %broadcast_subtract_fusion.perm_ref, s32[1]{0:T(128)} %bitcast.wraps_ref, bf16[2,384,128,128]{3,2,1,0:T(8,128)(2,1)} %bitcast.11), custom_call_target="tpu_custom_call" | custom-call | tf_op jit(solution)/shard_map/relayout_left/pallas_call | solution.py:71
  33.8 8.4 %relayout_right.6 = (bf16[2,64,128,128]{3,2,1,0:T(8,128)(2,1)}, bf16[2,64,128,128]{3,2,1,0:T(8,128)(2,1)}) custom-call(s32[128]{0:T(128)} %broadcast_subtract_fusion.perm_ref, s32[1]{0:T(128)} %bitcast.wraps_ref, bf16[2,8,48,128,128]{4,3,2,1,0:T(8,128)(2,1)} %bitcast.12), custom_call_target="tpu_custom_call" | custom-call | tf_op jit(solution)/shard_map/relayout_right/pallas_call | solution.py:71
  44.4 8.5 %relayout_left.7 = (bf16[2,48,128,128]{3,2,1,0:T(8,128)(2,1)}, bf16[2,16,128,128]{3,2,1,0:T(8,128)(2,1)}, bf16[2,64,128,128]{3,2,1,0:T(8,128)(2,1)}) custom-call(s32[128]{0:T(128)} %broadcast_subtract_fusion.perm_ref, s32[1]{0:T(128)} %bitcast.wraps_ref, bf16[2,384,128,128]{3,2,1,0:T(8,128)(2,1)} %bitcast.13), custom_call_target="tpu_custom_call" | custom-call | tf_op jit(solution)/shard_map/relayout_left/pallas_call | solution.py:71
  53.1 8.4 %relayout_right.7 = (bf16[2,48,128,128]{3,2,1,0:T(8,128)(2,1)}, bf16[2,16,128,128]{3,2,1,0:T(8,128)(2,1)}, bf16[2,64,128,128]{3,2,1,0:T(8,128)(2,1)}) custom-call(s32[128]{0:T(128)} %broadcast_subtract_fusion.perm_ref, s32[1]{0:T(128)} %bitcast.wraps_ref, bf16[2,8,48,128,128]{4,3,2,1,0:T(8,128)(2,1)} %bitcast.14), custom_call_target="tpu_custom_call" | custom-call | tf_op jit(solution)/shard_map/relayout_right/pallas_call | solution.py:71
  63.0 6.0 %collective-permute-start.7 = (bf16[2,48,128,128]{3,2,1,0:T(8,128)(2,1)}, bf16[2,48,128,128]{3,2,1,0:T(8,128)(2,1)S(1)}, u32[]{:S(2)}, u32[]{:S(2)}) collective-permute-start(bf16[2,48,128,128]{3,2,1,0:T(8,128)(2,1)} %get-tuple-element.108), channel_id=1, source_target_pairs={{0,8},{8,16},{16,24},{24,32},{32,40},{40,48},{48,56},{56,64},{64,7... | collective-permute-start | bytes 9437192 | tf_op jit(solution)/shard_map/ppermute | solution.py:19
  69.0 8.8 %products.8 = f32[8,2,16,384]{3,2,1,0:T(8,128)} custom-call(bf16[2,64,64,128]{3,2,1,0:T(8,128)(2,1)} %copy-done.2, bf16[2,64,64,128]{3,2,1,0:T(8,128)(2,1)} %copy-done.3, bf16[2,64,64,128]{3,2,1,0:T(8,128)(2,1)} %get-tuple-element.103.refs_2_.refs_1_, bf16[2,64,64,128]{3,2,1,0:T(8,128)(2,1)} %get-tuple-element.104.refs_3_.refs_2_, ...), custom_call_target="tpu_custom_call" | custom-call | tf_op jit(solution)/shard_map/products/pallas_call | solution.py:139
  77.8 38.7 %collective-permute-done.3.refs_5_ = bf16[2,64,64,128]{3,2,1,0:T(8,128)(2,1)} collective-permute-done((bf16[2,64,64,128]{3,2,1,0:T(8,128)(2,1)}, bf16[2,64,64,128]{3,2,1,0:T(8,128)(2,1)}, u32[]{:S(2)}, u32[]{:S(2)}) %collective-permute-start.3) | collective-permute-done | bytes 2097184 | tf_op jit(solution)/shard_map/ppermute | solution.py:19
  116.5 8.7 %products.9 = f32[8,2,48,128]{3,2,1,0:T(8,128)} custom-call(bf16[2,64,64,128]{3,2,1,0:T(8,128)(2,1)} %get-tuple-element.99.refs_0_, bf16[2,64,64,128]{3,2,1,0:T(8,128)(2,1)} %get-tuple-element.100.refs_1_, bf16[2,64,128,128]{3,2,1,0:T(8,128)(2,1)} %get-tuple-element.101.refs_2_, bf16[2,64,128,128]{3,2,1,0:T(8,128)(2,1)} %get-tuple-element.102.refs_3_, ...), custom_call_target="tpu_custom_call" | custom-call | tf_op jit(solution)/shard_map/products/pallas_call | solution.py:139
  125.2 6.0 %all-to-all-start = ((f32[8,2,48,128]{3,2,1,0:T(8,128)}), f32[8,2,48,128]{3,2,1,0:T(8,128)S(1)}, u32[]{:S(2)}, u32[]{:S(2)}) async-start(f32[8,2,48,128]{3,2,1,0:T(8,128)} %products.9), calls=%async_computation | async-start | bytes 786432 | tf_op jit(solution)/shard_map/all_to_all | solution.py:186
  131.3 5.3 %collective-permute-start.6 = (bf16[2,16,128,128]{3,2,1,0:T(8,128)(2,1)}, bf16[2,16,128,128]{3,2,1,0:T(8,128)(2,1)}, u32[]{:S(2)}, u32[]{:S(2)}) collective-permute-start(bf16[2,16,128,128]{3,2,1,0:T(8,128)(2,1)} %get-tuple-element.107), channel_id=1, source_target_pairs={{0,8},{8,16},{16,24},{24,32},{32,40},{40,48},{48,56},{56,64},{64,7... | collective-permute-start | bytes 3145736 | tf_op jit(solution)/shard_map/ppermute | solution.py:19
  136.6 34.7 %all-to-all-done = f32[8,2,48,128]{3,2,1,0:T(8,128)S(1)} async-done(((f32[8,2,48,128]{3,2,1,0:T(8,128)}), f32[8,2,48,128]{3,2,1,0:T(8,128)S(1)}, u32[]{:S(2)}, u32[]{:S(2)}) %all-to-all-start) | async-done | bytes 393248 | tf_op jit(solution)/shard_map/all_to_all | solution.py:186
  175.5 8.8 %products.10 = f32[8,2,16,384]{3,2,1,0:T(8,128)} custom-call(bf16[2,64,128,128]{3,2,1,0:T(8,128)(2,1)} %collective-permute-done.4.refs_0_, bf16[2,64,64,128]{3,2,1,0:T(8,128)(2,1)} %get-tuple-element.103.refs_2_.refs_1_, bf16[2,64,64,128]{3,2,1,0:T(8,128)(2,1)} %get-tuple-element.104.refs_3_.refs_2_, ...), custom_call_target="tpu_custom_call" | custom-call | tf_op jit(solution)/shard_map/products/pallas_call | solution.py:139
  184.3 8.8 %products.11 = f32[8,2,48,128]{3,2,1,0:T(8,128)} custom-call(bf16[2,64,64,128]{3,2,1,0:T(8,128)(2,1)} %get-tuple-element.99.refs_0_, bf16[2,64,64,128]{3,2,1,0:T(8,128)(2,1)} %get-tuple-element.100.refs_1_, bf16[2,64,128,128]{3,2,1,0:T(8,128)(2,1)} %get-tuple-element.101.refs_2_, bf16[2,64,128,128]{3,2,1,0:T(8,128)(2,1)} %get-tuple-element.102.refs_3_, ...), custom_call_target="tpu_custom_call" | custom-call | tf_op jit(solution)/shard_map/products/pallas_call | solution.py:139
  193.1 12.9 %all_to_all.30 = f32[8,2,48,128]{3,2,1,0:T(8,128)} all-to-all(f32[8,2,48,128]{3,2,1,0:T(8,128)} %products.11), channel_id=1, replica_groups=mesh['kz'=16,'pw'=8] {'pw'}, dimensions={0} | all-to-all | bytes 786432 | tf_op jit(solution)/shard_map/all_to_all | solution.py:186
  210.1 7.5 %products.14.refs_5_ = f32[768,256]{1,0:T(8,128)} custom-call(bf16[2,64,64,128]{3,2,1,0:T(8,128)(2,1)} %get-tuple-element.99.refs_0_, bf16[2,64,64,128]{3,2,1,0:T(8,128)(2,1)} %get-tuple-element.100.refs_1_, bf16[2,64,128,128]{3,2,1,0:T(8,128)(2,1)} %get-tuple-element.101.refs_2_, bf16[2,64,128,128]{3,2,1,0:T(8,128)(2,1)} %get-tuple-element.102.refs_3_, ...), custom_call_target="tpu_custom_call" | custom-call | tf_op jit(solution)/shard_map/products/pallas_call | solution.py:139
  223.5 7.5 %products.12.refs_5_ = f32[256,768]{1,0:T(8,128)} custom-call(bf16[2,48,128,128]{3,2,1,0:T(8,128)(2,1)} %copy-done, bf16[2,64,64,128]{3,2,1,0:T(8,128)(2,1)} %get-tuple-element.103.refs_2_.refs_1_, bf16[2,64,64,128]{3,2,1,0:T(8,128)(2,1)} %get-tuple-element.104.refs_3_.refs_2_, bf16[2,64,128,128]{3,2,1,0:T(8,128)(2,1)} %get-tuple-element.105.refs_4_.refs_3_, ...), custom_call_target="tpu_custom_call" | custom-call | tf_op jit(solution)/shard_map/products/pallas_call | solution.py:139
  230.9 4.2 %products.13 = f32[8,2,16,384]{3,2,1,0:T(8,128)} custom-call(bf16[2,16,128,128]{3,2,1,0:T(8,128)(2,1)} %collective-permute-done.6.refs_0_, bf16[2,64,64,128]{3,2,1,0:T(8,128)(2,1)} %get-tuple-element.103.refs_2_.refs_1_, bf16[2,64,64,128]{3,2,1,0:T(8,128)(2,1)} %get-tuple-element.104.refs_3_.refs_2_, ...), custom_call_target="tpu_custom_call" | custom-call | tf_op jit(solution)/shard_map/products/pallas_call | solution.py:139
  235.1 12.1 %all_to_all.31 = f32[8,2,16,384]{3,2,1,0:T(8,128)S(1)} all-to-all(f32[8,2,16,384]{3,2,1,0:T(8,128)} %products.13), channel_id=1, replica_groups=mesh['kz'=16,'pw'=8] {'pw'}, dimensions={0} | all-to-all | bytes 786432 | tf_op jit(solution)/shard_map/all_to_all | solution.py:184
  258.9 4.8 %collective-permute-done.11 = f32[2,16,384]{2,1,0:T(8,128)S(1)} collective-permute-done((f32[2,16,384]{2,1,0:T(8,128)S(1)}, f32[2,16,384]{2,1,0:T(8,128)S(1)}, u32[]{:S(2)}, u32[]{:S(2)}) %collective-permute-start.11) | collective-permute-done | bytes 49184 | tf_op jit(solution)/shard_map/ppermute | solution.py:19
  (47 shorter events, 32.8 us)
Async XLA Ops:
  5.9 36.8 %collective-permute-start.2 = (bf16[2,64,64,128]{3,2,1,0:T(8,128)(2,1)}, bf16[2,64,64,128]{3,2,1,0:T(8,128)(2,1)S(1)}, u32[]{:S(2)}, u32[]{:S(2)}) collective-permute-start(bf16[2,64,64,128]{3,2,1,0:T(8,128)(2,1)} %get-tuple-element.85), channel_id=1, source_target_pairs={{0,120},{8,0},{16,8},{24,16},{32,24},{40,32},{48,40},{56,48},{64,5... | collective-permute-start | bytes 6291464 | tf_op jit(solution)/shard_map/ppermute | solution.py:19
  11.2 41.7 %collective-permute-start = (bf16[2,64,64,128]{3,2,1,0:T(8,128)(2,1)}, bf16[2,64,64,128]{3,2,1,0:T(8,128)(2,1)S(1)}, u32[]{:S(2)}, u32[]{:S(2)}) collective-permute-start(bf16[2,64,64,128]{3,2,1,0:T(8,128)(2,1)} %get-tuple-element.83), channel_id=1, source_target_pairs={{0,8},{8,16},{16,24},{24,32},{32,40},{40,48},{48,56},{56,64},{64,7... | collective-permute-start | bytes 6291464 | tf_op jit(solution)/shard_map/ppermute | solution.py:19
  25.3 36.4 %collective-permute-start.1 = (bf16[2,64,64,128]{3,2,1,0:T(8,128)(2,1)}, bf16[2,64,64,128]{3,2,1,0:T(8,128)(2,1)S(1)}, u32[]{:S(2)}, u32[]{:S(2)}) collective-permute-start(bf16[2,64,64,128]{3,2,1,0:T(8,128)(2,1)} %get-tuple-element.84), channel_id=1, source_target_pairs={{0,8},{8,16},{16,24},{24,32},{32,40},{40,48},{48,56},{56,64},{64,7... | collective-permute-start | bytes 6291464 | tf_op jit(solution)/shard_map/ppermute | solution.py:19
  42.2 89.1 %collective-permute-start.4 = (bf16[2,64,128,128]{3,2,1,0:T(8,128)(2,1)}, bf16[2,64,128,128]{3,2,1,0:T(8,128)(2,1)}, u32[]{:S(2)}, u32[]{:S(2)}) collective-permute-start(bf16[2,64,128,128]{3,2,1,0:T(8,128)(2,1)} %get-tuple-element.96), channel_id=1, source_target_pairs={{0,8},{8,16},{16,24},{24,32},{32,40},{40,48},{48,56},{56,64},{64,7... | collective-permute-start | bytes 12582920 | tf_op jit(solution)/shard_map/ppermute | solution.py:19
  42.2 142.1 %collective-permute-start.5 = (bf16[2,64,128,128]{3,2,1,0:T(8,128)(2,1)}, bf16[2,64,128,128]{3,2,1,0:T(8,128)(2,1)}, u32[]{:S(2)}, u32[]{:S(2)}) collective-permute-start(bf16[2,64,128,128]{3,2,1,0:T(8,128)(2,1)} %get-tuple-element.97), channel_id=1, source_target_pairs={{0,120},{8,0},{16,8},{24,16},{32,24},{40,32},{48,40},{56,48},{64,5... | collective-permute-start | bytes 12582920 | tf_op jit(solution)/shard_map/ppermute | solution.py:19
  42.7 10.2 %copy-start.1 = (bf16[2,64,64,128]{3,2,1,0:T(8,128)(2,1)}, bf16[2,64,64,128]{3,2,1,0:T(8,128)(2,1)S(1)}, u32[]{:S(2)}) copy-start(bf16[2,64,64,128]{3,2,1,0:T(8,128)(2,1)S(1)} %collective-permute-done.2.refs_4_) | copy-start | bytes 6291460
  42.7 73.8 %collective-permute-start.3 = (bf16[2,64,64,128]{3,2,1,0:T(8,128)(2,1)}, bf16[2,64,64,128]{3,2,1,0:T(8,128)(2,1)}, u32[]{:S(2)}, u32[]{:S(2)}) collective-permute-start(bf16[2,64,64,128]{3,2,1,0:T(8,128)(2,1)} %get-tuple-element.86), channel_id=1, source_target_pairs={{0,120},{8,0},{16,8},{24,16},{32,24},{40,32},{48,40},{56,48},{64,5... | collective-permute-start | bytes 6291464 | tf_op jit(solution)/shard_map/ppermute | solution.py:19
  52.9 8.6 %copy-start.2 = (bf16[2,64,64,128]{3,2,1,0:T(8,128)(2,1)}, bf16[2,64,64,128]{3,2,1,0:T(8,128)(2,1)S(1)}, u32[]{:S(2)}) copy-start(bf16[2,64,64,128]{3,2,1,0:T(8,128)(2,1)S(1)} %collective-permute-done.refs_0_) | copy-start | bytes 6291460
  52.9 157.1 %collective-permute-start.9 = (bf16[2,48,128,128]{3,2,1,0:T(8,128)(2,1)}, bf16[2,48,128,128]{3,2,1,0:T(8,128)(2,1)}, u32[]{:S(2)}, u32[]{:S(2)}) collective-permute-start(bf16[2,48,128,128]{3,2,1,0:T(8,128)(2,1)} %get-tuple-element.110), channel_id=1, source_target_pairs={{0,120},{8,0},{16,8},{24,16},{32,24},{40,32},{48,40},{56,48},{64,5... | collective-permute-start | bytes 9437192 | tf_op jit(solution)/shard_map/ppermute | solution.py:19
  61.6 1.3 copy-start.3
  63.0 158.8 %collective-permute-start.7 = (bf16[2,48,128,128]{3,2,1,0:T(8,128)(2,1)}, bf16[2,48,128,128]{3,2,1,0:T(8,128)(2,1)S(1)}, u32[]{:S(2)}, u32[]{:S(2)}) collective-permute-start(bf16[2,48,128,128]{3,2,1,0:T(8,128)(2,1)} %get-tuple-element.108), channel_id=1, source_target_pairs={{0,8},{8,16},{16,24},{24,32},{32,40},{40,48},{48,56},{56,64},{64,7... | collective-permute-start | bytes 9437192 | tf_op jit(solution)/shard_map/ppermute | solution.py:19
  125.2 46.1 %all-to-all-start = ((f32[8,2,48,128]{3,2,1,0:T(8,128)}), f32[8,2,48,128]{3,2,1,0:T(8,128)S(1)}, u32[]{:S(2)}, u32[]{:S(2)}) async-start(f32[8,2,48,128]{3,2,1,0:T(8,128)} %products.9), calls=%async_computation | async-start | bytes 786432 | tf_op jit(solution)/shard_map/all_to_all | solution.py:186
  131.3 86.3 %collective-permute-start.8 = (bf16[2,16,128,128]{3,2,1,0:T(8,128)(2,1)}, bf16[2,16,128,128]{3,2,1,0:T(8,128)(2,1)}, u32[]{:S(2)}, u32[]{:S(2)}) collective-permute-start(bf16[2,16,128,128]{3,2,1,0:T(8,128)(2,1)} %get-tuple-element.109), channel_id=1, source_target_pairs={{0,120},{8,0},{16,8},{24,16},{32,24},{40,32},{48,40},{56,48},{64,5... | collective-permute-start | bytes 3145736 | tf_op jit(solution)/shard_map/ppermute | solution.py:19
  131.3 99.6 %collective-permute-start.6 = (bf16[2,16,128,128]{3,2,1,0:T(8,128)(2,1)}, bf16[2,16,128,128]{3,2,1,0:T(8,128)(2,1)}, u32[]{:S(2)}, u32[]{:S(2)}) collective-permute-start(bf16[2,16,128,128]{3,2,1,0:T(8,128)(2,1)} %get-tuple-element.107), channel_id=1, source_target_pairs={{0,8},{8,16},{16,24},{24,32},{32,40},{40,48},{48,56},{56,64},{64,7... | collective-permute-start | bytes 3145736 | tf_op jit(solution)/shard_map/ppermute | solution.py:19
  171.4 21.7 %all-to-all-start.3 = ((f32[8,2,16,384]{3,2,1,0:T(8,128)}), f32[8,2,16,384]{3,2,1,0:T(8,128)}, u32[]{:S(2)}, u32[]{:S(2)}) async-start(f32[8,2,16,384]{3,2,1,0:T(8,128)} %products.8), calls=%async_computation.3 | async-start | bytes 786432 | tf_op jit(solution)/shard_map/all_to_all | solution.py:184
  206.0 29.2 %all-to-all-start.4 = ((f32[8,2,16,384]{3,2,1,0:T(8,128)}), f32[8,2,16,384]{3,2,1,0:T(8,128)}, u32[]{:S(2)}, u32[]{:S(2)}) async-start(f32[8,2,16,384]{3,2,1,0:T(8,128)} %products.10), calls=%async_computation.4 | async-start | bytes 786432 | tf_op jit(solution)/shard_map/all_to_all | solution.py:184
  221.8 1.7 copy-start
  235.1 21.6 %copy-start.4 = (f32[8,2,48,128]{3,2,1,0:T(8,128)S(1)}, f32[8,2,48,128]{3,2,1,0:T(8,128)}, u32[]{:S(2)}) copy-start(f32[8,2,48,128]{3,2,1,0:T(8,128)} %all_to_all.30) | copy-start | bytes 1179652
  247.3 10.2 %all-to-all-start.2 = ((f32[8,2,48,128]{3,2,1,0:T(8,128)}), f32[8,2,48,128]{3,2,1,0:T(8,128)S(1)}, u32[]{:S(2)}, u32[]{:S(2)}) async-start(f32[8,2,48,128]{3,2,1,0:T(8,128)} %products.15), calls=%async_computation.2 | async-start | bytes 786432 | tf_op jit(solution)/shard_map/all_to_all | solution.py:186
  251.7 7.2 %collective-permute-start.10 = (f32[2,16,384]{2,1,0:T(8,128)S(1)}, f32[2,16,384]{2,1,0:T(8,128)S(1)}, u32[]{:S(2)}, u32[]{:S(2)}) collective-permute-start(f32[2,16,384]{2,1,0:T(8,128)S(1)} %reduce_sum.57), channel_id=1, source_target_pairs={{0,120},{8,0},{16,8},{24,16},{32,24},{40,32},{48,40},{56,48},{64,5... | collective-permute-start | bytes 147464 | tf_op jit(solution)/shard_map/ppermute | solution.py:19
  256.5 7.2 %collective-permute-start.11 = (f32[2,16,384]{2,1,0:T(8,128)S(1)}, f32[2,16,384]{2,1,0:T(8,128)S(1)}, u32[]{:S(2)}, u32[]{:S(2)}) collective-permute-start(f32[2,16,384]{2,1,0:T(8,128)S(1)} %reduce_sum.58), channel_id=1, source_target_pairs={{0,120},{8,0},{16,8},{24,16},{32,24},{40,32},{48,40},{56,48},{64,5... | collective-permute-start | bytes 147464 | tf_op jit(solution)/shard_map/ppermute | solution.py:19
  256.6 7.6 %collective-permute-start.12 = (f32[2,16,384]{2,1,0:T(8,128)S(1)}, f32[2,16,384]{2,1,0:T(8,128)S(1)}, u32[]{:S(2)}, u32[]{:S(2)}) collective-permute-start(f32[2,16,384]{2,1,0:T(8,128)S(1)} %reduce_sum.59), channel_id=1, source_target_pairs={{0,120},{8,0},{16,8},{24,16},{32,24},{40,32},{48,40},{56,48},{64,5... | collective-permute-start | bytes 147464 | tf_op jit(solution)/shard_map/ppermute | solution.py:19

commit v2 on v1

v2 whole, which is shorter than its diff:
```python
import jax
import jax.numpy as jnp
from jax import lax
from jax.experimental import pallas as pl
from jax.experimental.pallas import tpu as pltpu
from jax.sharding import PartitionSpec as P

SUB = 64
LANES = 128
PITCH = SUB + 1
CHUNKS = ((0, 1, (64,)), (1, 1, (64,)), (2, 2, (64,)), (4, 2, (48, 16)))
GROUPS = ((0, 1), (2,), (3,))
STEP = 16
RELAYOUT_COST = 5_000_000_000
PRODUCT_COST = 3
PARAMS = pltpu.CompilerParams(vmem_limit_bytes=56 << 20)


def shifted(value, axis, steps):
    count = lax.axis_size(axis)
    return lax.ppermute(value, axis, [(s, (s + steps) % count) for s in range(count)])


def relayout(states, perm, wraps, chunk, left):
    first, units, pieces = chunk
    sticks = states.shape[2]
    half = sticks // 2
    bands = units * SUB

    def body(perm_ref, wraps_ref, x_ref, *refs):
        outs, scratch = refs[:-1], refs[-1]
        x = x_ref.at[0]
        for m in range(SUB):
            row = x[m] if left else x[m // 8, m % 8]
            scratch[pl.ds(m, sticks, stride=PITCH), :] = row.astype(jnp.float32)

        def put(s, value):
            value = value.astype(jnp.bfloat16)
            sent = s < half if left else s >= half
            if not sent:
                outs[-1][0, s % half] = value
                return
            at = s % half
            for piece, size in enumerate(pieces):
                if at < size:
                    outs[piece][0, at] = value
                    return
                at -= size

        def plain():
            for s in range(sticks):
                put(s, scratch[pl.ds(s * PITCH, SUB), :])

        def wrapped():
            keep = lax.broadcasted_iota(jnp.int32, (SUB, LANES), 1) < LANES - 1
            for s in range(sticks):
                value = scratch[pl.ds(perm_ref[s] * PITCH, SUB), :]
                put(s, jnp.where(keep, pltpu.roll(value, LANES - 1, 1), 0.0))

        if left:
            pl.when(wraps_ref[0] == 0)(plain)
            pl.when(wraps_ref[0] != 0)(wrapped)
        else:
            plain()

    if left:
        view = states
        in_spec = pl.BlockSpec((1, SUB, sticks, LANES), lambda c, g, *_: (c, first + g, 0, 0))
    else:
        view = states.reshape(2, 8, states.shape[1] // 8, sticks, LANES)
        in_spec = pl.BlockSpec((1, 8, 8, sticks, LANES), lambda c, g, *_: (c, 0, first + g, 0, 0))
    sizes = (*pieces, half)
    return pl.pallas_call(
        body,
        grid_spec=pltpu.PrefetchScalarGridSpec(
            num_scalar_prefetch=2,
            grid=(2, units),
            in_specs=[in_spec],
            out_specs=[pl.BlockSpec((1, n, SUB, LANES), lambda c, g, *_: (c, 0, g, 0)) for n in sizes],
            scratch_shapes=[pltpu.VMEM((sticks * PITCH, LANES), jnp.float32)],
        ),
        out_shape=[jax.ShapeDtypeStruct((2, n, bands, LANES), jnp.bfloat16) for n in sizes],
        compiler_params=PARAMS,
        cost_estimate=pl.CostEstimate(flops=RELAYOUT_COST * units, transcendentals=0, bytes_accessed=8 * bands * sticks * LANES),
        name="relayout_left" if left else "relayout_right",
    )(perm, wraps, view)


def products(left, right, start, finish):
    sides = (left, right)
    steps = left[3] // STEP
    heights = [sum(r.shape[2] for r in rows) for rows, *_ in sides]
    widths = [sum(c.shape[2] for c in columns) for _, columns, *_ in sides]
    shapes = [(2 * h, 2 * w) for h, w in zip(heights, widths)]

    def stack(refs):
        return jnp.concatenate(
            [jnp.concatenate([r[c, j] for j in range(STEP)], -1) for c in range(2) for r in refs], 0
        )

    def body(*refs):
        refs = list(refs)
        take = lambda n: [refs.pop(0) for _ in range(n)]
        operands = [(take(len(rows)), take(len(columns))) for rows, columns, *_ in sides]
        starts = take(2) if start else None
        outs = take(1) if finish else take(2)
        totals = take(2)
        step = pl.program_id(0)
        for side, (rows, columns) in enumerate(operands):
            new = lax.dot_general(
                stack(rows), stack(columns), (((1,), (1,)), ((), ())), preferred_element_type=jnp.float32
            )

            @pl.when(step == 0)
            def _():
                totals[side][...] = starts[side][...] + new if start else new

            @pl.when(step > 0)
            def _():
                totals[side][...] += new

        @pl.when(step == steps - 1)
        def _():
            for side in range(2):
                total, h, w = totals[side], heights[side], widths[side]
                if not finish:
                    outs[side][...] = total[...]
                    continue
                real = total[:h, :w] + total[h:, w:]
                imag = total[:h, w:] - total[h:, :w]
                for part, value in enumerate((real, imag)):
                    for u in range(h // SUB):
                        for q in range(8):
                            block = value[u * SUB + q * 8 : u * SUB + q * 8 + 8]
                            for n in range(w // LANES):
                                at = (n * (h // SUB) + u) * 8
                                outs[0][q, side, part, at : at + 8] = block[:, n * LANES : (n + 1) * LANES]

    def spec(array, offset):
        return pl.BlockSpec((2, STEP, array.shape[2], LANES), lambda s: (0, offset // STEP + s, 0, 0))

    in_specs, operands = [], []
    for rows, columns, (row_offset, column_offset), _ in sides:
        in_specs += [spec(r, row_offset) for r in rows] + [spec(c, column_offset) for c in columns]
        operands += [*rows, *columns]
    whole = [pl.BlockSpec(shape, lambda s: (0, 0)) for shape in shapes]
    if start:
        in_specs += whole
        operands += start
    if finish:
        out_shape = [(8, 2, 2, 48, LANES)]
        out_specs = [pl.BlockSpec(out_shape[0], lambda s: (0, 0, 0, 0, 0))]
    else:
        out_shape, out_specs = shapes, whole
    return pl.pallas_call(
        body,
        grid=(steps,),
        in_specs=in_specs,
        out_specs=out_specs,
        out_shape=[jax.ShapeDtypeStruct(shape, jnp.float32) for shape in out_shape],
        scratch_shapes=[pltpu.VMEM(shape, jnp.float32) for shape in shapes],
        compiler_params=PARAMS,
        cost_estimate=pl.CostEstimate(
            flops=PRODUCT_COST * 2 * steps * STEP * LANES * sum(h * w for h, w in shapes),
            transcendentals=0,
            bytes_accessed=4 * steps * STEP * LANES * sum(h + w for h, w in shapes),
        ),
        name="products",
    )(*operands)


def after(value, *others):
    return lax.optimization_barrier((value, others))[0]


def reduced(total):
    return lax.all_to_all(total, "pw", 0, 0, tiled=True).sum(0)


def reduced_in_two(total):
    count = lax.axis_size("pw")
    groups = [list(range(p, count, 2)) for p in range(2)]
    halves = total.reshape(count // 2, 2, *total.shape[1:])
    halves = lax.all_to_all(halves, "pw", 0, 0, axis_index_groups=groups, tiled=True).sum(0)
    side = lax.axis_index("pw") % 2
    kept = lax.dynamic_index_in_dim(halves, side, 0, keepdims=False)
    sent = lax.dynamic_index_in_dim(halves, 1 - side, 0, keepdims=False)
    return kept + lax.ppermute(sent, "pw", [(p, p ^ 1) for p in range(count)])


def shards(states, stick_perm):
    states = states[0]
    sticks = states.shape[2]
    perm = stick_perm - lax.axis_index("pw") * sticks
    token = (lax.axis_index("kz") == 0).astype(jnp.int32).reshape(1)
    columns, rows, from_right, from_left = [], [], [], []
    for index, chunk in enumerate(CHUNKS):
        for left in (True, False):
            if index > 1:
                token = after(token, (from_right if left else from_left)[index - 2][0])
            *sent, kept = relayout(states, perm, token, chunk, left)
            token, kept = lax.optimization_barrier((token, kept))
            (columns if left else rows).append(kept)
            for piece in range(1, len(sent)):
                sent[piece] = after(sent[piece], (from_right if left else from_left)[index - 1][0])
            (from_right if left else from_left).append([shifted(p, "kz", -1 if left else 1) for p in sent])

    left_parts, right_parts = [], []
    for group in GROUPS:
        offset, totals = 0, None
        pieces = CHUNKS[group[0]][2]
        for index, size in enumerate(pieces):
            last = index == len(pieces) - 1
            arrived = [[side[c][index] for c in group] for side in (from_right, from_left)]
            if index:
                arrived, left_parts, right_parts = lax.optimization_barrier((arrived, left_parts, right_parts))
            totals = products(
                (rows, arrived[0], (offset, 0), size), (arrived[1], columns, (0, offset), size), totals, last
            )
            offset += size
        rows, columns, totals = lax.optimization_barrier((rows, columns, totals))
        mine = reduced(totals[0]) if group == GROUPS[-1] else reduced_in_two(totals[0])
        left_parts.append(mine[0])
        right_parts.append(shifted(mine[1], "kz", -1))
    right_parts = [jnp.concatenate([r[:, 16 * n : 16 * n + 16] for n in range(3)], 2) for r in right_parts]
    margin = jnp.concatenate(left_parts, 2) + jnp.concatenate(right_parts, 1)
    return jnp.transpose(margin, (1, 0, 2))[:, None]


def solution(mesh):
    in_specs = (P("kz", None, None, "pw", None), P("pw"))
    out_specs = P("pw", "kz", None, None)
    return jax.shard_map(shards, mesh=mesh, in_specs=in_specs, out_specs=out_specs, check_vma=False)
```

time: 266 us -> 203 us (0.76)
  waiting for transfers between devices: 81 us -> 36.8 us
  blocking collectives: 25 us -> 15.7 us
  starting transfers between devices: 40.7 us -> 32.4 us
  Pallas kernels: 111 us -> 114 us
    all_to_all x4 -> x2, waiting for transfers between devices: 35.4 us -> 0.01 us  [reduced_in_two(): lax.all_to_all(halves, 'pw', 0, 0, axis_index_groups=groups, tiled=True)]
    ppermute x13, waiting for transfers between devices: 45.6 us -> 24.6 us  [shifted(): lax.ppermute(value, axis, [(s, (s + steps) % count) for s in range(count)])]
    ppermute x0 -> x2, waiting for transfers between devices: none -> 12.2 us  [reduced_in_two(): return kept + lax.ppermute(sent, 'pw', [(p, p ^ 1) for p in range(count)])]
    all_to_all x2 -> x1, blocking collectives: 25 us -> 15.7 us  [reduced(): return lax.all_to_all(total, 'pw', 0, 0, tiled=True).sum(0)]
    all_to_all x4 -> x2, starting transfers between devices: 17.7 us -> 10.2 us  [reduced_in_two(): lax.all_to_all(halves, 'pw', 0, 0, axis_index_groups=groups, tiled=True)]
    pallas_call x8 -> x4, Pallas kernels: 58.4 us -> 61.8 us  [products(): pl.pallas_call(body, grid=(steps,), in_specs=in_specs, out_specs=out_spec...]
    ppermute x13, starting transfers between devices: 23 us -> 19.7 us  [shifted(): lax.ppermute(value, axis, [(s, (s + steps) % count) for s in range(count)])]
  transfers between devices with their start and end apart: 17 -> 17, of which waited for: 7 -> 6; matrix products, arithmetic and copies ran while one was open for 1% -> 0% of each run, Pallas kernels for 40% -> 51%
where the time goes in v2:
time: 203 us
  Pallas kernels  114 us (56%)
  waiting for transfers between devices  36.8 us (18%)
  starting transfers between devices  32.4 us (16%)
  blocking collectives  15.7 us (8%)
  local copies, waits for them, and re-layouts  2.14 us (1%)
    pallas_call x4, Pallas kernels, products(): pl.pallas_call(body, grid=(steps,), in_specs=in_specs, out_specs=out_spec...  61.8 us
    pallas_call x8, Pallas kernels, relayout(): pl.pallas_call(body, grid_spec=pltpu.PrefetchScalarGridSpec(num_scalar_pr...  52.5 us
    ppermute x13, waiting for transfers between devices, shifted(): lax.ppermute(value, axis, [(s, (s + steps) % count) for s in range(count)])  24.6 us
    ppermute x13, starting transfers between devices, shifted(): lax.ppermute(value, axis, [(s, (s + steps) % count) for s in range(count)])  19.7 us
    all_to_all x1, blocking collectives, reduced(): return lax.all_to_all(total, 'pw', 0, 0, tiled=True).sum(0)  15.7 us
    ppermute x2, waiting for transfers between devices, reduced_in_two(): return kept + lax.ppermute(sent, 'pw', [(p, p ^ 1) for p in range(count)])  12.2 us
    all_to_all x2, starting transfers between devices, reduced_in_two(): lax.all_to_all(halves, 'pw', 0, 0, axis_index_groups=groups, tiled=True)  10.2 us
  transfers between devices with their start and end apart: 17, of which 6 were waited for; matrix products, arithmetic and copies ran while one was open for 0% of the time, Pallas kernels for 51%

profile of v2, /device:TPU:7, one launch (start us, length us, event | category | flops | bytes accessed | tf_op | source)
XLA Modules:
  0.0 202.9 jit_solution(7691289638514791629)
XLA Ops:
  1.2 4.7 %relayout_left.4 = (bf16[2,64,64,128]{3,2,1,0:T(8,128)(2,1)}, bf16[2,64,64,128]{3,2,1,0:T(8,128)(2,1)}) custom-call(s32[128]{0:T(128)} %broadcast_subtract_fusion.perm_ref, s32[1]{0:T(128)} %bitcast.wraps_ref, bf16[2,384,128,128]{3,2,1,0:T(8,128)(2,1)} %bitcast.29), custom_call_target="tpu_custom_call" | custom-call | flops 5000000000 | bytes 8388608 | tf_op jit(solution)/shard_map/relayout_left/pallas_call | solution.py:73
  6.6 4.6 %relayout_right.4 = (bf16[2,64,64,128]{3,2,1,0:T(8,128)(2,1)}, bf16[2,64,64,128]{3,2,1,0:T(8,128)(2,1)}) custom-call(s32[128]{0:T(128)} %broadcast_subtract_fusion.perm_ref, s32[1]{0:T(128)} %bitcast.wraps_ref, bf16[2,8,48,128,128]{4,3,2,1,0:T(8,128)(2,1)} %bitcast.30), custom_call_target="tpu_custom_call" | custom-call | flops 5000000000 | bytes 8388608 | tf_op jit(solution)/shard_map/relayout_right/pallas_call | solution.py:73
  11.2 4.7 %collective-permute-start.1 = (bf16[2,64,64,128]{3,2,1,0:T(8,128)(2,1)}, bf16[2,64,64,128]{3,2,1,0:T(8,128)(2,1)S(1)}, u32[]{:S(2)}, u32[]{:S(2)}) collective-permute-start(bf16[2,64,64,128]{3,2,1,0:T(8,128)(2,1)} %get-tuple-element.83), channel_id=1, source_target_pairs={{0,8},{8,16},{16,24},{24,32},{32,40},{40,48},{48,56},{56,64},{64,7... | collective-permute-start | bytes 6291464 | tf_op jit(solution)/shard_map/ppermute | solution.py:21
  15.9 4.7 %relayout_left.5 = (bf16[2,64,64,128]{3,2,1,0:T(8,128)(2,1)}, bf16[2,64,64,128]{3,2,1,0:T(8,128)(2,1)}) custom-call(s32[128]{0:T(128)} %broadcast_subtract_fusion.perm_ref, s32[1]{0:T(128)} %bitcast.wraps_ref, bf16[2,384,128,128]{3,2,1,0:T(8,128)(2,1)} %bitcast.31), custom_call_target="tpu_custom_call" | custom-call | flops 5000000000 | bytes 8388608 | tf_op jit(solution)/shard_map/relayout_left/pallas_call | solution.py:73
  20.6 4.7 %relayout_right.5 = (bf16[2,64,64,128]{3,2,1,0:T(8,128)(2,1)}, bf16[2,64,64,128]{3,2,1,0:T(8,128)(2,1)}) custom-call(s32[128]{0:T(128)} %broadcast_subtract_fusion.perm_ref, s32[1]{0:T(128)} %bitcast.wraps_ref, bf16[2,8,48,128,128]{4,3,2,1,0:T(8,128)(2,1)} %bitcast.32), custom_call_target="tpu_custom_call" | custom-call | flops 5000000000 | bytes 8388608 | tf_op jit(solution)/shard_map/relayout_right/pallas_call | solution.py:73
  25.2 5.4 %collective-permute-start.5 = (bf16[2,64,64,128]{3,2,1,0:T(8,128)(2,1)}, bf16[2,64,64,128]{3,2,1,0:T(8,128)(2,1)}, u32[]{:S(2)}, u32[]{:S(2)}) collective-permute-start(bf16[2,64,64,128]{3,2,1,0:T(8,128)(2,1)} %get-tuple-element.94), channel_id=1, source_target_pairs={{0,8},{8,16},{16,24},{24,32},{32,40},{40,48},{48,56},{56,64},{64,7... | collective-permute-start | bytes 6291464 | tf_op jit(solution)/shard_map/ppermute | solution.py:21
  30.6 4.6 %collective-permute-done.refs_4_ = bf16[2,64,64,128]{3,2,1,0:T(8,128)(2,1)S(1)} collective-permute-done((bf16[2,64,64,128]{3,2,1,0:T(8,128)(2,1)}, bf16[2,64,64,128]{3,2,1,0:T(8,128)(2,1)S(1)}, u32[]{:S(2)}, u32[]{:S(2)}) %collective-permute-start) | collective-permute-done | bytes 2097184 | tf_op jit(solution)/shard_map/ppermute | solution.py:21
  35.2 8.5 %relayout_left.6 = (bf16[2,64,128,128]{3,2,1,0:T(8,128)(2,1)}, bf16[2,64,128,128]{3,2,1,0:T(8,128)(2,1)}) custom-call(s32[128]{0:T(128)} %broadcast_subtract_fusion.perm_ref, s32[1]{0:T(128)} %bitcast.wraps_ref, bf16[2,384,128,128]{3,2,1,0:T(8,128)(2,1)} %bitcast.33), custom_call_target="tpu_custom_call" | custom-call | flops 10000000000 | bytes 16777216 | tf_op jit(solution)/shard_map/relayout_left/pallas_call | solution.py:73
  43.7 8.4 %relayout_right.6 = (bf16[2,64,128,128]{3,2,1,0:T(8,128)(2,1)}, bf16[2,64,128,128]{3,2,1,0:T(8,128)(2,1)}) custom-call(s32[128]{0:T(128)} %broadcast_subtract_fusion.perm_ref, s32[1]{0:T(128)} %bitcast.wraps_ref, bf16[2,8,48,128,128]{4,3,2,1,0:T(8,128)(2,1)} %bitcast.34), custom_call_target="tpu_custom_call" | custom-call | flops 10000000000 | bytes 16777216 | tf_op jit(solution)/shard_map/relayout_right/pallas_call | solution.py:73
  53.6 4.0 %collective-permute-done.2.refs_5_ = bf16[2,64,64,128]{3,2,1,0:T(8,128)(2,1)S(1)} collective-permute-done((bf16[2,64,64,128]{3,2,1,0:T(8,128)(2,1)}, bf16[2,64,64,128]{3,2,1,0:T(8,128)(2,1)S(1)}, u32[]{:S(2)}, u32[]{:S(2)}) %collective-permute-start.2) | collective-permute-done | bytes 2097184 | tf_op jit(solution)/shard_map/ppermute | solution.py:21
  57.6 8.5 %relayout_left.7 = (bf16[2,48,128,128]{3,2,1,0:T(8,128)(2,1)}, bf16[2,16,128,128]{3,2,1,0:T(8,128)(2,1)}, bf16[2,64,128,128]{3,2,1,0:T(8,128)(2,1)}) custom-call(s32[128]{0:T(128)} %broadcast_subtract_fusion.perm_ref, s32[1]{0:T(128)} %bitcast.wraps_ref, bf16[2,384,128,128]{3,2,1,0:T(8,128)(2,1)} %bitcast.35), custom_call_target="tpu_custom_call" | custom-call | flops 10000000000 | bytes 16777216 | tf_op jit(solution)/shard_map/relayout_left/pallas_call | solution.py:73
  66.1 8.4 %relayout_right.7 = (bf16[2,48,128,128]{3,2,1,0:T(8,128)(2,1)}, bf16[2,16,128,128]{3,2,1,0:T(8,128)(2,1)}, bf16[2,64,128,128]{3,2,1,0:T(8,128)(2,1)}) custom-call(s32[128]{0:T(128)} %broadcast_subtract_fusion.perm_ref, s32[1]{0:T(128)} %bitcast.wraps_ref, bf16[2,8,48,128,128]{4,3,2,1,0:T(8,128)(2,1)} %bitcast.36), custom_call_target="tpu_custom_call" | custom-call | flops 10000000000 | bytes 16777216 | tf_op jit(solution)/shard_map/relayout_right/pallas_call | solution.py:73
  74.6 19.6 %products.4 = f32[8,2,2,48,128]{4,3,2,1,0:T(8,128)} custom-call(bf16[2,64,64,128]{3,2,1,0:T(8,128)(2,1)} %get-tuple-element.120.refs_0_, bf16[2,64,64,128]{3,2,1,0:T(8,128)(2,1)} %get-tuple-element.121.refs_1_, bf16[2,64,128,128]{3,2,1,0:T(8,128)(2,1)} %get-tuple-element.122.refs_2_, bf16[2,64,128,128]{3,2,1,0:T(8,128)(2,1)} %get-tuple-element.123.refs_3_, ...), custom_call_target="tpu_custom_call" | custom-call | flops 19327352832 | bytes 67108864 | tf_op jit(solution)/shard_map/products/pallas_call | solution.py:155
  94.2 5.0 %all-to-all-start = ((f32[4,2,2,2,48,128]{5,4,3,2,1,0:T(8,128)}), f32[4,2,2,2,48,128]{5,4,3,2,1,0:T(8,128)S(1)}, u32[]{:S(2)}, u32[]{:S(2)}) async-start(f32[4,2,2,2,48,128]{5,4,3,2,1,0:T(8,128)} %bitcast.38), calls=%async_computation | async-start | bytes 1572864 | tf_op jit(solution)/shard_map/all_to_all | solution.py:184
  101.1 5.5 %collective-permute-done.6.refs_5_ = bf16[2,64,128,128]{3,2,1,0:T(8,128)(2,1)} collective-permute-done((bf16[2,64,128,128]{3,2,1,0:T(8,128)(2,1)}, bf16[2,64,128,128]{3,2,1,0:T(8,128)(2,1)}, u32[]{:S(2)}, u32[]{:S(2)}) %collective-permute-start.6) | collective-permute-done | bytes 4194336 | tf_op jit(solution)/shard_map/ppermute | solution.py:21
  106.6 19.6 %products.5 = f32[8,2,2,48,128]{4,3,2,1,0:T(8,128)} custom-call(bf16[2,64,64,128]{3,2,1,0:T(8,128)(2,1)} %get-tuple-element.120.refs_0_, bf16[2,64,64,128]{3,2,1,0:T(8,128)(2,1)} %get-tuple-element.121.refs_1_, bf16[2,64,128,128]{3,2,1,0:T(8,128)(2,1)} %get-tuple-element.122.refs_2_, bf16[2,64,128,128]{3,2,1,0:T(8,128)(2,1)} %get-tuple-element.123.refs_3_, ...), custom_call_target="tpu_custom_call" | custom-call | flops 19327352832 | bytes 67108864 | tf_op jit(solution)/shard_map/products/pallas_call | solution.py:155
  126.2 5.2 %all-to-all-start.1 = ((f32[4,2,2,2,48,128]{5,4,3,2,1,0:T(8,128)}), f32[4,2,2,2,48,128]{5,4,3,2,1,0:T(8,128)S(1)}, u32[]{:S(2)}, u32[]{:S(2)}) async-start(f32[4,2,2,2,48,128]{5,4,3,2,1,0:T(8,128)} %bitcast.37), calls=%async_computation.1 | async-start | bytes 1572864 | tf_op jit(solution)/shard_map/all_to_all | solution.py:184
  132.8 12.2 %collective-permute-done.8 = f32[2,2,48,128]{3,2,1,0:T(8,128)S(1)} collective-permute-done((f32[2,2,48,128]{3,2,1,0:T(8,128)S(1)}, f32[2,2,48,128]{3,2,1,0:T(8,128)S(1)}, u32[]{:S(2)}, u32[]{:S(2)}) %collective-permute-start.8) | collective-permute-done | bytes 98336 | tf_op jit(solution)/shard_map/ppermute | solution.py:188
  147.1 4.7 %collective-permute-start.7 = (bf16[2,16,128,128]{3,2,1,0:T(8,128)(2,1)}, bf16[2,16,128,128]{3,2,1,0:T(8,128)(2,1)S(1)}, u32[]{:S(2)}, u32[]{:S(2)}) collective-permute-start(bf16[2,16,128,128]{3,2,1,0:T(8,128)(2,1)} %get-tuple-element.98), channel_id=1, source_target_pairs={{0,8},{8,16},{16,24},{24,32},{32,40},{40,48},{48,56},{56,64},{64,7... | collective-permute-start | bytes 3145736 | tf_op jit(solution)/shard_map/ppermute | solution.py:21
  151.9 16.0 %products.6 = (f32[768,256]{1,0:T(8,128)}, f32[256,768]{1,0:T(8,128)}) custom-call(bf16[2,64,64,128]{3,2,1,0:T(8,128)(2,1)} %get-tuple-element.120.refs_0_, bf16[2,64,64,128]{3,2,1,0:T(8,128)(2,1)} %get-tuple-element.121.refs_1_, bf16[2,64,128,128]{3,2,1,0:T(8,128)(2,1)} %get-tuple-element.122.refs_2_, bf16[2,64,128,128]{3,2,1,0:T(8,128)(2,1)} %get-tuple-element.123.refs_3_, ...), custom_call_target="tpu_custom_call" | custom-call | flops 14495514624 | bytes 50331648 | tf_op jit(solution)/shard_map/products/pallas_call | solution.py:155
  167.9 2.2 %collective-permute-done.11 = f32[2,48,128]{2,1,0:T(8,128)S(1)} collective-permute-done((f32[2,48,128]{2,1,0:T(8,128)S(1)}, f32[2,48,128]{2,1,0:T(8,128)S(1)}, u32[]{:S(2)}, u32[]{:S(2)}) %collective-permute-start.11) | collective-permute-done | bytes 49184 | tf_op jit(solution)/shard_map/ppermute | solution.py:21
  171.5 6.6 %products.7 = f32[8,2,2,48,128]{4,3,2,1,0:T(8,128)} custom-call(bf16[2,64,64,128]{3,2,1,0:T(8,128)(2,1)} %get-tuple-element.120.refs_0_, bf16[2,64,64,128]{3,2,1,0:T(8,128)(2,1)} %get-tuple-element.121.refs_1_, bf16[2,64,128,128]{3,2,1,0:T(8,128)(2,1)} %get-tuple-element.122.refs_2_, bf16[2,64,128,128]{3,2,1,0:T(8,128)(2,1)} %get-tuple-element.123.refs_3_, ...), custom_call_target="tpu_custom_call" | custom-call | flops 4831838208 | bytes 16777216 | tf_op jit(solution)/shard_map/products/pallas_call | solution.py:155
  178.0 15.7 %all_to_all.15 = f32[8,2,2,48,128]{4,3,2,1,0:T(8,128)S(1)} all-to-all(f32[8,2,2,48,128]{4,3,2,1,0:T(8,128)} %products.7), channel_id=1, replica_groups=mesh['kz'=16,'pw'=8] {'pw'}, dimensions={0} | all-to-all | bytes 1572864 | tf_op jit(solution)/shard_map/all_to_all | solution.py:177
  193.9 8.2 %collective-permute-done.14 = f32[2,48,128]{2,1,0:T(8,128)S(1)} collective-permute-done((f32[2,48,128]{2,1,0:T(8,128)S(1)}, f32[2,48,128]{2,1,0:T(8,128)S(1)}, u32[]{:S(2)}, u32[]{:S(2)}) %collective-permute-start.14) | collective-permute-done | bytes 49184 | tf_op jit(solution)/shard_map/ppermute | solution.py:21
  (50 shorter events, 11.0 us)
Async XLA Ops:
  5.9 29.3 %collective-permute-start = (bf16[2,64,64,128]{3,2,1,0:T(8,128)(2,1)}, bf16[2,64,64,128]{3,2,1,0:T(8,128)(2,1)S(1)}, u32[]{:S(2)}, u32[]{:S(2)}) collective-permute-start(bf16[2,64,64,128]{3,2,1,0:T(8,128)(2,1)} %get-tuple-element.79), channel_id=1, source_target_pairs={{0,120},{8,0},{16,8},{24,16},{32,24},{40,32},{48,40},{56,48},{64,5... | collective-permute-start | bytes 6291464 | tf_op jit(solution)/shard_map/ppermute | solution.py:21
  11.2 32.5 %collective-permute-start.1 = (bf16[2,64,64,128]{3,2,1,0:T(8,128)(2,1)}, bf16[2,64,64,128]{3,2,1,0:T(8,128)(2,1)S(1)}, u32[]{:S(2)}, u32[]{:S(2)}) collective-permute-start(bf16[2,64,64,128]{3,2,1,0:T(8,128)(2,1)} %get-tuple-element.83), channel_id=1, source_target_pairs={{0,8},{8,16},{16,24},{24,32},{32,40},{40,48},{48,56},{56,64},{64,7... | collective-permute-start | bytes 6291464 | tf_op jit(solution)/shard_map/ppermute | solution.py:21
  20.6 37.0 %collective-permute-start.2 = (bf16[2,64,64,128]{3,2,1,0:T(8,128)(2,1)}, bf16[2,64,64,128]{3,2,1,0:T(8,128)(2,1)S(1)}, u32[]{:S(2)}, u32[]{:S(2)}) collective-permute-start(bf16[2,64,64,128]{3,2,1,0:T(8,128)(2,1)} %get-tuple-element.87), channel_id=1, source_target_pairs={{0,120},{8,0},{16,8},{24,16},{32,24},{40,32},{48,40},{56,48},{64,5... | collective-permute-start | bytes 6291464 | tf_op jit(solution)/shard_map/ppermute | solution.py:21
  25.2 40.9 %collective-permute-start.5 = (bf16[2,64,64,128]{3,2,1,0:T(8,128)(2,1)}, bf16[2,64,64,128]{3,2,1,0:T(8,128)(2,1)}, u32[]{:S(2)}, u32[]{:S(2)}) collective-permute-start(bf16[2,64,64,128]{3,2,1,0:T(8,128)(2,1)} %get-tuple-element.94), channel_id=1, source_target_pairs={{0,8},{8,16},{16,24},{24,32},{32,40},{40,48},{48,56},{56,64},{64,7... | collective-permute-start | bytes 6291464 | tf_op jit(solution)/shard_map/ppermute | solution.py:21
  35.2 8.5 %copy-start.2 = (bf16[2,64,64,128]{3,2,1,0:T(8,128)(2,1)}, bf16[2,64,64,128]{3,2,1,0:T(8,128)(2,1)S(1)}, u32[]{:S(2)}) copy-start(bf16[2,64,64,128]{3,2,1,0:T(8,128)(2,1)S(1)} %collective-permute-done.refs_4_) | copy-start | bytes 6291460
  43.6 8.4 %copy-start.3 = (bf16[2,64,64,128]{3,2,1,0:T(8,128)(2,1)}, bf16[2,64,64,128]{3,2,1,0:T(8,128)(2,1)S(1)}, u32[]{:S(2)}) copy-start(bf16[2,64,64,128]{3,2,1,0:T(8,128)(2,1)S(1)} %collective-permute-done.1.refs_6_) | copy-start | bytes 6291460
  52.1 54.5 %collective-permute-start.6 = (bf16[2,64,128,128]{3,2,1,0:T(8,128)(2,1)}, bf16[2,64,128,128]{3,2,1,0:T(8,128)(2,1)}, u32[]{:S(2)}, u32[]{:S(2)}) collective-permute-start(bf16[2,64,128,128]{3,2,1,0:T(8,128)(2,1)} %get-tuple-element.97), channel_id=1, source_target_pairs={{0,8},{8,16},{16,24},{24,32},{32,40},{40,48},{48,56},{56,64},{64,7... | collective-permute-start | bytes 12582920 | tf_op jit(solution)/shard_map/ppermute | solution.py:21
  53.6 53.0 %collective-permute-start.3 = (bf16[2,64,128,128]{3,2,1,0:T(8,128)(2,1)}, bf16[2,64,128,128]{3,2,1,0:T(8,128)(2,1)}, u32[]{:S(2)}, u32[]{:S(2)}) collective-permute-start(bf16[2,64,128,128]{3,2,1,0:T(8,128)(2,1)} %get-tuple-element.90), channel_id=1, source_target_pairs={{0,120},{8,0},{16,8},{24,16},{32,24},{40,32},{48,40},{56,48},{64,5... | collective-permute-start | bytes 12582920 | tf_op jit(solution)/shard_map/ppermute | solution.py:21
  57.6 8.5 %copy-start.4 = (bf16[2,64,64,128]{3,2,1,0:T(8,128)(2,1)}, bf16[2,64,64,128]{3,2,1,0:T(8,128)(2,1)S(1)}, u32[]{:S(2)}) copy-start(bf16[2,64,64,128]{3,2,1,0:T(8,128)(2,1)S(1)} %collective-permute-done.2.refs_5_) | copy-start | bytes 6291460
  94.2 32.0 %all-to-all-start = ((f32[4,2,2,2,48,128]{5,4,3,2,1,0:T(8,128)}), f32[4,2,2,2,48,128]{5,4,3,2,1,0:T(8,128)S(1)}, u32[]{:S(2)}, u32[]{:S(2)}) async-start(f32[4,2,2,2,48,128]{5,4,3,2,1,0:T(8,128)} %bitcast.38), calls=%async_computation | async-start | bytes 1572864 | tf_op jit(solution)/shard_map/all_to_all | solution.py:184
  99.2 52.6 %collective-permute-start.13 = (bf16[2,48,128,128]{3,2,1,0:T(8,128)(2,1)}, bf16[2,48,128,128]{3,2,1,0:T(8,128)(2,1)}, u32[]{:S(2)}, u32[]{:S(2)}) collective-permute-start(bf16[2,48,128,128]{3,2,1,0:T(8,128)(2,1)} %get-tuple-element.131), channel_id=1, source_target_pairs={{0,8},{8,16},{16,24},{24,32},{32,40},{40,48},{48,56},{56,64},{64,7... | collective-permute-start | bytes 9437192 | tf_op jit(solution)/shard_map/ppermute | solution.py:21
  101.1 50.8 %collective-permute-start.12 = (bf16[2,48,128,128]{3,2,1,0:T(8,128)(2,1)}, bf16[2,48,128,128]{3,2,1,0:T(8,128)(2,1)}, u32[]{:S(2)}, u32[]{:S(2)}) collective-permute-start(bf16[2,48,128,128]{3,2,1,0:T(8,128)(2,1)} %get-tuple-element.130), channel_id=1, source_target_pairs={{0,120},{8,0},{16,8},{24,16},{32,24},{40,32},{48,40},{56,48},{64,5... | collective-permute-start | bytes 9437192 | tf_op jit(solution)/shard_map/ppermute | solution.py:21
  126.2 25.5 %copy-start.5 = (bf16[2,16,128,128]{3,2,1,0:T(8,128)(2,1)S(1)}, bf16[2,16,128,128]{3,2,1,0:T(8,128)(2,1)}, u32[]{:S(2)}) copy-start(bf16[2,16,128,128]{3,2,1,0:T(8,128)(2,1)} %get-tuple-element.91) | copy-start | bytes 3145732
  126.2 18.9 %all-to-all-start.1 = ((f32[4,2,2,2,48,128]{5,4,3,2,1,0:T(8,128)}), f32[4,2,2,2,48,128]{5,4,3,2,1,0:T(8,128)S(1)}, u32[]{:S(2)}, u32[]{:S(2)}) async-start(f32[4,2,2,2,48,128]{5,4,3,2,1,0:T(8,128)} %bitcast.37), calls=%async_computation.1 | async-start | bytes 1572864 | tf_op jit(solution)/shard_map/all_to_all | solution.py:184
  131.5 13.6 %collective-permute-start.8 = (f32[2,2,48,128]{3,2,1,0:T(8,128)S(1)}, f32[2,2,48,128]{3,2,1,0:T(8,128)S(1)}, u32[]{:S(2)}, u32[]{:S(2)}) collective-permute-start(f32[2,2,48,128]{3,2,1,0:T(8,128)S(1)} %dynamic-slice_bitcast_fusion.1), channel_id=1, source_target_pairs={{0,1},{1,0},{2,3},{3,2},{4,5},{5,4},{6,7},{7,6},{8,9},{9,8},{10,11... | collective-permute-start | bytes 294920 | tf_op jit(solution)/shard_map/ppermute | solution.py:188
  145.2 6.6 %collective-permute-start.9 = (f32[2,2,48,128]{3,2,1,0:T(8,128)S(1)}, f32[2,2,48,128]{3,2,1,0:T(8,128)S(1)}, u32[]{:S(2)}, u32[]{:S(2)}) collective-permute-start(f32[2,2,48,128]{3,2,1,0:T(8,128)S(1)} %dynamic-slice_bitcast_fusion), channel_id=1, source_target_pairs={{0,1},{1,0},{2,3},{3,2},{4,5},{5,4},{6,7},{7,6},{8,9},{9,8},{10,11... | collective-permute-start | bytes 294920 | tf_op jit(solution)/shard_map/ppermute | solution.py:188
  146.3 21.6 %collective-permute-start.10 = (f32[2,48,128]{2,1,0:T(8,128)S(1)}, f32[2,48,128]{2,1,0:T(8,128)S(1)}, u32[]{:S(2)}, u32[]{:S(2)}) collective-permute-start(f32[2,48,128]{2,1,0:T(8,128)S(1)} %get-tuple-element.141), channel_id=1, source_target_pairs={{0,120},{8,0},{16,8},{24,16},{32,24},{40,32},{48,40},{56,48},{64,5... | collective-permute-start | bytes 147464 | tf_op jit(solution)/shard_map/ppermute | solution.py:21
  147.1 23.1 %collective-permute-start.7 = (bf16[2,16,128,128]{3,2,1,0:T(8,128)(2,1)}, bf16[2,16,128,128]{3,2,1,0:T(8,128)(2,1)S(1)}, u32[]{:S(2)}, u32[]{:S(2)}) collective-permute-start(bf16[2,16,128,128]{3,2,1,0:T(8,128)(2,1)} %get-tuple-element.98), channel_id=1, source_target_pairs={{0,8},{8,16},{16,24},{24,32},{32,40},{40,48},{48,56},{56,64},{64,7... | collective-permute-start | bytes 3145736 | tf_op jit(solution)/shard_map/ppermute | solution.py:21
  151.8 18.4 %collective-permute-start.4 = (bf16[2,16,128,128]{3,2,1,0:T(8,128)(2,1)S(1)}, bf16[2,16,128,128]{3,2,1,0:T(8,128)(2,1)S(1)}, u32[]{:S(2)}, u32[]{:S(2)}) collective-permute-start(bf16[2,16,128,128]{3,2,1,0:T(8,128)(2,1)S(1)} %copy-done.5), channel_id=1, source_target_pairs={{0,120},{8,0},{16,8},{24,16},{32,24},{40,32},{48,40},{56,48},{64,5... | collective-permute-start | bytes 3145736 | tf_op jit(solution)/shard_map/ppermute | solution.py:21
  151.8 18.3 %collective-permute-start.11 = (f32[2,48,128]{2,1,0:T(8,128)S(1)}, f32[2,48,128]{2,1,0:T(8,128)S(1)}, u32[]{:S(2)}, u32[]{:S(2)}) collective-permute-start(f32[2,48,128]{2,1,0:T(8,128)S(1)} %get-tuple-element.139), channel_id=1, source_target_pairs={{0,120},{8,0},{16,8},{24,16},{32,24},{40,32},{48,40},{56,48},{64,5... | collective-permute-start | bytes 147464 | tf_op jit(solution)/shard_map/ppermute | solution.py:21
  170.1 1.0 copy-start
  170.1 1.3 copy-start.1
  193.8 8.3 %collective-permute-start.14 = (f32[2,48,128]{2,1,0:T(8,128)S(1)}, f32[2,48,128]{2,1,0:T(8,128)S(1)}, u32[]{:S(2)}, u32[]{:S(2)}) collective-permute-start(f32[2,48,128]{2,1,0:T(8,128)S(1)} %get-tuple-element.137), channel_id=1, source_target_pairs={{0,120},{8,0},{16,8},{24,16},{32,24},{40,32},{48,40},{56,48},{64,5... | collective-permute-start | bytes 147464 | tf_op jit(solution)/shard_map/ppermute | solution.py:21

commit v3 on v2

v3 whole, which is shorter than its diff:
```python
import jax
import jax.numpy as jnp
from jax import lax
from jax.experimental import pallas as pl
from jax.experimental.pallas import tpu as pltpu
from jax.sharding import PartitionSpec as P

LANES = 128
CHUNKS = ((0, 64, 1, (64,)), (64, 64, 1, (64,)), (128, 64, 2, (64,)), (256, 64, 2, (48, 16)))
GROUPS = ((0, 1), (2,), (3,))
STEP = 16
RELAYOUT_COST = 5_000_000_000
PRODUCT_COST = 3
TAIL = 16
PARAMS = pltpu.CompilerParams(vmem_limit_bytes=56 << 20)


def shifted(value, axis, steps):
    count = lax.axis_size(axis)
    return lax.ppermute(value, axis, [(s, (s + steps) % count) for s in range(count)])


def relayout(states, perm, wraps, chunk, left):
    first, sub, units, pieces = chunk
    pitch = sub + 1
    each = sub // 8
    sticks = states.shape[2]
    half = sticks // 2
    bands = units * sub

    def body(perm_ref, wraps_ref, x_ref, *refs):
        outs, scratch = refs[:-1], refs[-1]
        x = x_ref.at[0]
        for m in range(sub):
            row = x[m] if left else x[m // each, m % each]
            scratch[pl.ds(m, sticks, stride=pitch), :] = row.astype(jnp.float32)

        def put(s, value):
            value = value.astype(jnp.bfloat16)
            sent = s < half if left else s >= half
            if not sent:
                outs[-2][0, s % half] = value
                if s % half >= half - TAIL:
                    outs[-1][0, s % half - (half - TAIL)] = value
                return
            at = s % half
            for piece, size in enumerate(pieces):
                if at < size:
                    outs[piece][0, at] = value
                    return
                at -= size

        def plain():
            for s in range(sticks):
                put(s, scratch[pl.ds(s * pitch, sub), :])

        def wrapped():
            keep = lax.broadcasted_iota(jnp.int32, (sub, LANES), 1) < LANES - 1
            for s in range(sticks):
                value = scratch[pl.ds(perm_ref[s] * pitch, sub), :]
                put(s, jnp.where(keep, pltpu.roll(value, LANES - 1, 1), 0.0))

        if left:
            pl.when(wraps_ref[0] == 0)(plain)
            pl.when(wraps_ref[0] != 0)(wrapped)
        else:
            plain()

    if left:
        view = states
        in_spec = pl.BlockSpec((1, sub, sticks, LANES), lambda c, g, *_: (c, first // sub + g, 0, 0))
    else:
        view = states.reshape(2, 8, states.shape[1] // 8, sticks, LANES)
        in_spec = pl.BlockSpec((1, 8, each, sticks, LANES), lambda c, g, *_: (c, 0, first // sub + g, 0, 0))
    sizes = (*pieces, half, TAIL)
    return pl.pallas_call(
        body,
        grid_spec=pltpu.PrefetchScalarGridSpec(
            num_scalar_prefetch=2,
            grid=(2, units),
            in_specs=[in_spec],
            out_specs=[pl.BlockSpec((1, n, sub, LANES), lambda c, g, *_: (c, 0, g, 0)) for n in sizes],
            scratch_shapes=[pltpu.VMEM((sticks * pitch, LANES), jnp.float32)],
        ),
        out_shape=[jax.ShapeDtypeStruct((2, n, bands, LANES), jnp.bfloat16) for n in sizes],
        compiler_params=PARAMS,
        cost_estimate=pl.CostEstimate(flops=RELAYOUT_COST * bands // 64, transcendentals=0, bytes_accessed=8 * bands * sticks * LANES),
        name="relayout_left" if left else "relayout_right",
    )(perm, wraps, view)


def products(left, right, units, size, start, finish, resident, cost):
    sides = (left, right)
    steps = 1 if resident else size // STEP
    heights = [sum(r.shape[2] for r in rows) for rows, _ in sides]
    widths = [sum(c.shape[2] for c in columns) for _, columns in sides]
    shapes = [(2 * h, 2 * w) for h, w in zip(heights, widths)]

    def stack(refs):
        return jnp.concatenate(
            [jnp.concatenate([r[c, j] for j in range(STEP)], -1) for c in range(2) for r in refs], 0
        )

    def body(*refs):
        refs = list(refs)
        take = lambda n: [refs.pop(0) for _ in range(n)]
        operands = [(take(len(rows)), take(len(columns))) for rows, columns in sides]
        starts = take(2) if start else None
        outs = take(1) if finish else take(2)
        totals = take(2)
        step = pl.program_id(0)

        @pl.when(step == 0)
        def _():
            for side in range(2):
                totals[side][...] = starts[side][...] if start else jnp.zeros(shapes[side], jnp.float32)

        for side, (rows, columns) in enumerate(operands):
            totals[side][...] += lax.dot_general(
                stack(rows), stack(columns), (((1,), (1,)), ((), ())), preferred_element_type=jnp.float32
            )

        @pl.when(step == steps - 1)
        def _():
            for side in range(2):
                total, h, w = totals[side], heights[side], widths[side]
                if not finish:
                    outs[side][...] = total[...]
                    continue
                real = total[:h, :w] + total[h:, w:]
                imag = total[:h, w:] - total[h:, :w]
                for part, value in enumerate((real, imag)):
                    at, to = 0, 0
                    for unit in units[side]:
                        each = unit // 8
                        for q in range(8):
                            block = value[at : at + each]
                            at += each
                            for n in range(w // LANES):
                                into = n * (h // 8) + to
                                outs[0][q, side, part, into : into + each] = block[:, n * LANES : (n + 1) * LANES]
                        to += each

    def spec(array):
        if resident:
            return pl.BlockSpec(memory_space=pltpu.VMEM)
        return pl.BlockSpec((2, STEP, array.shape[2], LANES), lambda s: (0, s, 0, 0))

    in_specs, operands = [], []
    for rows, columns in sides:
        in_specs += [spec(r) for r in (*rows, *columns)]
        operands += [*rows, *columns]
    whole = [pl.BlockSpec(shape, lambda s: (0, 0)) for shape in shapes]
    if start:
        in_specs += [pl.BlockSpec(memory_space=pltpu.VMEM)] * 2
        operands += start
    if finish:
        out_shape = [(8, 2, 2, 48, LANES)]
        out_specs = [pl.BlockSpec(out_shape[0], lambda s: (0, 0, 0, 0, 0))]
    else:
        out_shape, out_specs = shapes, whole
    return pl.pallas_call(
        body,
        grid=(steps,),
        in_specs=in_specs,
        out_specs=out_specs,
        out_shape=[jax.ShapeDtypeStruct(shape, jnp.float32) for shape in out_shape],
        scratch_shapes=[pltpu.VMEM(shape, jnp.float32) for shape in shapes],
        compiler_params=pltpu.CompilerParams(vmem_limit_bytes=(20 if resident else 56) << 20),
        cost_estimate=pl.CostEstimate(
            flops=cost * 2 * steps * STEP * LANES * sum(h * w for h, w in shapes),
            transcendentals=0,
            bytes_accessed=4 * steps * STEP * LANES * sum(h + w for h, w in shapes),
        ),
        name="products",
    )(*operands)


def after(value, *others):
    return lax.optimization_barrier((value, others))[0]


def summed(total):
    return lax.all_to_all(total, "pw", 0, 0, tiled=True).sum(0)


def summed_apart(total):
    count = lax.axis_size("pw")
    groups = [list(range(p, count, 2)) for p in range(2)]
    pairs = total.reshape(count // 2, 2, *total.shape[1:])
    return lax.all_to_all(pairs, "pw", 0, 0, axis_index_groups=groups, tiled=True).sum(0)


def summed_near(pairs):
    side = lax.axis_index("pw") % 2
    kept = lax.dynamic_index_in_dim(pairs, side, 1, keepdims=False)
    sent = lax.dynamic_index_in_dim(pairs, 1 - side, 1, keepdims=False)
    return kept + lax.ppermute(sent, "pw", [(p, p ^ 1) for p in range(lax.axis_size("pw"))])


def shards(states, stick_perm):
    states = states[0]
    sticks = states.shape[2]
    perm = stick_perm - lax.axis_index("pw") * sticks
    token = (lax.axis_index("kz") == 0).astype(jnp.int32).reshape(1)
    columns, rows, from_right, from_left = [], [], [], []
    tail_columns, tail_rows = [], []
    for index, chunk in enumerate(CHUNKS):
        for left in (True, False):
            if index > 1:
                token = after(token, (from_right if left else from_left)[index - 2][0])
            *sent, kept, tail = relayout(states, perm, token, chunk, left)
            token, kept = lax.optimization_barrier((token, kept))
            (columns if left else rows).append(kept)
            (tail_columns if left else tail_rows).append(tail)
            for piece in range(1, len(sent)):
                if not left:
                    sent[piece] = after(sent[piece], from_right[index - 1][0])
            (from_right if left else from_left).append([shifted(p, "kz", -1 if left else 1) for p in sent])

    runs = [[chunk[1]] * chunk[2] for chunk in CHUNKS]
    early = []
    for group in GROUPS:
        totals = None
        pieces = CHUNKS[group[0]][3]
        units = (sum(runs, []), sum((runs[c] for c in group), []))
        for index, size in enumerate(pieces):
            last = index == len(pieces) - 1
            arrived = [[side[c][index] for c in group] for side in (from_right, from_left)]
            own = (tail_rows, tail_columns) if index else (rows, columns)
            if index:
                arrived, totals = lax.optimization_barrier((arrived, totals))
            totals = products(
                (own[0], arrived[0]), (arrived[1], own[1]), units, size, totals, last, index > 0, PRODUCT_COST
            )
        rows, columns, totals = lax.optimization_barrier((rows, columns, totals))
        if group != GROUPS[-1]:
            early.append(summed_apart(totals[0]))
    parts = jnp.concatenate([summed_near(jnp.stack(early)), summed(totals[0])[None]])
    groups, _, _, height, _ = parts.shape
    from_left_part = shifted(parts[:, 1], "kz", -1).reshape(groups, 2, groups, height // groups, LANES)
    left = jnp.transpose(parts[:, 0], (2, 1, 0, 3)).reshape(height, 2, groups * LANES)
    right = jnp.transpose(from_left_part, (0, 3, 1, 2, 4)).reshape(height, 2, groups * LANES)
    return (left + right)[:, None]


def solution(mesh):
    in_specs = (P("kz", None, None, "pw", None), P("pw"))
    out_specs = P("pw", "kz", None, None)
    return jax.shard_map(shards, mesh=mesh, in_specs=in_specs, out_specs=out_specs, check_vma=False)
```

time: 203 us -> 189 us (0.931)
  Pallas kernels: 114 us -> 97.2 us
  blocking collectives: 15.7 us -> 0 us
  waiting for transfers between devices: 36.8 us -> 45.9 us
  starting transfers between devices: 32.4 us -> 37.8 us
  local copies, waits for them, and re-layouts: 2.14 us -> 4.6 us
    pallas_call x4, Pallas kernels: 61.8 us -> 43.1 us  [products(): pl.pallas_call(body, grid=(steps,), in_specs=in_specs, out_specs=out_spec...]
    all_to_all x1 -> x0, blocking collectives: 15.7 us -> none  [reduced(): return lax.all_to_all(total, 'pw', 0, 0, tiled=True).sum(0)]
    ppermute x13 -> x11, waiting for transfers between devices: 24.6 us -> 34.7 us  [shifted(): lax.ppermute(value, axis, [(s, (s + steps) % count) for s in range(count)])]
    all_to_all x2 -> x3, starting transfers between devices: 10.2 us -> 16.1 us  [the longest x2 10.1 us: summed_apart(): lax.all_to_all(pairs, 'pw', 0, 0, axis_index_groups=groups, tiled=True)]
    unnamed x12 -> x26, local copies, waits for them, and re-layouts: 1.33 us -> 3.52 us
    ppermute x2 -> x1, waiting for transfers between devices: 12.2 us -> 11.2 us  [summed_near(): lax.ppermute(sent, 'pw', [(p, p ^ 1) for p in range(lax.axis_size('pw'))])]
    ppermute x13 -> x11, starting transfers between devices: 19.7 us -> 20.1 us  [shifted(): lax.ppermute(value, axis, [(s, (s + steps) % count) for s in range(count)])]
  transfers between devices with their start and end apart: 17 -> 15, of which waited for: 6 -> 6; matrix products, arithmetic and copies ran while one was open for 0% -> 1% of each run, Pallas kernels for 51% -> 49%
where the time goes in v3:
time: 189 us; the launch traced here: 188 us
  Pallas kernels  97.2 us (51%)
  waiting for transfers between devices  45.9 us (24%)
  starting transfers between devices  37.8 us (20%)
  local copies, waits for them, and re-layouts  4.6 us (2%)
  other arithmetic  2.53 us (1%)
    pallas_call x8, Pallas kernels, relayout(): pl.pallas_call(body, grid_spec=pltpu.PrefetchScalarGridSpec(num_scalar_pr...  54.1 us
    pallas_call x4, Pallas kernels, products(): pl.pallas_call(body, grid=(steps,), in_specs=in_specs, out_specs=out_spec...  43.1 us
    ppermute x11, waiting for transfers between devices, shifted(): lax.ppermute(value, axis, [(s, (s + steps) % count) for s in range(count)])  34.7 us
    ppermute x11, starting transfers between devices, shifted(): lax.ppermute(value, axis, [(s, (s + steps) % count) for s in range(count)])  20.1 us
    ppermute x1, waiting for transfers between devices, summed_near(): lax.ppermute(sent, 'pw', [(p, p ^ 1) for p in range(lax.axis_size('pw'))])  11.2 us
    all_to_all x2, starting transfers between devices, summed_apart(): lax.all_to_all(pairs, 'pw', 0, 0, axis_index_groups=groups, tiled=True)  10.1 us
    all_to_all x1, starting transfers between devices, summed(): return lax.all_to_all(total, 'pw', 0, 0, tiled=True).sum(0)  6.05 us
  transfers between devices with their start and end apart: 15, of which 6 were waited for; matrix products, arithmetic and copies ran while one was open for 1% of the time, Pallas kernels for 49%

profile of v3, /device:TPU:7, one launch (start us, length us, event | category | flops | bytes accessed | tf_op | source)
XLA Modules:
  0.0 188.3 jit_solution(16876123230652169367)
XLA Ops:
  1.2 4.9 %relayout_left.4 = (bf16[2,64,64,128]{3,2,1,0:T(8,128)(2,1)}, bf16[2,64,64,128]{3,2,1,0:T(8,128)(2,1)}, bf16[2,16,64,128]{3,2,1,0:T(8,128)(2,1)}) custom-call(s32[128]{0:T(128)} %broadcast_subtract_fusion.perm_ref, s32[1]{0:T(128)} %bitcast.wraps_ref, bf16[2,384,128,128]{3,2,1,0:T(8,128)(2,1)} %bitcast.27), custom_call_target="tpu_custom_call" | custom-call | flops 5000000000 | bytes 8388608 | tf_op jit(solution)/shard_map/relayout_left/pallas_call | solution.py:76
  6.8 4.7 %relayout_right.4 = (bf16[2,64,64,128]{3,2,1,0:T(8,128)(2,1)}, bf16[2,64,64,128]{3,2,1,0:T(8,128)(2,1)}, bf16[2,16,64,128]{3,2,1,0:T(8,128)(2,1)}) custom-call(s32[128]{0:T(128)} %broadcast_subtract_fusion.perm_ref, s32[1]{0:T(128)} %bitcast.wraps_ref, bf16[2,8,48,128,128]{4,3,2,1,0:T(8,128)(2,1)} %bitcast.28), custom_call_target="tpu_custom_call" | custom-call | flops 5000000000 | bytes 8388608 | tf_op jit(solution)/shard_map/relayout_right/pallas_call | solution.py:76
  11.5 4.7 %collective-permute-start.1 = (bf16[2,64,64,128]{3,2,1,0:T(8,128)(2,1)}, bf16[2,64,64,128]{3,2,1,0:T(8,128)(2,1)S(1)}, u32[]{:S(2)}, u32[]{:S(2)}) collective-permute-start(bf16[2,64,64,128]{3,2,1,0:T(8,128)(2,1)} %get-tuple-element.90), channel_id=1, source_target_pairs={{0,8},{8,16},{16,24},{24,32},{32,40},{40,48},{48,56},{56,64},{64,7... | collective-permute-start | bytes 6291464 | tf_op jit(solution)/shard_map/ppermute | solution.py:20
  16.2 4.9 %relayout_left.5 = (bf16[2,64,64,128]{3,2,1,0:T(8,128)(2,1)}, bf16[2,64,64,128]{3,2,1,0:T(8,128)(2,1)}, bf16[2,16,64,128]{3,2,1,0:T(8,128)(2,1)}) custom-call(s32[128]{0:T(128)} %broadcast_subtract_fusion.perm_ref, s32[1]{0:T(128)} %bitcast.wraps_ref, bf16[2,384,128,128]{3,2,1,0:T(8,128)(2,1)} %bitcast.29), custom_call_target="tpu_custom_call" | custom-call | flops 5000000000 | bytes 8388608 | tf_op jit(solution)/shard_map/relayout_left/pallas_call | solution.py:76
  21.1 4.7 %relayout_right.5 = (bf16[2,64,64,128]{3,2,1,0:T(8,128)(2,1)}, bf16[2,64,64,128]{3,2,1,0:T(8,128)(2,1)}, bf16[2,16,64,128]{3,2,1,0:T(8,128)(2,1)}) custom-call(s32[128]{0:T(128)} %broadcast_subtract_fusion.perm_ref, s32[1]{0:T(128)} %bitcast.wraps_ref, bf16[2,8,48,128,128]{4,3,2,1,0:T(8,128)(2,1)} %bitcast.30), custom_call_target="tpu_custom_call" | custom-call | flops 5000000000 | bytes 8388608 | tf_op jit(solution)/shard_map/relayout_right/pallas_call | solution.py:76
  25.8 5.4 %collective-permute-start.3 = (bf16[2,64,64,128]{3,2,1,0:T(8,128)(2,1)}, bf16[2,64,64,128]{3,2,1,0:T(8,128)(2,1)}, u32[]{:S(2)}, u32[]{:S(2)}) collective-permute-start(bf16[2,64,64,128]{3,2,1,0:T(8,128)(2,1)} %get-tuple-element.99), channel_id=1, source_target_pairs={{0,8},{8,16},{16,24},{24,32},{32,40},{40,48},{48,56},{56,64},{64,7... | collective-permute-start | bytes 6291464 | tf_op jit(solution)/shard_map/ppermute | solution.py:20
  31.1 4.2 %collective-permute-done.refs_4_ = bf16[2,64,64,128]{3,2,1,0:T(8,128)(2,1)S(1)} collective-permute-done((bf16[2,64,64,128]{3,2,1,0:T(8,128)(2,1)}, bf16[2,64,64,128]{3,2,1,0:T(8,128)(2,1)S(1)}, u32[]{:S(2)}, u32[]{:S(2)}) %collective-permute-start) | collective-permute-done | bytes 2097184 | tf_op jit(solution)/shard_map/ppermute | solution.py:20
  35.4 8.7 %relayout_left.6 = (bf16[2,64,128,128]{3,2,1,0:T(8,128)(2,1)}, bf16[2,64,128,128]{3,2,1,0:T(8,128)(2,1)}, bf16[2,16,128,128]{3,2,1,0:T(8,128)(2,1)}) custom-call(s32[128]{0:T(128)} %broadcast_subtract_fusion.perm_ref, s32[1]{0:T(128)} %bitcast.wraps_ref, bf16[2,384,128,128]{3,2,1,0:T(8,128)(2,1)} %bitcast.31), custom_call_target="tpu_custom_call" | custom-call | flops 10000000000 | bytes 16777216 | tf_op jit(solution)/shard_map/relayout_left/pallas_call | solution.py:76
  44.1 8.8 %relayout_right.6 = (bf16[2,64,128,128]{3,2,1,0:T(8,128)(2,1)}, bf16[2,64,128,128]{3,2,1,0:T(8,128)(2,1)}, bf16[2,16,128,128]{3,2,1,0:T(8,128)(2,1)}) custom-call(s32[128]{0:T(128)} %broadcast_subtract_fusion.perm_ref, s32[1]{0:T(128)} %bitcast.wraps_ref, bf16[2,8,48,128,128]{4,3,2,1,0:T(8,128)(2,1)} %bitcast.32), custom_call_target="tpu_custom_call" | custom-call | flops 10000000000 | bytes 16777216 | tf_op jit(solution)/shard_map/relayout_right/pallas_call | solution.py:76
  54.3 3.6 %collective-permute-done.2.refs_5_ = bf16[2,64,64,128]{3,2,1,0:T(8,128)(2,1)S(1)} collective-permute-done((bf16[2,64,64,128]{3,2,1,0:T(8,128)(2,1)}, bf16[2,64,64,128]{3,2,1,0:T(8,128)(2,1)S(1)}, u32[]{:S(2)}, u32[]{:S(2)}) %collective-permute-start.2) | collective-permute-done | bytes 2097184 | tf_op jit(solution)/shard_map/ppermute | solution.py:20
  57.9 8.7 %relayout_left.7 = (bf16[2,48,128,128]{3,2,1,0:T(8,128)(2,1)}, bf16[2,16,128,128]{3,2,1,0:T(8,128)(2,1)}, bf16[2,64,128,128]{3,2,1,0:T(8,128)(2,1)}, bf16[2,16,128,128]{3,2,1,0:T(8,128)(2,1)}) custom-call(s32[128]{0:T(128)} %broadcast_subtract_fusion.perm_ref, s32[1]{0:T(128)} %bitcast.wraps_ref, bf16[2,384,128,128]{3,2,1,0:T(8,128)(2,1)} %bitcast.33), custom_call_target="tpu_custom_call" | custom-call | flops 10000000000 | bytes 16777216 | tf_op jit(solution)/shard_map/relayout_left/pallas_call | solution.py:76
  66.6 8.7 %relayout_right.7 = (bf16[2,48,128,128]{3,2,1,0:T(8,128)(2,1)}, bf16[2,16,128,128]{3,2,1,0:T(8,128)(2,1)}, bf16[2,64,128,128]{3,2,1,0:T(8,128)(2,1)}, bf16[2,16,128,128]{3,2,1,0:T(8,128)(2,1)}) custom-call(s32[128]{0:T(128)} %broadcast_subtract_fusion.perm_ref, s32[1]{0:T(128)} %bitcast.wraps_ref, bf16[2,8,48,128,128]{4,3,2,1,0:T(8,128)(2,1)} %bitcast.34), custom_call_target="tpu_custom_call" | custom-call | flops 10000000000 | bytes 16777216 | tf_op jit(solution)/shard_map/relayout_right/pallas_call | solution.py:76
  77.1 14.2 %products.4 = f32[8,2,2,48,128]{4,3,2,1,0:T(8,128)} custom-call(bf16[2,64,64,128]{3,2,1,0:T(8,128)(2,1)} %get-tuple-element.119.refs_0_, bf16[2,64,64,128]{3,2,1,0:T(8,128)(2,1)} %get-tuple-element.120.refs_1_, bf16[2,64,128,128]{3,2,1,0:T(8,128)(2,1)} %get-tuple-element.121.refs_2_, bf16[2,64,128,128]{3,2,1,0:T(8,128)(2,1)} %get-tuple-element.122.refs_3_, ...), custom_call_target="tpu_custom_call" | custom-call | flops 19327352832 | bytes 67108864 | tf_op jit(solution)/shard_map/products/pallas_call | solution.py:162
  91.3 5.0 %all-to-all-start = ((f32[4,2,2,2,48,128]{5,4,3,2,1,0:T(8,128)}), f32[4,2,2,2,48,128]{5,4,3,2,1,0:T(8,128)S(1)}, u32[]{:S(2)}, u32[]{:S(2)}) async-start(f32[4,2,2,2,48,128]{5,4,3,2,1,0:T(8,128)} %bitcast.40), calls=%async_computation | async-start | bytes 1572864 | tf_op jit(solution)/shard_map/all_to_all | solution.py:191
  96.3 10.6 %collective-permute-done.5.refs_5_ = bf16[2,64,128,128]{3,2,1,0:T(8,128)(2,1)} collective-permute-done((bf16[2,64,128,128]{3,2,1,0:T(8,128)(2,1)}, bf16[2,64,128,128]{3,2,1,0:T(8,128)(2,1)}, u32[]{:S(2)}, u32[]{:S(2)}) %collective-permute-start.5) | collective-permute-done | bytes 4194336 | tf_op jit(solution)/shard_map/ppermute | solution.py:20
  106.9 14.2 %products.5 = f32[8,2,2,48,128]{4,3,2,1,0:T(8,128)} custom-call(bf16[2,64,64,128]{3,2,1,0:T(8,128)(2,1)} %get-tuple-element.119.refs_0_, bf16[2,64,64,128]{3,2,1,0:T(8,128)(2,1)} %get-tuple-element.120.refs_1_, bf16[2,64,128,128]{3,2,1,0:T(8,128)(2,1)} %get-tuple-element.121.refs_2_, bf16[2,64,128,128]{3,2,1,0:T(8,128)(2,1)} %get-tuple-element.122.refs_3_, ...), custom_call_target="tpu_custom_call" | custom-call | flops 19327352832 | bytes 67108864 | tf_op jit(solution)/shard_map/products/pallas_call | solution.py:162
  121.1 6.1 %collective-permute-start.8 = (bf16[2,16,128,128]{3,2,1,0:T(8,128)(2,1)}, bf16[2,16,128,128]{3,2,1,0:T(8,128)(2,1)S(1)}, u32[]{:S(2)}, u32[]{:S(2)}) collective-permute-start(bf16[2,16,128,128]{3,2,1,0:T(8,128)(2,1)} %get-tuple-element.133), channel_id=1, source_target_pairs={{0,8},{8,16},{16,24},{24,32},{32,40},{40,48},{48,56},{56,64},{64,7... | collective-permute-start | bytes 3145736 | tf_op jit(solution)/shard_map/ppermute | solution.py:20
  127.2 5.0 %all-to-all-start.1 = ((f32[4,2,2,2,48,128]{5,4,3,2,1,0:T(8,128)}), f32[4,2,2,2,48,128]{5,4,3,2,1,0:T(8,128)}, u32[]{:S(2)}, u32[]{:S(2)}) async-start(f32[4,2,2,2,48,128]{5,4,3,2,1,0:T(8,128)} %bitcast.39), calls=%async_computation.1 | async-start | bytes 1572864 | tf_op jit(solution)/shard_map/all_to_all | solution.py:191
  132.3 8.3 %collective-permute-done.10.refs_5_ = bf16[2,48,128,128]{3,2,1,0:T(8,128)(2,1)} collective-permute-done((bf16[2,48,128,128]{3,2,1,0:T(8,128)(2,1)}, bf16[2,48,128,128]{3,2,1,0:T(8,128)(2,1)}, u32[]{:S(2)}, u32[]{:S(2)}) %collective-permute-start.10) | collective-permute-done | bytes 3145760 | tf_op jit(solution)/shard_map/ppermute | solution.py:20
  140.6 12.0 %products.6 = (f32[768,256]{1,0:T(8,128)}, f32[256,768]{1,0:T(8,128)}) custom-call(bf16[2,64,64,128]{3,2,1,0:T(8,128)(2,1)} %get-tuple-element.119.refs_0_, bf16[2,64,64,128]{3,2,1,0:T(8,128)(2,1)} %get-tuple-element.120.refs_1_, bf16[2,64,128,128]{3,2,1,0:T(8,128)(2,1)} %get-tuple-element.121.refs_2_, bf16[2,64,128,128]{3,2,1,0:T(8,128)(2,1)} %get-tuple-element.122.refs_3_, ...), custom_call_target="tpu_custom_call" | custom-call | flops 14495514624 | bytes 50331648 | tf_op jit(solution)/shard_map/products/pallas_call | solution.py:162
  156.2 2.7 %products.7 = f32[8,2,2,48,128]{4,3,2,1,0:T(8,128)} custom-call(bf16[2,16,64,128]{3,2,1,0:T(8,128)(2,1)S(1)} %copy-done.1, bf16[2,16,64,128]{3,2,1,0:T(8,128)(2,1)S(1)} %copy-done.3, bf16[2,16,128,128]{3,2,1,0:T(8,128)(2,1)S(1)} %copy-done.5, bf16[2,16,128,128]{3,2,1,0:T(8,128)(2,1)S(1)} %copy-done.7, ...), custom_call_target="tpu_custom_call" | custom-call | flops 4831838208 | bytes 16777216 | tf_op jit(solution)/shard_map/products/pallas_call | solution.py:162
  158.9 6.0 %all-to-all-start.2 = ((f32[8,2,2,48,128]{4,3,2,1,0:T(8,128)}), f32[8,2,2,48,128]{4,3,2,1,0:T(8,128)S(1)}, u32[]{:S(2)}, u32[]{:S(2)}) async-start(f32[8,2,2,48,128]{4,3,2,1,0:T(8,128)} %products.7), calls=%async_computation.2 | async-start | bytes 1572864 | tf_op jit(solution)/shard_map/all_to_all | solution.py:184
  167.7 11.2 %collective-permute-done.6 = f32[2,2,2,48,128]{4,3,2,0,1:T(8,128)S(1)} collective-permute-done((f32[2,2,2,48,128]{4,3,2,0,1:T(8,128)S(1)}, f32[2,2,2,48,128]{4,3,2,0,1:T(8,128)S(1)}, u32[]{:S(2)}, u32[]{:S(2)}) %collective-permute-start.6) | collective-permute-done | bytes 196640 | tf_op jit(solution)/shard_map/ppermute | solution.py:198
  179.4 8.0 %collective-permute-done.11 = f32[3,2,48,128]{3,2,1,0:T(8,128)S(1)} collective-permute-done((f32[3,2,48,128]{3,2,1,0:T(8,128)S(1)}, f32[3,2,48,128]{3,2,1,0:T(8,128)S(1)}, u32[]{:S(2)}, u32[]{:S(2)}) %collective-permute-start.11) | collective-permute-done | bytes 147488 | tf_op jit(solution)/shard_map/ppermute | solution.py:20
  (57 shorter events, 12.7 us)
Async XLA Ops:
  6.1 29.3 %collective-permute-start = (bf16[2,64,64,128]{3,2,1,0:T(8,128)(2,1)}, bf16[2,64,64,128]{3,2,1,0:T(8,128)(2,1)S(1)}, u32[]{:S(2)}, u32[]{:S(2)}) collective-permute-start(bf16[2,64,64,128]{3,2,1,0:T(8,128)(2,1)} %get-tuple-element.86), channel_id=1, source_target_pairs={{0,120},{8,0},{16,8},{24,16},{32,24},{40,32},{48,40},{56,48},{64,5... | collective-permute-start | bytes 6291464 | tf_op jit(solution)/shard_map/ppermute | solution.py:20
  11.5 32.5 %collective-permute-start.1 = (bf16[2,64,64,128]{3,2,1,0:T(8,128)(2,1)}, bf16[2,64,64,128]{3,2,1,0:T(8,128)(2,1)S(1)}, u32[]{:S(2)}, u32[]{:S(2)}) collective-permute-start(bf16[2,64,64,128]{3,2,1,0:T(8,128)(2,1)} %get-tuple-element.90), channel_id=1, source_target_pairs={{0,8},{8,16},{16,24},{24,32},{32,40},{40,48},{48,56},{56,64},{64,7... | collective-permute-start | bytes 6291464 | tf_op jit(solution)/shard_map/ppermute | solution.py:20
  21.1 36.7 %collective-permute-start.2 = (bf16[2,64,64,128]{3,2,1,0:T(8,128)(2,1)}, bf16[2,64,64,128]{3,2,1,0:T(8,128)(2,1)S(1)}, u32[]{:S(2)}, u32[]{:S(2)}) collective-permute-start(bf16[2,64,64,128]{3,2,1,0:T(8,128)(2,1)} %get-tuple-element.95), channel_id=1, source_target_pairs={{0,120},{8,0},{16,8},{24,16},{32,24},{40,32},{48,40},{56,48},{64,5... | collective-permute-start | bytes 6291464 | tf_op jit(solution)/shard_map/ppermute | solution.py:20
  25.8 40.8 %collective-permute-start.3 = (bf16[2,64,64,128]{3,2,1,0:T(8,128)(2,1)}, bf16[2,64,64,128]{3,2,1,0:T(8,128)(2,1)}, u32[]{:S(2)}, u32[]{:S(2)}) collective-permute-start(bf16[2,64,64,128]{3,2,1,0:T(8,128)(2,1)} %get-tuple-element.99), channel_id=1, source_target_pairs={{0,8},{8,16},{16,24},{24,32},{32,40},{40,48},{48,56},{56,64},{64,7... | collective-permute-start | bytes 6291464 | tf_op jit(solution)/shard_map/ppermute | solution.py:20
  44.1 8.8 %copy-start.11 = (bf16[2,64,64,128]{3,2,1,0:T(8,128)(2,1)}, bf16[2,64,64,128]{3,2,1,0:T(8,128)(2,1)S(1)}, u32[]{:S(2)}) copy-start(bf16[2,64,64,128]{3,2,1,0:T(8,128)(2,1)S(1)} %collective-permute-done.1.refs_6_) | copy-start | bytes 6291460
  52.8 54.1 %collective-permute-start.5 = (bf16[2,64,128,128]{3,2,1,0:T(8,128)(2,1)}, bf16[2,64,128,128]{3,2,1,0:T(8,128)(2,1)}, u32[]{:S(2)}, u32[]{:S(2)}) collective-permute-start(bf16[2,64,128,128]{3,2,1,0:T(8,128)(2,1)} %get-tuple-element.117), channel_id=1, source_target_pairs={{0,8},{8,16},{16,24},{24,32},{32,40},{40,48},{48,56},{56,64},{64,7... | collective-permute-start | bytes 12582920 | tf_op jit(solution)/shard_map/ppermute | solution.py:20
  54.3 52.6 %collective-permute-start.4 = (bf16[2,64,128,128]{3,2,1,0:T(8,128)(2,1)}, bf16[2,64,128,128]{3,2,1,0:T(8,128)(2,1)}, u32[]{:S(2)}, u32[]{:S(2)}) collective-permute-start(bf16[2,64,128,128]{3,2,1,0:T(8,128)(2,1)} %get-tuple-element.116), channel_id=1, source_target_pairs={{0,120},{8,0},{16,8},{24,16},{32,24},{40,32},{48,40},{56,48},{64,5... | collective-permute-start | bytes 12582920 | tf_op jit(solution)/shard_map/ppermute | solution.py:20
  57.9 8.7 %copy-start.12 = (bf16[2,64,64,128]{3,2,1,0:T(8,128)(2,1)}, bf16[2,64,64,128]{3,2,1,0:T(8,128)(2,1)S(1)}, u32[]{:S(2)}) copy-start(bf16[2,64,64,128]{3,2,1,0:T(8,128)(2,1)S(1)} %collective-permute-done.2.refs_5_) | copy-start | bytes 6291460
  75.3 65.3 %collective-permute-start.10 = (bf16[2,48,128,128]{3,2,1,0:T(8,128)(2,1)}, bf16[2,48,128,128]{3,2,1,0:T(8,128)(2,1)}, u32[]{:S(2)}, u32[]{:S(2)}) collective-permute-start(bf16[2,48,128,128]{3,2,1,0:T(8,128)(2,1)} %get-tuple-element.135), channel_id=1, source_target_pairs={{0,8},{8,16},{16,24},{24,32},{32,40},{40,48},{48,56},{56,64},{64,7... | collective-permute-start | bytes 9437192 | tf_op jit(solution)/shard_map/ppermute | solution.py:20
  77.1 63.5 %collective-permute-start.9 = (bf16[2,48,128,128]{3,2,1,0:T(8,128)(2,1)}, bf16[2,48,128,128]{3,2,1,0:T(8,128)(2,1)}, u32[]{:S(2)}, u32[]{:S(2)}) collective-permute-start(bf16[2,48,128,128]{3,2,1,0:T(8,128)(2,1)} %get-tuple-element.134), channel_id=1, source_target_pairs={{0,120},{8,0},{16,8},{24,16},{32,24},{40,32},{48,40},{56,48},{64,5... | collective-permute-start | bytes 9437192 | tf_op jit(solution)/shard_map/ppermute | solution.py:20
  91.3 35.9 %all-to-all-start = ((f32[4,2,2,2,48,128]{5,4,3,2,1,0:T(8,128)}), f32[4,2,2,2,48,128]{5,4,3,2,1,0:T(8,128)S(1)}, u32[]{:S(2)}, u32[]{:S(2)}) async-start(f32[4,2,2,2,48,128]{5,4,3,2,1,0:T(8,128)} %bitcast.40), calls=%async_computation | async-start | bytes 1572864 | tf_op jit(solution)/shard_map/all_to_all | solution.py:191
  96.3 56.3 %collective-permute-start.7 = (bf16[2,16,128,128]{3,2,1,0:T(8,128)(2,1)}, bf16[2,16,128,128]{3,2,1,0:T(8,128)(2,1)S(1)}, u32[]{:S(2)}, u32[]{:S(2)}) collective-permute-start(bf16[2,16,128,128]{3,2,1,0:T(8,128)(2,1)} %get-tuple-element.131), channel_id=1, source_target_pairs={{0,120},{8,0},{16,8},{24,16},{32,24},{40,32},{48,40},{56,48},{64,5... | collective-permute-start | bytes 3145736 | tf_op jit(solution)/shard_map/ppermute | solution.py:20
  121.1 31.5 %collective-permute-start.8 = (bf16[2,16,128,128]{3,2,1,0:T(8,128)(2,1)}, bf16[2,16,128,128]{3,2,1,0:T(8,128)(2,1)S(1)}, u32[]{:S(2)}, u32[]{:S(2)}) collective-permute-start(bf16[2,16,128,128]{3,2,1,0:T(8,128)(2,1)} %get-tuple-element.133), channel_id=1, source_target_pairs={{0,8},{8,16},{16,24},{24,32},{32,40},{40,48},{48,56},{56,64},{64,7... | collective-permute-start | bytes 3145736 | tf_op jit(solution)/shard_map/ppermute | solution.py:20
  127.2 31.7 %all-to-all-start.1 = ((f32[4,2,2,2,48,128]{5,4,3,2,1,0:T(8,128)}), f32[4,2,2,2,48,128]{5,4,3,2,1,0:T(8,128)}, u32[]{:S(2)}, u32[]{:S(2)}) async-start(f32[4,2,2,2,48,128]{5,4,3,2,1,0:T(8,128)} %bitcast.39), calls=%async_computation.1 | async-start | bytes 1572864 | tf_op jit(solution)/shard_map/all_to_all | solution.py:191
  132.3 20.3 %copy-start = (bf16[2,16,64,128]{3,2,1,0:T(8,128)(2,1)S(1)}, bf16[2,16,64,128]{3,2,1,0:T(8,128)(2,1)}, u32[]{:S(2)}) copy-start(bf16[2,16,64,128]{3,2,1,0:T(8,128)(2,1)} %get-tuple-element.140.refs_6_) | copy-start | bytes 1572868
  132.3 20.3 %copy-start.1 = (bf16[2,16,64,128]{3,2,1,0:T(8,128)(2,1)S(1)}, bf16[2,16,64,128]{3,2,1,0:T(8,128)(2,1)}, u32[]{:S(2)}) copy-start(bf16[2,16,64,128]{3,2,1,0:T(8,128)(2,1)} %get-tuple-element.127.refs_0_) | copy-start | bytes 1572868
  132.3 20.4 %copy-start.2 = (bf16[2,16,64,128]{3,2,1,0:T(8,128)(2,1)S(1)}, bf16[2,16,64,128]{3,2,1,0:T(8,128)(2,1)}, u32[]{:S(2)}) copy-start(bf16[2,16,64,128]{3,2,1,0:T(8,128)(2,1)} %get-tuple-element.141.refs_7_) | copy-start | bytes 1572868
  132.3 20.4 %copy-start.3 = (bf16[2,16,64,128]{3,2,1,0:T(8,128)(2,1)S(1)}, bf16[2,16,64,128]{3,2,1,0:T(8,128)(2,1)}, u32[]{:S(2)}) copy-start(bf16[2,16,64,128]{3,2,1,0:T(8,128)(2,1)} %get-tuple-element.128.refs_1_) | copy-start | bytes 1572868
  132.3 20.4 %copy-start.4 = (bf16[2,16,128,128]{3,2,1,0:T(8,128)(2,1)S(1)}, bf16[2,16,128,128]{3,2,1,0:T(8,128)(2,1)}, u32[]{:S(2)}) copy-start(bf16[2,16,128,128]{3,2,1,0:T(8,128)(2,1)} %get-tuple-element.142.refs_8_) | copy-start | bytes 3145732
  132.3 20.4 %copy-start.5 = (bf16[2,16,128,128]{3,2,1,0:T(8,128)(2,1)S(1)}, bf16[2,16,128,128]{3,2,1,0:T(8,128)(2,1)}, u32[]{:S(2)}) copy-start(bf16[2,16,128,128]{3,2,1,0:T(8,128)(2,1)} %get-tuple-element.129.refs_2_) | copy-start | bytes 3145732
  132.3 20.4 %copy-start.6 = (bf16[2,16,128,128]{3,2,1,0:T(8,128)(2,1)S(1)}, bf16[2,16,128,128]{3,2,1,0:T(8,128)(2,1)}, u32[]{:S(2)}) copy-start(bf16[2,16,128,128]{3,2,1,0:T(8,128)(2,1)} %get-tuple-element.143.refs_9_) | copy-start | bytes 3145732
  158.9 20.1 %all-to-all-start.2 = ((f32[8,2,2,48,128]{4,3,2,1,0:T(8,128)}), f32[8,2,2,48,128]{4,3,2,1,0:T(8,128)S(1)}, u32[]{:S(2)}, u32[]{:S(2)}) async-start(f32[8,2,2,48,128]{4,3,2,1,0:T(8,128)} %products.7), calls=%async_computation.2 | async-start | bytes 1572864 | tf_op jit(solution)/shard_map/all_to_all | solution.py:184
  166.2 12.8 %collective-permute-start.6 = (f32[2,2,2,48,128]{4,3,2,0,1:T(8,128)S(1)}, f32[2,2,2,48,128]{4,3,2,0,1:T(8,128)S(1)}, u32[]{:S(2)}, u32[]{:S(2)}) collective-permute-start(f32[2,2,2,48,128]{4,3,2,0,1:T(8,128)S(1)} %fusion.1), channel_id=1, source_target_pairs={{0,1},{1,0},{2,3},{3,2},{4,5},{5,4},{6,7},{7,6},{8,9},{9,8},{10,11... | collective-permute-start | bytes 589832 | tf_op jit(solution)/shard_map/ppermute | solution.py:198
  179.1 8.3 %collective-permute-start.11 = (f32[3,2,48,128]{3,2,1,0:T(8,128)S(1)}, f32[3,2,48,128]{3,2,1,0:T(8,128)S(1)}, u32[]{:S(2)}, u32[]{:S(2)}) collective-permute-start(f32[3,2,48,128]{3,2,1,0:T(8,128)S(1)} %get-tuple-element.147), channel_id=1, source_target_pairs={{0,120},{8,0},{16,8},{24,16},{32,24},{40,32},{48,40},{56,48},{64,5... | collective-permute-start | bytes 442376 | tf_op jit(solution)/shard_map/ppermute | solution.py:20
  (4 other events, 12.2 us)

commit v4 on v3

v4 whole, which is shorter than its diff:
```python
import jax
import jax.numpy as jnp
from jax import lax
from jax.experimental import pallas as pl
from jax.experimental.pallas import tpu as pltpu
from jax.sharding import PartitionSpec as P

LANES = 128
CHUNKS = ((0, 64, 1, (64,)), (64, 64, 1, (64,)), (128, 64, 2, (64,)), (256, 64, 2, (48, 16)))
SIDES = (True, False)
GROUPS = ((0, 1), (2,), (3,))
STEPS = {64: 16, 48: 16, 16: 8}
RELAYOUT_COST = 5_000_000_000
PRODUCT_COST = 2
PARAMS = pltpu.CompilerParams(vmem_limit_bytes=56 << 20)


def shifted(value, axis, steps):
    count = lax.axis_size(axis)
    return lax.ppermute(value, axis, [(s, (s + steps) % count) for s in range(count)])


def relayout(states, perm, wraps, chunk, left, own, sends=True):
    first, sub, units, pieces = chunk
    keeps = own is not None
    own = own or ()
    pitch = sub + 1
    each = sub // 8
    sticks = states.shape[2]
    half = sticks // 2
    bands = units * sub
    sent_half, kept_half = (range(half), range(half, sticks)) if left else (range(half, sticks), range(half))
    wanted = [*(sent_half if sends else ()), *(kept_half if keeps else ())]
    low = min(wanted)
    base = 0 if left else low
    pieces = pieces if sends else ()
    halves = (half,) if keeps else ()
    all_bands = states.shape[1]

    def body(perm_ref, wraps_ref, x_ref, *refs):
        outs, scratch = refs[len(own) : -1], refs[-1]

        def spread(start, count):
            for m in range(sub):
                row = x_ref.at[0, m] if left else x_ref.at[0, m // each, m % each]
                row = row[start - base : start - base + count].astype(jnp.float32)
                scratch[pl.ds(start * pitch + m, count, stride=pitch), :] = row

        def put(s, value):
            value = value.astype(jnp.bfloat16)
            at = s % half
            if s in kept_half:
                outs[-1][0, at] = value
                return
            for piece, size in enumerate(pieces):
                if at < size:
                    outs[piece][0, at] = value
                    return
                at -= size

        def plain():
            spread(low, len(wanted))
            for s in wanted:
                put(s, scratch[pl.ds(s * pitch, sub), :])

        def wrapped():
            spread(0, sticks)
            keep = lax.broadcasted_iota(jnp.int32, (sub, LANES), 1) < LANES - 1
            for s in wanted:
                value = scratch[pl.ds(perm_ref[s] * pitch, sub), :]
                put(s, jnp.where(keep, pltpu.roll(value, LANES - 1, 1), 0.0))

        if left:
            pl.when(wraps_ref[0] == 0)(plain)
            pl.when(wraps_ref[0] != 0)(wrapped)
        else:
            plain()

    if left:
        view = states
        in_spec = pl.BlockSpec((1, sub, sticks, LANES), lambda c, g, *_: (c, first // sub + g, 0, 0))
    else:
        view = states.reshape(2, 8, states.shape[1] // 8, sticks, LANES)
        block = (1, 8, each, len(wanted), LANES)
        in_spec = pl.BlockSpec(block, lambda c, g, *_: (c, 0, first // sub + g, low // len(wanted), 0))
    return pl.pallas_call(
        body,
        grid_spec=pltpu.PrefetchScalarGridSpec(
            num_scalar_prefetch=2,
            grid=(2, units),
            in_specs=[in_spec] + [pl.BlockSpec(memory_space=pl.ANY)] * len(own),
            out_specs=[pl.BlockSpec((1, n, sub, LANES), lambda c, g, *_: (c, 0, g, 0)) for n in pieces]
            + [pl.BlockSpec((1, n, sub, LANES), lambda c, g, *_: (c, 0, first // sub + g, 0)) for n in halves],
            scratch_shapes=[pltpu.VMEM((sticks * pitch, LANES), jnp.float32)],
        ),
        out_shape=[jax.ShapeDtypeStruct((2, n, bands, LANES), jnp.bfloat16) for n in pieces]
        + [jax.ShapeDtypeStruct((2, n, all_bands, LANES), jnp.bfloat16) for n in halves],
        input_output_aliases={3 + at: len(pieces) + at for at in range(len(own))},
        compiler_params=PARAMS,
        cost_estimate=pl.CostEstimate(
            flops=RELAYOUT_COST * bands // 64 * len(wanted) // sticks,
            transcendentals=0,
            bytes_accessed=8 * bands * len(wanted) * LANES,
        ),
        name="relayout_left" if left else "relayout_right",
    )(perm, wraps, view, *own)


def products(left, right, units, offset, size, start, finish):
    sides = (left, right)
    run = STEPS[size]
    steps = size // run
    heights = [sum(r.shape[2] for r in rows) for rows, _ in sides]
    widths = [sum(c.shape[2] for c in columns) for _, columns in sides]
    shapes = [(2 * h, 2 * w) for h, w in zip(heights, widths)]

    def stack(refs):
        return jnp.concatenate(
            [jnp.concatenate([r[c, j] for j in range(run)], -1) for c in range(2) for r in refs], 0
        )

    def body(*refs):
        refs = list(refs)
        take = lambda n: [refs.pop(0) for _ in range(n)]
        operands = [(take(len(rows)), take(len(columns))) for rows, columns in sides]
        starts = take(2) if start else None
        outs = take(1) if finish else take(2)
        totals = take(2)
        step = pl.program_id(0)

        @pl.when(step == 0)
        def _():
            for side in range(2):
                totals[side][...] = starts[side][...] if start else jnp.zeros(shapes[side], jnp.float32)

        for side, (rows, columns) in enumerate(operands):
            totals[side][...] += lax.dot_general(
                stack(rows), stack(columns), (((1,), (1,)), ((), ())), preferred_element_type=jnp.float32
            )

        @pl.when(step == steps - 1)
        def _():
            for side in range(2):
                total, h, w = totals[side], heights[side], widths[side]
                if not finish:
                    outs[side][...] = total[...]
                    continue
                real = total[:h, :w] + total[h:, w:]
                imag = total[:h, w:] - total[h:, :w]
                for part, value in enumerate((real, imag)):
                    at, to = 0, 0
                    for unit in units[side]:
                        each = unit // 8
                        for q in range(8):
                            block = value[at : at + each]
                            at += each
                            for n in range(w // LANES):
                                into = n * (h // 8) + to
                                outs[0][q, side, part, into : into + each] = block[:, n * LANES : (n + 1) * LANES]
                        to += each

    def spec(array, begin):
        return pl.BlockSpec((2, run, array.shape[2], LANES), lambda s: (0, begin // run + s, 0, 0))

    in_specs, operands = [], []
    for (rows, columns), (row_begin, column_begin) in zip(sides, ((offset, 0), (0, offset))):
        in_specs += [spec(r, row_begin) for r in rows] + [spec(c, column_begin) for c in columns]
        operands += [*rows, *columns]
    whole = [pl.BlockSpec(shape, lambda s: (0, 0)) for shape in shapes]
    if start:
        in_specs += whole
        operands += start
    if finish:
        out_shape = [(8, 2, 2, 48, LANES)]
        out_specs = [pl.BlockSpec(out_shape[0], lambda s: (0, 0, 0, 0, 0))]
    else:
        out_shape, out_specs = shapes, whole
    return pl.pallas_call(
        body,
        grid=(steps,),
        in_specs=in_specs,
        out_specs=out_specs,
        out_shape=[jax.ShapeDtypeStruct(shape, jnp.float32) for shape in out_shape],
        scratch_shapes=[pltpu.VMEM(shape, jnp.float32) for shape in shapes],
        compiler_params=PARAMS,
        cost_estimate=pl.CostEstimate(
            flops=PRODUCT_COST * 2 * size * LANES * sum(h * w for h, w in shapes),
            transcendentals=0,
            bytes_accessed=4 * size * LANES * sum(h + w for h, w in shapes),
        ),
        name="products",
    )(*operands)


def after(value, *others):
    return lax.optimization_barrier((value, others))[0]


def summed(total):
    return lax.all_to_all(total, "pw", 0, 0, tiled=True).sum(0)


def summed_apart(total):
    count = lax.axis_size("pw")
    groups = [list(range(p, count, 2)) for p in range(2)]
    pairs = total.reshape(count // 2, 2, *total.shape[1:])
    return lax.all_to_all(pairs, "pw", 0, 0, axis_index_groups=groups, tiled=True).sum(0)


def summed_near(pairs):
    side = lax.axis_index("pw") % 2
    kept = lax.dynamic_index_in_dim(pairs, side, 1, keepdims=False)
    sent = lax.dynamic_index_in_dim(pairs, 1 - side, 1, keepdims=False)
    return kept + lax.ppermute(sent, "pw", [(p, p ^ 1) for p in range(lax.axis_size("pw"))])


def shards(states, stick_perm):
    states = states[0]
    sticks = states.shape[2]
    perm = stick_perm - lax.axis_index("pw") * sticks
    token = (lax.axis_index("kz") == 0).astype(jnp.int32).reshape(1)
    own = {True: (), False: ()}
    arrivals = {True: [], False: []}
    for index, chunk in enumerate(CHUNKS):
        for left in SIDES:
            if index > 1:
                token = after(token, arrivals[left][index - 2][0])
            outs = relayout(states, perm, token, chunk, left, own[left] if index else None)
            token, outs = lax.optimization_barrier((token, outs))
            if index:
                *outs, kept = outs
                own[left] = (kept,)
            for piece in range(1, len(outs)):
                if left != SIDES[0]:
                    outs[piece] = after(outs[piece], arrivals[True][index - 1][0])
            arrivals[left].append([shifted(p, "kz", -1 if left else 1) for p in outs])
        if index == 1:
            for left in SIDES:
                own[left] = relayout(states, perm, token, CHUNKS[0], left, own[left], sends=False)
                token, own[left] = lax.optimization_barrier((token, own[left]))
    columns, rows = list(own[True]), list(own[False])
    from_right, from_left = arrivals[True], arrivals[False]

    runs = [[chunk[1]] * chunk[2] for chunk in CHUNKS]
    early = []
    for group in GROUPS:
        totals = None
        pieces = CHUNKS[group[0]][3]
        units = (sum(runs, []), sum((runs[c] for c in group), []))
        for index, size in enumerate(pieces):
            last = index == len(pieces) - 1
            arrived = [[side[c][index] for c in group] for side in (from_right, from_left)]
            if index:
                arrived, totals, early = lax.optimization_barrier((arrived, totals, early))
                near = summed_near(jnp.stack(early))
            totals = products(
                (rows, arrived[0]), (arrived[1], columns), units, sum(pieces[:index]), size, totals, last
            )
        rows, columns, totals, early = lax.optimization_barrier((rows, columns, totals, early))
        if group != GROUPS[-1]:
            early.append(summed_apart(totals[0]))
    near, totals = lax.optimization_barrier((near, totals))
    parts = jnp.concatenate([near, summed(totals[0])[None]])
    groups, _, _, height, _ = parts.shape
    from_left_part = shifted(parts[:, 1], "kz", -1).reshape(groups, 2, groups, height // groups, LANES)
    left = jnp.transpose(parts[:, 0], (2, 1, 0, 3)).reshape(height, 2, groups * LANES)
    right = jnp.transpose(from_left_part, (0, 3, 1, 2, 4)).reshape(height, 2, groups * LANES)
    return (left + right)[:, None]


def solution(mesh):
    in_specs = (P("kz", None, None, "pw", None), P("pw"))
    out_specs = P("pw", "kz", None, None)
    return jax.shard_map(shards, mesh=mesh, in_specs=in_specs, out_specs=out_specs, check_vma=False)
```

time: 189 us -> 186 us (0.984)
  blocking collectives: 0 us -> 18 us
  waiting for transfers between devices: 45.9 us -> 29.9 us
  starting transfers between devices: 37.8 us -> 29.5 us
  Pallas kernels: 97.2 us -> 105 us
  local copies, waits for them, and re-layouts: 4.6 us -> 1.1 us
    all_to_all x0 -> x1, blocking collectives: none -> 18 us  [summed(): return lax.all_to_all(total, 'pw', 0, 0, tiled=True).sum(0)]
    ppermute x11, waiting for transfers between devices: 34.7 us -> 18.1 us  [shifted(): lax.ppermute(value, axis, [(s, (s + steps) % count) for s in range(count)])]
    all_to_all x2, waiting for transfers between devices: 0.01 us -> 11.8 us  [summed_apart(): lax.all_to_all(pairs, 'pw', 0, 0, axis_index_groups=groups, tiled=True)]
    ppermute x1, waiting for transfers between devices: 11.2 us -> 0.01 us  [summed_near(): lax.ppermute(sent, 'pw', [(p, p ^ 1) for p in range(lax.axis_size('pw'))])]
    all_to_all x1 -> x0, starting transfers between devices: 6.05 us -> none  [summed(): return lax.all_to_all(total, 'pw', 0, 0, tiled=True).sum(0)]
    pallas_call x8 -> x10, Pallas kernels: 54.1 us -> 58.7 us  [relayout(): pl.pallas_call(body, grid_spec=pltpu.PrefetchScalarGridSpec(num_scalar_pr...]
    unnamed x26 -> x10, local copies, waits for them, and re-layouts: 3.52 us -> 0.02 us
    pallas_call x4, Pallas kernels: 43.1 us -> 46.4 us  [products(): pl.pallas_call(body, grid=(steps,), in_specs=in_specs, out_specs=out_spec...]
  transfers between devices with their start and end apart: 15 -> 14, of which waited for: 6 -> 3; matrix products, arithmetic and copies ran while one was open for 1% -> 0% of each run, Pallas kernels for 49% -> 55%
where the time goes in v4:
time: 186 us; the launch traced here: 185 us
  Pallas kernels  105 us (56%)
  waiting for transfers between devices  29.9 us (16%)
  starting transfers between devices  29.5 us (16%)
  blocking collectives  18 us (10%)
    pallas_call x10, Pallas kernels, relayout(): pl.pallas_call(body, grid_spec=pltpu.PrefetchScalarGridSpec(num_scalar_pr...  58.7 us
    pallas_call x4, Pallas kernels, products(): pl.pallas_call(body, grid=(steps,), in_specs=in_specs, out_specs=out_spec...  46.4 us
    ppermute x11, starting transfers between devices, shifted(): lax.ppermute(value, axis, [(s, (s + steps) % count) for s in range(count)])  19.6 us
    ppermute x11, waiting for transfers between devices, shifted(): lax.ppermute(value, axis, [(s, (s + steps) % count) for s in range(count)])  18.1 us
    all_to_all x1, blocking collectives, summed(): return lax.all_to_all(total, 'pw', 0, 0, tiled=True).sum(0)  18 us
    all_to_all x2, waiting for transfers between devices, summed_apart(): lax.all_to_all(pairs, 'pw', 0, 0, axis_index_groups=groups, tiled=True)  11.8 us
    all_to_all x2, starting transfers between devices, summed_apart(): lax.all_to_all(pairs, 'pw', 0, 0, axis_index_groups=groups, tiled=True)  8.51 us
  transfers between devices with their start and end apart: 14, of which 3 were waited for; matrix products, arithmetic and copies ran while one was open for 0% of the time, Pallas kernels for 55%

profile of v4, /device:TPU:7, one launch (start us, length us, event | category | flops | bytes accessed | tf_op | source)
XLA Modules:
  0.0 185.2 jit_solution(16799142838343582758)
XLA Ops:
  1.2 4.1 %relayout_left.5 = bf16[2,64,64,128]{3,2,1,0:T(8,128)(2,1)} custom-call(s32[128]{0:T(128)} %broadcast_subtract_fusion.perm_ref, s32[1]{0:T(128)} %bitcast.wraps_ref, bf16[2,384,128,128]{3,2,1,0:T(8,128)(2,1)} %bitcast.27), custom_call_target="tpu_custom_call" | custom-call | flops 2500000000 | bytes 4194304 | tf_op jit(solution)/shard_map/relayout_left/pallas_call | solution.py:86
  6.0 3.4 %relayout_right.5 = bf16[2,64,64,128]{3,2,1,0:T(8,128)(2,1)} custom-call(s32[128]{0:T(128)} %broadcast_subtract_fusion.perm_ref, s32[1]{0:T(128)} %bitcast.wraps_ref, bf16[2,8,48,128,128]{4,3,2,1,0:T(8,128)(2,1)} %bitcast.28), custom_call_target="tpu_custom_call" | custom-call | flops 2500000000 | bytes 4194304 | tf_op jit(solution)/shard_map/relayout_right/pallas_call | solution.py:86
  9.4 4.7 %collective-permute-start.1 = (bf16[2,64,64,128]{3,2,1,0:T(8,128)(2,1)}, bf16[2,64,64,128]{3,2,1,0:T(8,128)(2,1)S(1)}, u32[]{:S(2)}, u32[]{:S(2)}) collective-permute-start(bf16[2,64,64,128]{3,2,1,0:T(8,128)(2,1)} %relayout_right.5), channel_id=1, source_target_pairs={{0,8},{8,16},{16,24},{24,32},{32,40},{40,48},{48,56},{56,64},{64,7... | collective-permute-start | bytes 6291464 | tf_op jit(solution)/shard_map/ppermute | solution.py:20
  14.1 4.7 %relayout_left.6 = (bf16[2,64,64,128]{3,2,1,0:T(8,128)(2,1)}, bf16[2,64,384,128]{3,2,1,0:T(8,128)(2,1)}) custom-call(s32[128]{0:T(128)} %broadcast_subtract_fusion.perm_ref, s32[1]{0:T(128)} %bitcast.wraps_ref, bf16[2,384,128,128]{3,2,1,0:T(8,128)(2,1)} %bitcast.29), custom_call_target="tpu_custom_call" | custom-call | flops 5000000000 | bytes 8388608 | tf_op jit(solution)/shard_map/relayout_left/pallas_call | solution.py:86
  18.8 4.8 %relayout_right.6 = (bf16[2,64,64,128]{3,2,1,0:T(8,128)(2,1)}, bf16[2,64,384,128]{3,2,1,0:T(8,128)(2,1)}) custom-call(s32[128]{0:T(128)} %broadcast_subtract_fusion.perm_ref, s32[1]{0:T(128)} %bitcast.wraps_ref, bf16[2,8,48,128,128]{4,3,2,1,0:T(8,128)(2,1)} %bitcast.30), custom_call_target="tpu_custom_call" | custom-call | flops 5000000000 | bytes 8388608 | tf_op jit(solution)/shard_map/relayout_right/pallas_call | solution.py:86
  23.6 5.4 %collective-permute-start.4 = (bf16[2,64,64,128]{3,2,1,0:T(8,128)(2,1)}, bf16[2,64,64,128]{3,2,1,0:T(8,128)(2,1)}, u32[]{:S(2)}, u32[]{:S(2)}) collective-permute-start(bf16[2,64,64,128]{3,2,1,0:T(8,128)(2,1)} %get-tuple-element.101), channel_id=1, source_target_pairs={{0,8},{8,16},{16,24},{24,32},{32,40},{40,48},{48,56},{56,64},{64,7... | collective-permute-start | bytes 6291464 | tf_op jit(solution)/shard_map/ppermute | solution.py:20
  29.0 4.2 %relayout_left.7.refs_0_ = bf16[2,64,384,128]{3,2,1,0:T(8,128)(2,1)} custom-call(s32[128]{0:T(128)} %broadcast_subtract_fusion.perm_ref, s32[1]{0:T(128)} %bitcast.wraps_ref, bf16[2,384,128,128]{3,2,1,0:T(8,128)(2,1)} %bitcast.31, bf16[2,64,384,128]{3,2,1,0:T(8,128)(2,1)} %get-tuple-element.77.refs_0_), custom_call_target="tpu_custom_call", output_to_operand_aliasing={{}: (3, {})} | custom-call | flops 2500000000 | bytes 4194304 | tf_op jit(solution)/shard_map/relayout_left/pallas_call | solution.py:86
  33.2 3.5 %relayout_right.7.refs_0_ = bf16[2,64,384,128]{3,2,1,0:T(8,128)(2,1)} custom-call(s32[128]{0:T(128)} %broadcast_subtract_fusion.perm_ref, s32[1]{0:T(128)} %bitcast.wraps_ref, bf16[2,8,48,128,128]{4,3,2,1,0:T(8,128)(2,1)} %bitcast.32, bf16[2,64,384,128]{3,2,1,0:T(8,128)(2,1)} %get-tuple-element.79.refs_0_), custom_call_target="tpu_custom_call", output_to_operand_aliasing={{}: (3, {})} | custom-call | flops 2500000000 | bytes 4194304 | tf_op jit(solution)/shard_map/relayout_right/pallas_call | solution.py:86
  36.7 8.4 %relayout_left.8 = (bf16[2,64,128,128]{3,2,1,0:T(8,128)(2,1)}, bf16[2,64,384,128]{3,2,1,0:T(8,128)(2,1)}) custom-call(s32[128]{0:T(128)} %broadcast_subtract_fusion.perm_ref, s32[1]{0:T(128)} %bitcast.wraps_ref, bf16[2,384,128,128]{3,2,1,0:T(8,128)(2,1)} %bitcast.33, bf16[2,64,384,128]{3,2,1,0:T(8,128)(2,1)} %relayout_left.7.refs_0_), custom_call_target="tpu_custom_call", output_to_operand_aliasing={{1}: (3, {})} | custom-call | flops 10000000000 | bytes 16777216 | tf_op jit(solution)/shard_map/relayout_left/pallas_call | solution.py:86
  45.2 8.5 %relayout_right.8 = (bf16[2,64,128,128]{3,2,1,0:T(8,128)(2,1)}, bf16[2,64,384,128]{3,2,1,0:T(8,128)(2,1)}) custom-call(s32[128]{0:T(128)} %broadcast_subtract_fusion.perm_ref, s32[1]{0:T(128)} %bitcast.wraps_ref, bf16[2,8,48,128,128]{4,3,2,1,0:T(8,128)(2,1)} %bitcast.34, bf16[2,64,384,128]{3,2,1,0:T(8,128)(2,1)} %relayout_right.7.refs_0_), custom_call_target="tpu_custom_call", output_to_operand_aliasing={{1}: (3, {})} | custom-call | flops 10000000000 | bytes 16777216 | tf_op jit(solution)/shard_map/relayout_right/pallas_call | solution.py:86
  53.7 5.3 %collective-permute-start.7 = (bf16[2,64,128,128]{3,2,1,0:T(8,128)(2,1)}, bf16[2,64,128,128]{3,2,1,0:T(8,128)(2,1)}, u32[]{:S(2)}, u32[]{:S(2)}) collective-permute-start(bf16[2,64,128,128]{3,2,1,0:T(8,128)(2,1)} %get-tuple-element.114), channel_id=1, source_target_pairs={{0,8},{8,16},{16,24},{24,32},{32,40},{40,48},{48,56},{56,64},{64,7... | collective-permute-start | bytes 12582920 | tf_op jit(solution)/shard_map/ppermute | solution.py:20
  59.0 8.5 %relayout_left.9 = (bf16[2,48,128,128]{3,2,1,0:T(8,128)(2,1)}, bf16[2,16,128,128]{3,2,1,0:T(8,128)(2,1)}, bf16[2,64,384,128]{3,2,1,0:T(8,128)(2,1)}) custom-call(s32[128]{0:T(128)} %broadcast_subtract_fusion.perm_ref, s32[1]{0:T(128)} %bitcast.wraps_ref, bf16[2,384,128,128]{3,2,1,0:T(8,128)(2,1)} %bitcast.35, ...), custom_call_target="tpu_custom_call", output_to_operand_aliasing={{2}: (3, {})} | custom-call | flops 10000000000 | bytes 16777216 | tf_op jit(solution)/shard_map/relayout_left/pallas_call | solution.py:86
  67.5 8.6 %relayout_right.9 = (bf16[2,48,128,128]{3,2,1,0:T(8,128)(2,1)}, bf16[2,16,128,128]{3,2,1,0:T(8,128)(2,1)}, bf16[2,64,384,128]{3,2,1,0:T(8,128)(2,1)}) custom-call(s32[128]{0:T(128)} %broadcast_subtract_fusion.perm_ref, s32[1]{0:T(128)} %bitcast.wraps_ref, bf16[2,8,48,128,128]{4,3,2,1,0:T(8,128)(2,1)} %bitcast.36, ...), custom_call_target="tpu_custom_call", output_to_operand_aliasing={{2}: (3, {})} | custom-call | flops 10000000000 | bytes 16777216 | tf_op jit(solution)/shard_map/relayout_right/pallas_call | solution.py:86
  76.6 14.3 %products.4 = f32[8,2,2,48,128]{4,3,2,1,0:T(8,128)} custom-call(bf16[2,64,384,128]{3,2,1,0:T(8,128)(2,1)} %get-tuple-element.116.refs_0_, bf16[2,64,64,128]{3,2,1,0:T(8,128)(2,1)} %copy-done.2, bf16[2,64,64,128]{3,2,1,0:T(8,128)(2,1)} %copy-done.4, bf16[2,64,64,128]{3,2,1,0:T(8,128)(2,1)} %copy-done.3, ...), custom_call_target="tpu_custom_call" | custom-call | flops 12884901888 | bytes 67108864 | tf_op jit(solution)/shard_map/products/pallas_call | solution.py:178
  90.8 5.0 %all-to-all-start = ((f32[4,2,2,2,48,128]{5,4,3,2,1,0:T(8,128)}), f32[4,2,2,2,48,128]{5,4,3,2,1,0:T(8,128)S(1)}, u32[]{:S(2)}, u32[]{:S(2)}) async-start(f32[4,2,2,2,48,128]{5,4,3,2,1,0:T(8,128)} %bitcast.41), calls=%async_computation | async-start | bytes 1572864 | tf_op jit(solution)/shard_map/all_to_all | solution.py:207
  96.2 11.8 %all-to-all-done = f32[4,2,2,2,48,128]{5,4,3,2,1,0:T(8,128)S(1)} async-done(((f32[4,2,2,2,48,128]{5,4,3,2,1,0:T(8,128)}), f32[4,2,2,2,48,128]{5,4,3,2,1,0:T(8,128)S(1)}, u32[]{:S(2)}, u32[]{:S(2)}) %all-to-all-start) | async-done | bytes 786464 | tf_op jit(solution)/shard_map/all_to_all | solution.py:207
  108.0 2.6 %collective-permute-start.6 = (bf16[2,16,128,128]{3,2,1,0:T(8,128)(2,1)}, bf16[2,16,128,128]{3,2,1,0:T(8,128)(2,1)S(1)}, u32[]{:S(2)}, u32[]{:S(2)}) collective-permute-start(bf16[2,16,128,128]{3,2,1,0:T(8,128)(2,1)} %get-tuple-element.109), channel_id=1, source_target_pairs={{0,8},{8,16},{16,24},{24,32},{32,40},{40,48},{48,56},{56,64},{64,7... | collective-permute-start | bytes 3145736 | tf_op jit(solution)/shard_map/ppermute | solution.py:20
  110.6 14.3 %products.5 = f32[8,2,2,48,128]{4,3,2,1,0:T(8,128)} custom-call(bf16[2,64,384,128]{3,2,1,0:T(8,128)(2,1)} %get-tuple-element.116.refs_0_, bf16[2,64,128,128]{3,2,1,0:T(8,128)(2,1)} %collective-permute-done.5.refs_1_, bf16[2,64,128,128]{3,2,1,0:T(8,128)(2,1)} %collective-permute-done.7.refs_2_, bf16[2,64,384,128]{3,2,1,0:T(8,128)(2,1)} %get-tuple-element.119.refs_5_.refs_3_), custom_call_target="tpu_custom_call" | custom-call | flops 12884901888 | bytes 67108864 | tf_op jit(solution)/shard_map/products/pallas_call | solution.py:178
  124.9 3.5 %all-to-all-start.1 = ((f32[4,2,2,2,48,128]{5,4,3,2,1,0:T(8,128)}), f32[4,2,2,2,48,128]{5,4,3,2,1,0:T(8,128)S(1)}, u32[]{:S(2)}, u32[]{:S(2)}) async-start(f32[4,2,2,2,48,128]{5,4,3,2,1,0:T(8,128)} %bitcast.42), calls=%async_computation.1 | async-start | bytes 1572864 | tf_op jit(solution)/shard_map/all_to_all | solution.py:207
  128.4 10.1 %collective-permute-done.9.refs_2_ = bf16[2,48,128,128]{3,2,1,0:T(8,128)(2,1)} collective-permute-done((bf16[2,48,128,128]{3,2,1,0:T(8,128)(2,1)}, bf16[2,48,128,128]{3,2,1,0:T(8,128)(2,1)}, u32[]{:S(2)}, u32[]{:S(2)}) %collective-permute-start.9) | collective-permute-done | bytes 3145760 | tf_op jit(solution)/shard_map/ppermute | solution.py:20
  138.5 12.0 %products.6 = (f32[768,256]{1,0:T(8,128)}, f32[256,768]{1,0:T(8,128)}) custom-call(bf16[2,64,384,128]{3,2,1,0:T(8,128)(2,1)} %get-tuple-element.116.refs_0_, bf16[2,48,128,128]{3,2,1,0:T(8,128)(2,1)} %collective-permute-done.8.refs_1_, bf16[2,48,128,128]{3,2,1,0:T(8,128)(2,1)} %collective-permute-done.9.refs_2_, ...), custom_call_target="tpu_custom_call" | custom-call | flops 9663676416 | bytes 50331648 | tf_op jit(solution)/shard_map/products/pallas_call | solution.py:178
  152.0 5.9 %products.7 = f32[8,2,2,48,128]{4,3,2,1,0:T(8,128)} custom-call(bf16[2,64,384,128]{3,2,1,0:T(8,128)(2,1)} %get-tuple-element.116.refs_0_, bf16[2,16,128,128]{3,2,1,0:T(8,128)(2,1)} %copy-done, bf16[2,16,128,128]{3,2,1,0:T(8,128)(2,1)} %copy-done.1, bf16[2,64,384,128]{3,2,1,0:T(8,128)(2,1)} %get-tuple-element.119.refs_5_.refs_3_, ...), custom_call_target="tpu_custom_call" | custom-call | flops 3221225472 | bytes 16777216 | tf_op jit(solution)/shard_map/products/pallas_call | solution.py:178
  157.9 18.0 %all_to_all.15 = f32[8,2,2,48,128]{4,3,2,1,0:T(8,128)S(1)} all-to-all(f32[8,2,2,48,128]{4,3,2,1,0:T(8,128)} %products.7), channel_id=1, replica_groups=mesh['kz'=16,'pw'=8] {'pw'}, dimensions={0} | all-to-all | bytes 1572864 | tf_op jit(solution)/shard_map/all_to_all | solution.py:200
  176.3 8.0 %collective-permute-done.11 = f32[3,2,48,128]{3,2,1,0:T(8,128)S(1)} collective-permute-done((f32[3,2,48,128]{3,2,1,0:T(8,128)S(1)}, f32[3,2,48,128]{3,2,1,0:T(8,128)S(1)}, u32[]{:S(2)}, u32[]{:S(2)}) %collective-permute-start.11) | collective-permute-done | bytes 147488 | tf_op jit(solution)/shard_map/ppermute | solution.py:20
  (42 shorter events, 5.5 us)
Async XLA Ops:
  5.3 31.4 %collective-permute-start = (bf16[2,64,64,128]{3,2,1,0:T(8,128)(2,1)}, bf16[2,64,64,128]{3,2,1,0:T(8,128)(2,1)S(1)}, u32[]{:S(2)}, u32[]{:S(2)}) collective-permute-start(bf16[2,64,64,128]{3,2,1,0:T(8,128)(2,1)} %relayout_left.5), channel_id=1, source_target_pairs={{0,120},{8,0},{16,8},{24,16},{32,24},{40,32},{48,40},{56,48},{64,5... | collective-permute-start | bytes 6291464 | tf_op jit(solution)/shard_map/ppermute | solution.py:20
  9.4 35.7 %collective-permute-start.1 = (bf16[2,64,64,128]{3,2,1,0:T(8,128)(2,1)}, bf16[2,64,64,128]{3,2,1,0:T(8,128)(2,1)S(1)}, u32[]{:S(2)}, u32[]{:S(2)}) collective-permute-start(bf16[2,64,64,128]{3,2,1,0:T(8,128)(2,1)} %relayout_right.5), channel_id=1, source_target_pairs={{0,8},{8,16},{16,24},{24,32},{32,40},{40,48},{48,56},{56,64},{64,7... | collective-permute-start | bytes 6291464 | tf_op jit(solution)/shard_map/ppermute | solution.py:20
  18.8 40.2 %collective-permute-start.2 = (bf16[2,64,64,128]{3,2,1,0:T(8,128)(2,1)}, bf16[2,64,64,128]{3,2,1,0:T(8,128)(2,1)S(1)}, u32[]{:S(2)}, u32[]{:S(2)}) collective-permute-start(bf16[2,64,64,128]{3,2,1,0:T(8,128)(2,1)} %get-tuple-element.93), channel_id=1, source_target_pairs={{0,120},{8,0},{16,8},{24,16},{32,24},{40,32},{48,40},{56,48},{64,5... | collective-permute-start | bytes 6291464 | tf_op jit(solution)/shard_map/ppermute | solution.py:20
  23.6 43.9 %collective-permute-start.4 = (bf16[2,64,64,128]{3,2,1,0:T(8,128)(2,1)}, bf16[2,64,64,128]{3,2,1,0:T(8,128)(2,1)}, u32[]{:S(2)}, u32[]{:S(2)}) collective-permute-start(bf16[2,64,64,128]{3,2,1,0:T(8,128)(2,1)} %get-tuple-element.101), channel_id=1, source_target_pairs={{0,8},{8,16},{16,24},{24,32},{32,40},{40,48},{48,56},{56,64},{64,7... | collective-permute-start | bytes 6291464 | tf_op jit(solution)/shard_map/ppermute | solution.py:20
  36.7 8.4 %copy-start.2 = (bf16[2,64,64,128]{3,2,1,0:T(8,128)(2,1)}, bf16[2,64,64,128]{3,2,1,0:T(8,128)(2,1)S(1)}, u32[]{:S(2)}) copy-start(bf16[2,64,64,128]{3,2,1,0:T(8,128)(2,1)S(1)} %collective-permute-done.refs_1_) | copy-start | bytes 6291460
  45.1 8.6 %copy-start.3 = (bf16[2,64,64,128]{3,2,1,0:T(8,128)(2,1)}, bf16[2,64,64,128]{3,2,1,0:T(8,128)(2,1)S(1)}, u32[]{:S(2)}) copy-start(bf16[2,64,64,128]{3,2,1,0:T(8,128)(2,1)S(1)} %collective-permute-done.1.refs_3_) | copy-start | bytes 6291460
  45.2 62.9 %collective-permute-start.5 = (bf16[2,64,128,128]{3,2,1,0:T(8,128)(2,1)}, bf16[2,64,128,128]{3,2,1,0:T(8,128)(2,1)}, u32[]{:S(2)}, u32[]{:S(2)}) collective-permute-start(bf16[2,64,128,128]{3,2,1,0:T(8,128)(2,1)} %get-tuple-element.108), channel_id=1, source_target_pairs={{0,120},{8,0},{16,8},{24,16},{32,24},{40,32},{48,40},{56,48},{64,5... | collective-permute-start | bytes 12582920 | tf_op jit(solution)/shard_map/ppermute | solution.py:20
  53.7 56.9 %collective-permute-start.7 = (bf16[2,64,128,128]{3,2,1,0:T(8,128)(2,1)}, bf16[2,64,128,128]{3,2,1,0:T(8,128)(2,1)}, u32[]{:S(2)}, u32[]{:S(2)}) collective-permute-start(bf16[2,64,128,128]{3,2,1,0:T(8,128)(2,1)} %get-tuple-element.114), channel_id=1, source_target_pairs={{0,8},{8,16},{16,24},{24,32},{32,40},{40,48},{48,56},{56,64},{64,7... | collective-permute-start | bytes 12582920 | tf_op jit(solution)/shard_map/ppermute | solution.py:20
  59.0 8.5 %copy-start.4 = (bf16[2,64,64,128]{3,2,1,0:T(8,128)(2,1)}, bf16[2,64,64,128]{3,2,1,0:T(8,128)(2,1)S(1)}, u32[]{:S(2)}) copy-start(bf16[2,64,64,128]{3,2,1,0:T(8,128)(2,1)S(1)} %collective-permute-done.2.refs_2_) | copy-start | bytes 6291460
  76.1 62.4 %collective-permute-start.9 = (bf16[2,48,128,128]{3,2,1,0:T(8,128)(2,1)}, bf16[2,48,128,128]{3,2,1,0:T(8,128)(2,1)}, u32[]{:S(2)}, u32[]{:S(2)}) collective-permute-start(bf16[2,48,128,128]{3,2,1,0:T(8,128)(2,1)} %get-tuple-element.118), channel_id=1, source_target_pairs={{0,8},{8,16},{16,24},{24,32},{32,40},{40,48},{48,56},{56,64},{64,7... | collective-permute-start | bytes 9437192 | tf_op jit(solution)/shard_map/ppermute | solution.py:20
  76.1 62.4 %collective-permute-start.8 = (bf16[2,48,128,128]{3,2,1,0:T(8,128)(2,1)}, bf16[2,48,128,128]{3,2,1,0:T(8,128)(2,1)}, u32[]{:S(2)}, u32[]{:S(2)}) collective-permute-start(bf16[2,48,128,128]{3,2,1,0:T(8,128)(2,1)} %get-tuple-element.117), channel_id=1, source_target_pairs={{0,120},{8,0},{16,8},{24,16},{32,24},{40,32},{48,40},{56,48},{64,5... | collective-permute-start | bytes 9437192 | tf_op jit(solution)/shard_map/ppermute | solution.py:20
  90.8 17.1 %all-to-all-start = ((f32[4,2,2,2,48,128]{5,4,3,2,1,0:T(8,128)}), f32[4,2,2,2,48,128]{5,4,3,2,1,0:T(8,128)S(1)}, u32[]{:S(2)}, u32[]{:S(2)}) async-start(f32[4,2,2,2,48,128]{5,4,3,2,1,0:T(8,128)} %bitcast.41), calls=%async_computation | async-start | bytes 1572864 | tf_op jit(solution)/shard_map/all_to_all | solution.py:207
  95.9 54.7 %collective-permute-start.3 = (bf16[2,16,128,128]{3,2,1,0:T(8,128)(2,1)}, bf16[2,16,128,128]{3,2,1,0:T(8,128)(2,1)S(1)}, u32[]{:S(2)}, u32[]{:S(2)}) collective-permute-start(bf16[2,16,128,128]{3,2,1,0:T(8,128)(2,1)} %get-tuple-element.99), channel_id=1, source_target_pairs={{0,120},{8,0},{16,8},{24,16},{32,24},{40,32},{48,40},{56,48},{64,5... | collective-permute-start | bytes 3145736 | tf_op jit(solution)/shard_map/ppermute | solution.py:20
  108.0 42.6 %collective-permute-start.6 = (bf16[2,16,128,128]{3,2,1,0:T(8,128)(2,1)}, bf16[2,16,128,128]{3,2,1,0:T(8,128)(2,1)S(1)}, u32[]{:S(2)}, u32[]{:S(2)}) collective-permute-start(bf16[2,16,128,128]{3,2,1,0:T(8,128)(2,1)} %get-tuple-element.109), channel_id=1, source_target_pairs={{0,8},{8,16},{16,24},{24,32},{32,40},{40,48},{48,56},{56,64},{64,7... | collective-permute-start | bytes 3145736 | tf_op jit(solution)/shard_map/ppermute | solution.py:20
  124.9 25.6 %all-to-all-start.1 = ((f32[4,2,2,2,48,128]{5,4,3,2,1,0:T(8,128)}), f32[4,2,2,2,48,128]{5,4,3,2,1,0:T(8,128)S(1)}, u32[]{:S(2)}, u32[]{:S(2)}) async-start(f32[4,2,2,2,48,128]{5,4,3,2,1,0:T(8,128)} %bitcast.42), calls=%async_computation.1 | async-start | bytes 1572864 | tf_op jit(solution)/shard_map/all_to_all | solution.py:207
  150.6 1.4 copy-start
  150.6 1.4 copy-start.1
  150.6 7.3 %collective-permute-start.10 = (f32[2,2,2,48,128]{4,3,2,0,1:T(8,128)S(1)}, f32[2,2,2,48,128]{4,3,2,0,1:T(8,128)S(1)}, u32[]{:S(2)}, u32[]{:S(2)}) collective-permute-start(f32[2,2,2,48,128]{4,3,2,0,1:T(8,128)S(1)} %fusion.1), channel_id=1, source_target_pairs={{0,1},{1,0},{2,3},{3,2},{4,5},{5,4},{6,7},{7,6},{8,9},{9,8},{10,11... | collective-permute-start | bytes 589832 | tf_op jit(solution)/shard_map/ppermute | solution.py:214
  176.0 8.3 %collective-permute-start.11 = (f32[3,2,48,128]{3,2,1,0:T(8,128)S(1)}, f32[3,2,48,128]{3,2,1,0:T(8,128)S(1)}, u32[]{:S(2)}, u32[]{:S(2)}) collective-permute-start(f32[3,2,48,128]{3,2,1,0:T(8,128)S(1)} %get-tuple-element.133), channel_id=1, source_target_pairs={{0,120},{8,0},{16,8},{24,16},{32,24},{40,32},{48,40},{56,48},{64,5... | collective-permute-start | bytes 442376 | tf_op jit(solution)/shard_map/ppermute | solution.py:20

commit v5 on v4

--- a/solution.py
+++ b/solution.py
@@ -20,7 +20,7 @@
     return lax.ppermute(value, axis, [(s, (s + steps) % count) for s in range(count)])
 
 
-def relayout(states, perm, wraps, chunk, left, own, sends=True):
+def relayout(states, perm, base_stick, wraps, chunk, left, own, sends=True):
     first, sub, units, pieces = chunk
     keeps = own is not None
     own = own or ()
@@ -37,7 +37,7 @@
     halves = (half,) if keeps else ()
     all_bands = states.shape[1]
 
-    def body(perm_ref, wraps_ref, x_ref, *refs):
+    def body(perm_ref, base_ref, wraps_ref, x_ref, *refs):
         outs, scratch = refs[len(own) : -1], refs[-1]
 
         def spread(start, count):
@@ -67,7 +67,7 @@
             spread(0, sticks)
             keep = lax.broadcasted_iota(jnp.int32, (sub, LANES), 1) < LANES - 1
             for s in wanted:
-                value = scratch[pl.ds(perm_ref[s] * pitch, sub), :]
+                value = scratch[pl.ds((perm_ref[s] - base_ref[0]) * pitch, sub), :]
                 put(s, jnp.where(keep, pltpu.roll(value, LANES - 1, 1), 0.0))
 
         if left:
@@ -86,7 +86,7 @@
     return pl.pallas_call(
         body,
         grid_spec=pltpu.PrefetchScalarGridSpec(
-            num_scalar_prefetch=2,
+            num_scalar_prefetch=3,
             grid=(2, units),
             in_specs=[in_spec] + [pl.BlockSpec(memory_space=pl.ANY)] * len(own),
             out_specs=[pl.BlockSpec((1, n, sub, LANES), lambda c, g, *_: (c, 0, g, 0)) for n in pieces]
@@ -95,7 +95,7 @@
         ),
         out_shape=[jax.ShapeDtypeStruct((2, n, bands, LANES), jnp.bfloat16) for n in pieces]
         + [jax.ShapeDtypeStruct((2, n, all_bands, LANES), jnp.bfloat16) for n in halves],
-        input_output_aliases={3 + at: len(pieces) + at for at in range(len(own))},
+        input_output_aliases={4 + at: len(pieces) + at for at in range(len(own))},
         compiler_params=PARAMS,
         cost_estimate=pl.CostEstimate(
             flops=RELAYOUT_COST * bands // 64 * len(wanted) // sticks,
@@ -103,7 +103,7 @@
             bytes_accessed=8 * bands * len(wanted) * LANES,
         ),
         name="relayout_left" if left else "relayout_right",
-    )(perm, wraps, view, *own)
+    )(perm, base_stick, wraps, view, *own)
 
 
 def products(left, right, units, offset, size, start, finish):
@@ -217,7 +217,7 @@
 def shards(states, stick_perm):
     states = states[0]
     sticks = states.shape[2]
-    perm = stick_perm - lax.axis_index("pw") * sticks
+    base_stick = (lax.axis_index("pw") * sticks).astype(jnp.int32).reshape(1)
     token = (lax.axis_index("kz") == 0).astype(jnp.int32).reshape(1)
     own = {True: (), False: ()}
     arrivals = {True: [], False: []}
@@ -225,7 +225,7 @@
         for left in SIDES:
             if index > 1:
                 token = after(token, arrivals[left][index - 2][0])
-            outs = relayout(states, perm, token, chunk, left, own[left] if index else None)
+            outs = relayout(states, stick_perm, base_stick, token, chunk, left, own[left] if index else None)
             token, outs = lax.optimization_barrier((token, outs))
             if index:
                 *outs, kept = outs
@@ -236,7 +236,7 @@
             arrivals[left].append([shifted(p, "kz", -1 if left else 1) for p in outs])
         if index == 1:
             for left in SIDES:
-                own[left] = relayout(states, perm, token, CHUNKS[0], left, own[left], sends=False)
+                own[left] = relayout(states, stick_perm, base_stick, token, CHUNKS[0], left, own[left], sends=False)
                 token, own[left] = lax.optimization_barrier((token, own[left]))
     columns, rows = list(own[True]), list(own[False])
     from_right, from_left = arrivals[True], arrivals[False]

time: 186 us -> 185 us (level)
  no operation moved by 1% of the time
where the time goes in v5:
time: 185 us; the launch traced here: 184 us
  Pallas kernels  105 us (57%)
  waiting for transfers between devices  29.9 us (16%)
  starting transfers between devices  29.5 us (16%)
  blocking collectives  18 us (10%)
    pallas_call x10, Pallas kernels, relayout(): pl.pallas_call(body, grid_spec=pltpu.PrefetchScalarGridSpec(num_scalar_pr...  58.7 us
    pallas_call x4, Pallas kernels, products(): pl.pallas_call(body, grid=(steps,), in_specs=in_specs, out_specs=out_spec...  46.4 us
    ppermute x11, starting transfers between devices, shifted(): lax.ppermute(value, axis, [(s, (s + steps) % count) for s in range(count)])  19.6 us
    ppermute x11, waiting for transfers between devices, shifted(): lax.ppermute(value, axis, [(s, (s + steps) % count) for s in range(count)])  18.1 us
    all_to_all x1, blocking collectives, summed(): return lax.all_to_all(total, 'pw', 0, 0, tiled=True).sum(0)  18 us
    all_to_all x2, waiting for transfers between devices, summed_apart(): lax.all_to_all(pairs, 'pw', 0, 0, axis_index_groups=groups, tiled=True)  11.8 us
    all_to_all x2, starting transfers between devices, summed_apart(): lax.all_to_all(pairs, 'pw', 0, 0, axis_index_groups=groups, tiled=True)  8.53 us
  transfers between devices with their start and end apart: 14, of which 3 were waited for; matrix products, arithmetic and copies ran while one was open for 0% of the time, Pallas kernels for 55%

profile of v5, /device:TPU:7, one launch (start us, length us, event | category | flops | bytes accessed | tf_op | source)
XLA Modules:
  0.0 184.1 jit_solution(16951735232748933704)
XLA Ops:
  0.0 4.1 %relayout_left.5 = bf16[2,64,64,128]{3,2,1,0:T(8,128)(2,1)} custom-call(s32[128]{0:T(128)} %perm_ref.19, s32[1]{0:T(128)} %bitcast.1.base_ref, s32[1]{0:T(128)} %bitcast.wraps_ref, bf16[2,384,128,128]{3,2,1,0:T(8,128)(2,1)} %bitcast.28), custom_call_target="tpu_custom_call" | custom-call | flops 2500000000 | bytes 4194304 | tf_op jit(solution)/shard_map/relayout_left/pallas_call | solution.py:86
  4.8 3.4 %relayout_right.5 = bf16[2,64,64,128]{3,2,1,0:T(8,128)(2,1)} custom-call(s32[128]{0:T(128)} %perm_ref.19, s32[1]{0:T(128)} %bitcast.1.base_ref, s32[1]{0:T(128)} %bitcast.wraps_ref, bf16[2,8,48,128,128]{4,3,2,1,0:T(8,128)(2,1)} %bitcast.29), custom_call_target="tpu_custom_call" | custom-call | flops 2500000000 | bytes 4194304 | tf_op jit(solution)/shard_map/relayout_right/pallas_call | solution.py:86
  8.3 4.7 %collective-permute-start.1 = (bf16[2,64,64,128]{3,2,1,0:T(8,128)(2,1)}, bf16[2,64,64,128]{3,2,1,0:T(8,128)(2,1)S(1)}, u32[]{:S(2)}, u32[]{:S(2)}) collective-permute-start(bf16[2,64,64,128]{3,2,1,0:T(8,128)(2,1)} %relayout_right.5), channel_id=1, source_target_pairs={{0,8},{8,16},{16,24},{24,32},{32,40},{40,48},{48,56},{56,64},{64,7... | collective-permute-start | bytes 6291464 | tf_op jit(solution)/shard_map/ppermute | solution.py:20
  12.9 4.7 %relayout_left.6 = (bf16[2,64,64,128]{3,2,1,0:T(8,128)(2,1)}, bf16[2,64,384,128]{3,2,1,0:T(8,128)(2,1)}) custom-call(s32[128]{0:T(128)} %perm_ref.19, s32[1]{0:T(128)} %bitcast.1.base_ref, s32[1]{0:T(128)} %bitcast.wraps_ref, bf16[2,384,128,128]{3,2,1,0:T(8,128)(2,1)} %bitcast.30), custom_call_target="tpu_custom_call" | custom-call | flops 5000000000 | bytes 8388608 | tf_op jit(solution)/shard_map/relayout_left/pallas_call | solution.py:86
  17.7 4.8 %relayout_right.6 = (bf16[2,64,64,128]{3,2,1,0:T(8,128)(2,1)}, bf16[2,64,384,128]{3,2,1,0:T(8,128)(2,1)}) custom-call(s32[128]{0:T(128)} %perm_ref.19, s32[1]{0:T(128)} %bitcast.1.base_ref, s32[1]{0:T(128)} %bitcast.wraps_ref, bf16[2,8,48,128,128]{4,3,2,1,0:T(8,128)(2,1)} %bitcast.31), custom_call_target="tpu_custom_call" | custom-call | flops 5000000000 | bytes 8388608 | tf_op jit(solution)/shard_map/relayout_right/pallas_call | solution.py:86
  22.5 5.4 %collective-permute-start.4 = (bf16[2,64,64,128]{3,2,1,0:T(8,128)(2,1)}, bf16[2,64,64,128]{3,2,1,0:T(8,128)(2,1)}, u32[]{:S(2)}, u32[]{:S(2)}) collective-permute-start(bf16[2,64,64,128]{3,2,1,0:T(8,128)(2,1)} %get-tuple-element.101), channel_id=1, source_target_pairs={{0,8},{8,16},{16,24},{24,32},{32,40},{40,48},{48,56},{56,64},{64,7... | collective-permute-start | bytes 6291464 | tf_op jit(solution)/shard_map/ppermute | solution.py:20
  27.8 4.2 %relayout_left.7.refs_0_ = bf16[2,64,384,128]{3,2,1,0:T(8,128)(2,1)} custom-call(s32[128]{0:T(128)} %perm_ref.19, s32[1]{0:T(128)} %bitcast.1.base_ref, s32[1]{0:T(128)} %bitcast.wraps_ref, bf16[2,384,128,128]{3,2,1,0:T(8,128)(2,1)} %bitcast.32, bf16[2,64,384,128]{3,2,1,0:T(8,128)(2,1)} %get-tuple-element.77.refs_0_), custom_call_target="tpu_custom_call", output_to_operand_aliasing={{}: (4, {})} | custom-call | flops 2500000000 | bytes 4194304 | tf_op jit(solution)/shard_map/relayout_left/pallas_call | solution.py:86
  32.0 3.5 %relayout_right.7.refs_0_ = bf16[2,64,384,128]{3,2,1,0:T(8,128)(2,1)} custom-call(s32[128]{0:T(128)} %perm_ref.19, s32[1]{0:T(128)} %bitcast.1.base_ref, s32[1]{0:T(128)} %bitcast.wraps_ref, bf16[2,8,48,128,128]{4,3,2,1,0:T(8,128)(2,1)} %bitcast.33, bf16[2,64,384,128]{3,2,1,0:T(8,128)(2,1)} %get-tuple-element.79.refs_0_), custom_call_target="tpu_custom_call", output_to_operand_aliasing={{}: (4, {})} | custom-call | flops 2500000000 | bytes 4194304 | tf_op jit(solution)/shard_map/relayout_right/pallas_call | solution.py:86
  35.5 8.4 %relayout_left.8 = (bf16[2,64,128,128]{3,2,1,0:T(8,128)(2,1)}, bf16[2,64,384,128]{3,2,1,0:T(8,128)(2,1)}) custom-call(s32[128]{0:T(128)} %perm_ref.19, s32[1]{0:T(128)} %bitcast.1.base_ref, s32[1]{0:T(128)} %bitcast.wraps_ref, bf16[2,384,128,128]{3,2,1,0:T(8,128)(2,1)} %bitcast.34, ...), custom_call_target="tpu_custom_call", output_to_operand_aliasing={{1}: (4, {})} | custom-call | flops 10000000000 | bytes 16777216 | tf_op jit(solution)/shard_map/relayout_left/pallas_call | solution.py:86
  44.1 8.5 %relayout_right.8 = (bf16[2,64,128,128]{3,2,1,0:T(8,128)(2,1)}, bf16[2,64,384,128]{3,2,1,0:T(8,128)(2,1)}) custom-call(s32[128]{0:T(128)} %perm_ref.19, s32[1]{0:T(128)} %bitcast.1.base_ref, s32[1]{0:T(128)} %bitcast.wraps_ref, bf16[2,8,48,128,128]{4,3,2,1,0:T(8,128)(2,1)} %bitcast.35, ...), custom_call_target="tpu_custom_call", output_to_operand_aliasing={{1}: (4, {})} | custom-call | flops 10000000000 | bytes 16777216 | tf_op jit(solution)/shard_map/relayout_right/pallas_call | solution.py:86
  52.5 5.3 %collective-permute-start.7 = (bf16[2,64,128,128]{3,2,1,0:T(8,128)(2,1)}, bf16[2,64,128,128]{3,2,1,0:T(8,128)(2,1)}, u32[]{:S(2)}, u32[]{:S(2)}) collective-permute-start(bf16[2,64,128,128]{3,2,1,0:T(8,128)(2,1)} %get-tuple-element.114), channel_id=1, source_target_pairs={{0,8},{8,16},{16,24},{24,32},{32,40},{40,48},{48,56},{56,64},{64,7... | collective-permute-start | bytes 12582920 | tf_op jit(solution)/shard_map/ppermute | solution.py:20
  57.9 8.5 %relayout_left.9 = (bf16[2,48,128,128]{3,2,1,0:T(8,128)(2,1)}, bf16[2,16,128,128]{3,2,1,0:T(8,128)(2,1)}, bf16[2,64,384,128]{3,2,1,0:T(8,128)(2,1)}) custom-call(s32[128]{0:T(128)} %perm_ref.19, s32[1]{0:T(128)} %bitcast.1.base_ref, s32[1]{0:T(128)} %bitcast.wraps_ref, bf16[2,384,128,128]{3,2,1,0:T(8,128)(2,1)} %bitcast.36, ...), custom_call_target="tpu_custom_call", output_to_operand_aliasing={{2}: (4, {})} | custom-call | flops 10000000000 | bytes 16777216 | tf_op jit(solution)/shard_map/relayout_left/pallas_call | solution.py:86
  66.3 8.6 %relayout_right.9 = (bf16[2,48,128,128]{3,2,1,0:T(8,128)(2,1)}, bf16[2,16,128,128]{3,2,1,0:T(8,128)(2,1)}, bf16[2,64,384,128]{3,2,1,0:T(8,128)(2,1)}) custom-call(s32[128]{0:T(128)} %perm_ref.19, s32[1]{0:T(128)} %bitcast.1.base_ref, s32[1]{0:T(128)} %bitcast.wraps_ref, bf16[2,8,48,128,128]{4,3,2,1,0:T(8,128)(2,1)} %bitcast.37, ...), custom_call_target="tpu_custom_call", output_to_operand_aliasing={{2}: (4, {})} | custom-call | flops 10000000000 | bytes 16777216 | tf_op jit(solution)/shard_map/relayout_right/pallas_call | solution.py:86
  75.4 14.3 %products.4 = f32[8,2,2,48,128]{4,3,2,1,0:T(8,128)} custom-call(bf16[2,64,384,128]{3,2,1,0:T(8,128)(2,1)} %get-tuple-element.116.refs_0_, bf16[2,64,64,128]{3,2,1,0:T(8,128)(2,1)} %copy-done.2, bf16[2,64,64,128]{3,2,1,0:T(8,128)(2,1)} %copy-done.4, bf16[2,64,64,128]{3,2,1,0:T(8,128)(2,1)} %copy-done.3, ...), custom_call_target="tpu_custom_call" | custom-call | flops 12884901888 | bytes 67108864 | tf_op jit(solution)/shard_map/products/pallas_call | solution.py:178
  89.7 5.0 %all-to-all-start = ((f32[4,2,2,2,48,128]{5,4,3,2,1,0:T(8,128)}), f32[4,2,2,2,48,128]{5,4,3,2,1,0:T(8,128)S(1)}, u32[]{:S(2)}, u32[]{:S(2)}) async-start(f32[4,2,2,2,48,128]{5,4,3,2,1,0:T(8,128)} %bitcast.42), calls=%async_computation | async-start | bytes 1572864 | tf_op jit(solution)/shard_map/all_to_all | solution.py:207
  95.0 11.8 %all-to-all-done = f32[4,2,2,2,48,128]{5,4,3,2,1,0:T(8,128)S(1)} async-done(((f32[4,2,2,2,48,128]{5,4,3,2,1,0:T(8,128)}), f32[4,2,2,2,48,128]{5,4,3,2,1,0:T(8,128)S(1)}, u32[]{:S(2)}, u32[]{:S(2)}) %all-to-all-start) | async-done | bytes 786464 | tf_op jit(solution)/shard_map/all_to_all | solution.py:207
  106.9 2.6 %collective-permute-start.6 = (bf16[2,16,128,128]{3,2,1,0:T(8,128)(2,1)}, bf16[2,16,128,128]{3,2,1,0:T(8,128)(2,1)S(1)}, u32[]{:S(2)}, u32[]{:S(2)}) collective-permute-start(bf16[2,16,128,128]{3,2,1,0:T(8,128)(2,1)} %get-tuple-element.109), channel_id=1, source_target_pairs={{0,8},{8,16},{16,24},{24,32},{32,40},{40,48},{48,56},{56,64},{64,7... | collective-permute-start | bytes 3145736 | tf_op jit(solution)/shard_map/ppermute | solution.py:20
  109.5 14.3 %products.5 = f32[8,2,2,48,128]{4,3,2,1,0:T(8,128)} custom-call(bf16[2,64,384,128]{3,2,1,0:T(8,128)(2,1)} %get-tuple-element.116.refs_0_, bf16[2,64,128,128]{3,2,1,0:T(8,128)(2,1)} %collective-permute-done.5.refs_1_, bf16[2,64,128,128]{3,2,1,0:T(8,128)(2,1)} %collective-permute-done.7.refs_2_, bf16[2,64,384,128]{3,2,1,0:T(8,128)(2,1)} %get-tuple-element.119.refs_5_.refs_3_), custom_call_target="tpu_custom_call" | custom-call | flops 12884901888 | bytes 67108864 | tf_op jit(solution)/shard_map/products/pallas_call | solution.py:178
  123.8 3.5 %all-to-all-start.1 = ((f32[4,2,2,2,48,128]{5,4,3,2,1,0:T(8,128)}), f32[4,2,2,2,48,128]{5,4,3,2,1,0:T(8,128)S(1)}, u32[]{:S(2)}, u32[]{:S(2)}) async-start(f32[4,2,2,2,48,128]{5,4,3,2,1,0:T(8,128)} %bitcast.43), calls=%async_computation.1 | async-start | bytes 1572864 | tf_op jit(solution)/shard_map/all_to_all | solution.py:207
  127.3 10.1 %collective-permute-done.9.refs_2_ = bf16[2,48,128,128]{3,2,1,0:T(8,128)(2,1)} collective-permute-done((bf16[2,48,128,128]{3,2,1,0:T(8,128)(2,1)}, bf16[2,48,128,128]{3,2,1,0:T(8,128)(2,1)}, u32[]{:S(2)}, u32[]{:S(2)}) %collective-permute-start.9) | collective-permute-done | bytes 3145760 | tf_op jit(solution)/shard_map/ppermute | solution.py:20
  137.4 12.0 %products.6 = (f32[768,256]{1,0:T(8,128)}, f32[256,768]{1,0:T(8,128)}) custom-call(bf16[2,64,384,128]{3,2,1,0:T(8,128)(2,1)} %get-tuple-element.116.refs_0_, bf16[2,48,128,128]{3,2,1,0:T(8,128)(2,1)} %collective-permute-done.8.refs_1_, bf16[2,48,128,128]{3,2,1,0:T(8,128)(2,1)} %collective-permute-done.9.refs_2_, ...), custom_call_target="tpu_custom_call" | custom-call | flops 9663676416 | bytes 50331648 | tf_op jit(solution)/shard_map/products/pallas_call | solution.py:178
  150.8 5.9 %products.7 = f32[8,2,2,48,128]{4,3,2,1,0:T(8,128)} custom-call(bf16[2,64,384,128]{3,2,1,0:T(8,128)(2,1)} %get-tuple-element.116.refs_0_, bf16[2,16,128,128]{3,2,1,0:T(8,128)(2,1)} %copy-done, bf16[2,16,128,128]{3,2,1,0:T(8,128)(2,1)} %copy-done.1, bf16[2,64,384,128]{3,2,1,0:T(8,128)(2,1)} %get-tuple-element.119.refs_5_.refs_3_, ...), custom_call_target="tpu_custom_call" | custom-call | flops 3221225472 | bytes 16777216 | tf_op jit(solution)/shard_map/products/pallas_call | solution.py:178
  156.8 18.0 %all_to_all.15 = f32[8,2,2,48,128]{4,3,2,1,0:T(8,128)S(1)} all-to-all(f32[8,2,2,48,128]{4,3,2,1,0:T(8,128)} %products.7), channel_id=1, replica_groups=mesh['kz'=16,'pw'=8] {'pw'}, dimensions={0} | all-to-all | bytes 1572864 | tf_op jit(solution)/shard_map/all_to_all | solution.py:200
  175.2 8.0 %collective-permute-done.11 = f32[3,2,48,128]{3,2,1,0:T(8,128)S(1)} collective-permute-done((f32[3,2,48,128]{3,2,1,0:T(8,128)S(1)}, f32[3,2,48,128]{3,2,1,0:T(8,128)S(1)}, u32[]{:S(2)}, u32[]{:S(2)}) %collective-permute-start.11) | collective-permute-done | bytes 147488 | tf_op jit(solution)/shard_map/ppermute | solution.py:20
  (41 shorter events, 4.3 us)
Async XLA Ops:
  4.1 31.4 %collective-permute-start = (bf16[2,64,64,128]{3,2,1,0:T(8,128)(2,1)}, bf16[2,64,64,128]{3,2,1,0:T(8,128)(2,1)S(1)}, u32[]{:S(2)}, u32[]{:S(2)}) collective-permute-start(bf16[2,64,64,128]{3,2,1,0:T(8,128)(2,1)} %relayout_left.5), channel_id=1, source_target_pairs={{0,120},{8,0},{16,8},{24,16},{32,24},{40,32},{48,40},{56,48},{64,5... | collective-permute-start | bytes 6291464 | tf_op jit(solution)/shard_map/ppermute | solution.py:20
  8.3 35.7 %collective-permute-start.1 = (bf16[2,64,64,128]{3,2,1,0:T(8,128)(2,1)}, bf16[2,64,64,128]{3,2,1,0:T(8,128)(2,1)S(1)}, u32[]{:S(2)}, u32[]{:S(2)}) collective-permute-start(bf16[2,64,64,128]{3,2,1,0:T(8,128)(2,1)} %relayout_right.5), channel_id=1, source_target_pairs={{0,8},{8,16},{16,24},{24,32},{32,40},{40,48},{48,56},{56,64},{64,7... | collective-permute-start | bytes 6291464 | tf_op jit(solution)/shard_map/ppermute | solution.py:20
  17.7 40.2 %collective-permute-start.2 = (bf16[2,64,64,128]{3,2,1,0:T(8,128)(2,1)}, bf16[2,64,64,128]{3,2,1,0:T(8,128)(2,1)S(1)}, u32[]{:S(2)}, u32[]{:S(2)}) collective-permute-start(bf16[2,64,64,128]{3,2,1,0:T(8,128)(2,1)} %get-tuple-element.93), channel_id=1, source_target_pairs={{0,120},{8,0},{16,8},{24,16},{32,24},{40,32},{48,40},{56,48},{64,5... | collective-permute-start | bytes 6291464 | tf_op jit(solution)/shard_map/ppermute | solution.py:20
  22.5 43.9 %collective-permute-start.4 = (bf16[2,64,64,128]{3,2,1,0:T(8,128)(2,1)}, bf16[2,64,64,128]{3,2,1,0:T(8,128)(2,1)}, u32[]{:S(2)}, u32[]{:S(2)}) collective-permute-start(bf16[2,64,64,128]{3,2,1,0:T(8,128)(2,1)} %get-tuple-element.101), channel_id=1, source_target_pairs={{0,8},{8,16},{16,24},{24,32},{32,40},{40,48},{48,56},{56,64},{64,7... | collective-permute-start | bytes 6291464 | tf_op jit(solution)/shard_map/ppermute | solution.py:20
  35.5 8.4 %copy-start.2 = (bf16[2,64,64,128]{3,2,1,0:T(8,128)(2,1)}, bf16[2,64,64,128]{3,2,1,0:T(8,128)(2,1)S(1)}, u32[]{:S(2)}) copy-start(bf16[2,64,64,128]{3,2,1,0:T(8,128)(2,1)S(1)} %collective-permute-done.refs_1_) | copy-start | bytes 6291460
  44.0 8.6 %copy-start.3 = (bf16[2,64,64,128]{3,2,1,0:T(8,128)(2,1)}, bf16[2,64,64,128]{3,2,1,0:T(8,128)(2,1)S(1)}, u32[]{:S(2)}) copy-start(bf16[2,64,64,128]{3,2,1,0:T(8,128)(2,1)S(1)} %collective-permute-done.1.refs_3_) | copy-start | bytes 6291460
  44.0 62.9 %collective-permute-start.5 = (bf16[2,64,128,128]{3,2,1,0:T(8,128)(2,1)}, bf16[2,64,128,128]{3,2,1,0:T(8,128)(2,1)}, u32[]{:S(2)}, u32[]{:S(2)}) collective-permute-start(bf16[2,64,128,128]{3,2,1,0:T(8,128)(2,1)} %get-tuple-element.108), channel_id=1, source_target_pairs={{0,120},{8,0},{16,8},{24,16},{32,24},{40,32},{48,40},{56,48},{64,5... | collective-permute-start | bytes 12582920 | tf_op jit(solution)/shard_map/ppermute | solution.py:20
  52.5 56.9 %collective-permute-start.7 = (bf16[2,64,128,128]{3,2,1,0:T(8,128)(2,1)}, bf16[2,64,128,128]{3,2,1,0:T(8,128)(2,1)}, u32[]{:S(2)}, u32[]{:S(2)}) collective-permute-start(bf16[2,64,128,128]{3,2,1,0:T(8,128)(2,1)} %get-tuple-element.114), channel_id=1, source_target_pairs={{0,8},{8,16},{16,24},{24,32},{32,40},{40,48},{48,56},{56,64},{64,7... | collective-permute-start | bytes 12582920 | tf_op jit(solution)/shard_map/ppermute | solution.py:20
  57.9 8.5 %copy-start.4 = (bf16[2,64,64,128]{3,2,1,0:T(8,128)(2,1)}, bf16[2,64,64,128]{3,2,1,0:T(8,128)(2,1)S(1)}, u32[]{:S(2)}) copy-start(bf16[2,64,64,128]{3,2,1,0:T(8,128)(2,1)S(1)} %collective-permute-done.2.refs_2_) | copy-start | bytes 6291460
  74.9 62.4 %collective-permute-start.9 = (bf16[2,48,128,128]{3,2,1,0:T(8,128)(2,1)}, bf16[2,48,128,128]{3,2,1,0:T(8,128)(2,1)}, u32[]{:S(2)}, u32[]{:S(2)}) collective-permute-start(bf16[2,48,128,128]{3,2,1,0:T(8,128)(2,1)} %get-tuple-element.118), channel_id=1, source_target_pairs={{0,8},{8,16},{16,24},{24,32},{32,40},{40,48},{48,56},{56,64},{64,7... | collective-permute-start | bytes 9437192 | tf_op jit(solution)/shard_map/ppermute | solution.py:20
  74.9 62.4 %collective-permute-start.8 = (bf16[2,48,128,128]{3,2,1,0:T(8,128)(2,1)}, bf16[2,48,128,128]{3,2,1,0:T(8,128)(2,1)}, u32[]{:S(2)}, u32[]{:S(2)}) collective-permute-start(bf16[2,48,128,128]{3,2,1,0:T(8,128)(2,1)} %get-tuple-element.117), channel_id=1, source_target_pairs={{0,120},{8,0},{16,8},{24,16},{32,24},{40,32},{48,40},{56,48},{64,5... | collective-permute-start | bytes 9437192 | tf_op jit(solution)/shard_map/ppermute | solution.py:20
  89.7 17.2 %all-to-all-start = ((f32[4,2,2,2,48,128]{5,4,3,2,1,0:T(8,128)}), f32[4,2,2,2,48,128]{5,4,3,2,1,0:T(8,128)S(1)}, u32[]{:S(2)}, u32[]{:S(2)}) async-start(f32[4,2,2,2,48,128]{5,4,3,2,1,0:T(8,128)} %bitcast.42), calls=%async_computation | async-start | bytes 1572864 | tf_op jit(solution)/shard_map/all_to_all | solution.py:207
  94.7 54.7 %collective-permute-start.3 = (bf16[2,16,128,128]{3,2,1,0:T(8,128)(2,1)}, bf16[2,16,128,128]{3,2,1,0:T(8,128)(2,1)S(1)}, u32[]{:S(2)}, u32[]{:S(2)}) collective-permute-start(bf16[2,16,128,128]{3,2,1,0:T(8,128)(2,1)} %get-tuple-element.99), channel_id=1, source_target_pairs={{0,120},{8,0},{16,8},{24,16},{32,24},{40,32},{48,40},{56,48},{64,5... | collective-permute-start | bytes 3145736 | tf_op jit(solution)/shard_map/ppermute | solution.py:20
  106.9 42.5 %collective-permute-start.6 = (bf16[2,16,128,128]{3,2,1,0:T(8,128)(2,1)}, bf16[2,16,128,128]{3,2,1,0:T(8,128)(2,1)S(1)}, u32[]{:S(2)}, u32[]{:S(2)}) collective-permute-start(bf16[2,16,128,128]{3,2,1,0:T(8,128)(2,1)} %get-tuple-element.109), channel_id=1, source_target_pairs={{0,8},{8,16},{16,24},{24,32},{32,40},{40,48},{48,56},{56,64},{64,7... | collective-permute-start | bytes 3145736 | tf_op jit(solution)/shard_map/ppermute | solution.py:20
  123.8 25.6 %all-to-all-start.1 = ((f32[4,2,2,2,48,128]{5,4,3,2,1,0:T(8,128)}), f32[4,2,2,2,48,128]{5,4,3,2,1,0:T(8,128)S(1)}, u32[]{:S(2)}, u32[]{:S(2)}) async-start(f32[4,2,2,2,48,128]{5,4,3,2,1,0:T(8,128)} %bitcast.43), calls=%async_computation.1 | async-start | bytes 1572864 | tf_op jit(solution)/shard_map/all_to_all | solution.py:207
  149.4 1.4 copy-start
  149.4 1.4 copy-start.1
  149.5 7.3 %collective-permute-start.10 = (f32[2,2,2,48,128]{4,3,2,0,1:T(8,128)S(1)}, f32[2,2,2,48,128]{4,3,2,0,1:T(8,128)S(1)}, u32[]{:S(2)}, u32[]{:S(2)}) collective-permute-start(f32[2,2,2,48,128]{4,3,2,0,1:T(8,128)S(1)} %fusion.1), channel_id=1, source_target_pairs={{0,1},{1,0},{2,3},{3,2},{4,5},{5,4},{6,7},{7,6},{8,9},{9,8},{10,11... | collective-permute-start | bytes 589832 | tf_op jit(solution)/shard_map/ppermute | solution.py:214
  174.9 8.3 %collective-permute-start.11 = (f32[3,2,48,128]{3,2,1,0:T(8,128)S(1)}, f32[3,2,48,128]{3,2,1,0:T(8,128)S(1)}, u32[]{:S(2)}, u32[]{:S(2)}) collective-permute-start(f32[3,2,48,128]{3,2,1,0:T(8,128)S(1)} %get-tuple-element.133), channel_id=1, source_target_pairs={{0,120},{8,0},{16,8},{24,16},{32,24},{40,32},{48,40},{56,48},{64,5... | collective-permute-start | bytes 442376 | tf_op jit(solution)/shard_map/ppermute | solution.py:20
